TPU v7x, 32 devices: a whole 2x2x4 slice. The times are simulated.
32 devices in a mesh: rows: 32 (over z, y, x, core).
Axes of the slice: x: 2, y: 2, z: 4, core: 2. Of those that a mesh axis runs over, the one named last changes fastest.
Arguments:
- snapshots: float32 [262144, 128], P('rows')
- send_list: int32 [1024, 64], P('rows'), may hold values from 0 to 8191
- stencil: int32 [524288, 8], P('rows'), may hold values from 0 to 2047, as said below
- weights: float32 [524288, 8], P('rows'), may hold values from 0.2 to 1
Outputs:
- basis: float32 [524288, 128], P('rows')
- r_factor: float32 [128, 128], replicated
Inputs may be any that keep to these rules, and one draw needn't show every extreme that they name: `send_list`: every slot carries a node; a node may fill several slots. `stencil`: all 8 donors of a row lie on one peer: local row k of device d takes them from peer (d + k // 512) mod 32. Every slot that a device receives is read by some of its rows.
All inputs are finite; a program needn't handle non-finite values.
Results may differ from a plain program's by a relative error of at most 0.0003.
Values sent between devices are 32-bit elements; how exact they have to be, the bound alone decides.
No kernel may reach another device: no remote copies, remote signals or barrier semaphores. Data moves between devices by JAX's collectives and lax.ppermute only.
A program may use at most 192 MiB of HBM per device.

v0:
```python
import jax
import jax.numpy as jnp
from jax import lax
from jax.sharding import PartitionSpec as P


def product(left, right):
    return jnp.dot(left, right, precision=lax.Precision.HIGHEST, preferred_element_type=jnp.float32)


def upper_inverse(upper):
    count = upper.shape[0]
    if count == 1:
        return 1.0 / upper
    half = count // 2
    top_inv = upper_inverse(upper[:half, :half])
    low_inv = upper_inverse(upper[half:, half:])
    corner = -product(product(top_inv, upper[:half, half:]), low_inv)
    zeros_block = jnp.zeros((count - half, half), jnp.float32)
    top_rows = jnp.concatenate([top_inv, corner], axis=1)
    low_rows = jnp.concatenate([zeros_block, low_inv], axis=1)
    return jnp.concatenate([top_rows, low_rows], axis=0)


def normed_factor(block, total_rows):
    local = product(block.T, block)
    gram = lax.psum(local, "rows")
    upper = jnp.linalg.cholesky(gram / total_rows).T
    return upper


def body(snapshots, send_list, stencil, weights):
    peers = lax.axis_size("rows")
    row_count = stencil.shape[0]
    total_rows = row_count * peers
    outgoing = snapshots[send_list]
    received = lax.all_to_all(outgoing, "rows", split_axis=0, concat_axis=0, tiled=True)
    flat = received.reshape(received.shape[0] * received.shape[1], received.shape[2])
    field = jnp.zeros((row_count, flat.shape[1]), jnp.float32)
    for s in range(stencil.shape[1]):
        field = field + weights[:, s][:, None] * flat[stencil[:, s]]
    first = normed_factor(field, total_rows)
    middle = product(field, upper_inverse(first))
    second = normed_factor(middle, total_rows)
    basis = product(middle, upper_inverse(second))
    r_factor = product(second, first)
    return (basis, r_factor)


def solution(mesh):
    return jax.shard_map(
        body,
        mesh=mesh,
        in_specs=(P("rows", None), P("rows", None), P("rows", None), P("rows", None)),
        out_specs=(P("rows", None), P()),
        check_vma=False,
    )
```

profile of v0, /device:TPU:0, one launch (start us, length us, event | category | flops | bytes accessed | tf_op | source)
XLA Modules:
  0.0 1184.0 jit_solution(2221506955138115921)
XLA Ops:
  7.2 0.8 compare_select_fusion.8
  8.1 9.8 gather_fusion
  17.9 7.3 all-to-all-start
  25.3 0.7 compare_select_fusion.7
  26.1 1.1 fusion.1773
  27.2 24.3 %all-to-all-done = f32[32,64,128]{2,1,0:T(8,128)S(1)} async-done(((f32[32,64,128]{2,1,0:T(8,128)}), f32[32,64,128]{2,1,0:T(8,128)S(1)}, u32[]{:S(2)}, u32[]{:S(2)}) %all-to-all-start) | async-done | bytes 1048608 | tf_op jit(solution)/shard_map/all_to_all | solution.py:37
  51.4 54.7 %gather_fusion.1 = f32[16384,128]{1,0:T(8,128)} fusion(f32[2048,128]{1,0:T(8,128)S(1)} %bitcast.288, s32[16384]{0:T(1024)S(1)} %broadcast_clamp_fusion.7), kind=kCustom, calls=%fused_computation.1 | custom fusion | bytes 16842752 | tf_op jit(solution)/shard_map/gather | solution.py:41
  106.2 54.8 %gather_fusion.2 = f32[16384,128]{1,0:T(8,128)} fusion(f32[2048,128]{1,0:T(8,128)S(1)} %bitcast.289, s32[16384]{0:T(1024)S(1)} %broadcast_clamp_fusion.6), kind=kCustom, calls=%fused_computation.2 | custom fusion | bytes 16842752 | tf_op jit(solution)/shard_map/gather | solution.py:41
  161.0 54.8 %gather_fusion.3 = f32[16384,128]{1,0:T(8,128)} fusion(f32[2048,128]{1,0:T(8,128)S(1)} %bitcast.290, s32[16384]{0:T(1024)S(1)} %broadcast_clamp_fusion.5), kind=kCustom, calls=%fused_computation.3 | custom fusion | bytes 16842752 | tf_op jit(solution)/shard_map/gather | solution.py:41
  215.7 54.8 %gather_fusion.4 = f32[16384,128]{1,0:T(8,128)} fusion(f32[2048,128]{1,0:T(8,128)S(1)} %bitcast.291, s32[16384]{0:T(1024)S(1)} %broadcast_clamp_fusion.4), kind=kCustom, calls=%fused_computation.4 | custom fusion | bytes 16842752 | tf_op jit(solution)/shard_map/gather | solution.py:41
  270.5 54.8 %gather_fusion.5 = f32[16384,128]{1,0:T(8,128)} fusion(f32[2048,128]{1,0:T(8,128)S(1)} %bitcast.292, s32[16384]{0:T(1024)S(1)} %broadcast_clamp_fusion.3), kind=kCustom, calls=%fused_computation.5 | custom fusion | bytes 16842752 | tf_op jit(solution)/shard_map/gather | solution.py:41
  325.3 54.8 %gather_fusion.6 = f32[16384,128]{1,0:T(8,128)} fusion(f32[2048,128]{1,0:T(8,128)S(1)} %bitcast.293, s32[16384]{0:T(1024)S(1)} %broadcast_clamp_fusion.2), kind=kCustom, calls=%fused_computation.6 | custom fusion | bytes 16842752 | tf_op jit(solution)/shard_map/gather | solution.py:41
  380.1 54.7 %gather_fusion.7 = f32[16384,128]{1,0:T(8,128)} fusion(f32[2048,128]{1,0:T(8,128)S(1)} %bitcast.294, s32[16384]{0:T(1024)S(1)} %broadcast_clamp_fusion.1), kind=kCustom, calls=%fused_computation.7 | custom fusion | bytes 16842752 | tf_op jit(solution)/shard_map/gather | solution.py:41
  434.9 54.9 %gather_fusion.8 = f32[16384,128]{1,0:T(8,128)} fusion(f32[2048,128]{1,0:T(8,128)S(1)} %bitcast.295, s32[16384]{0:T(1024)S(1)} %broadcast_clamp_fusion), kind=kCustom, calls=%fused_computation.8 | custom fusion | bytes 16842752 | tf_op jit(solution)/shard_map/gather | solution.py:41
  489.8 25.8 %multiply_add_fusion = f32[16384,128]{1,0:T(8,128)S(1)} fusion(f32[16384,128]{1,0:T(8,128)} %gather_fusion.8, f32[16384,128]{1,0:T(8,128)} %gather_fusion.7, f32[16384,128]{1,0:T(8,128)} %gather_fusion.6, f32[16384,128]{1,0:T(8,128)} %gather_fusion.5, f32[16384,128]{1,0:T(8,128)} %gather_fusion.4, f32[16384,128]{1,0:T(8,128)} %gather_fusion.3, ...), kind=kLoop, calls=%fused_computation.9 | loop fusion | flops 31457280 | bytes 76021760 | tf_op jit(solution)/shard_map/add | solution.py:41
  515.6 3.4 copy-done.1
  519.0 14.9 %fusion.1794 = f32[128,128]{0,1:T(8,128)} fusion(f32[16384,128]{1,0:T(8,128)S(1)} %multiply_add_fusion), kind=kOutput, calls=%fused_computation.2092 | convolution fusion | flops 3221225472 | bytes 8454144 | tf_op jit(solution)/shard_map/dot_general | solution.py:8
  533.9 116.6 %all-reduce.129.cloned.1.call-done = f32[128,128]{0,1:T(8,128)} async-done(((f32[128,128]{0,1:T(8,128)}), f32[128,128]{0,1:T(8,128)}) %all-reduce.129.cloned.1.call-update) | async-done | bytes 65552 | tf_op jit(solution)/shard_map/psum | solution.py:27
  650.6 0.8 broadcast_multiply_fusion.1
  651.5 0.9 fusion.65
  652.4 11.7 cholesky.44
  664.1 0.6 compare_reduce_fusion.1
  664.8 0.6 fusion.67
  665.3 0.7 fusion.1785
  666.1 0.7 fusion.1784
  666.8 0.7 fusion.1786
  667.5 0.7 fusion.1787
  668.2 0.7 fusion.1788
  669.0 0.6 slice.3140
  669.6 0.7 fusion.1790
  670.3 0.7 fusion.1789
  671.0 0.7 fusion.1791
  671.7 0.7 fusion.1792
  672.5 0.7 fusion.1793
  673.2 0.7 slice.3268
  711.7 0.3 fusion.520
  750.2 0.3 fusion.544
  789.2 0.3 fusion.568
  829.5 0.3 fusion.80
  830.0 10.1 fusion.13
  840.1 3.3 copy-done
  843.4 14.6 %fusion.1795 = f32[128,128]{0,1:T(8,128)} fusion(f32[16384,128]{1,0:T(8,128)S(1)} %fusion.13), kind=kOutput, calls=%fused_computation.2093 | convolution fusion | flops 3221225472 | bytes 8454144 | tf_op jit(solution)/shard_map/dot_general | solution.py:8
  858.0 118.5 %all-reduce.131.cloned.1.call-done = f32[128,128]{0,1:T(8,128)} async-done(((f32[128,128]{0,1:T(8,128)}), f32[128,128]{0,1:T(8,128)}) %all-reduce.131.cloned.1.call-update) | async-done | bytes 65552 | tf_op jit(solution)/shard_map/psum | solution.py:27
  976.5 0.8 broadcast_multiply_fusion
  977.4 0.9 fusion.64
  978.3 11.7 cholesky.55
  990.0 0.6 compare_reduce_fusion
  990.6 2.1 fusion.66
  992.8 0.7 fusion.68
  993.4 0.7 fusion.1775
  994.2 0.7 fusion.1774
  994.9 0.7 fusion.1776
  995.6 0.7 fusion.1778
  996.4 0.7 fusion.1777
  997.1 0.6 slice.3395
  997.7 0.7 fusion.1780
  998.4 0.7 fusion.1779
  999.2 0.7 fusion.1781
  999.9 0.7 fusion.1783
  1000.6 0.7 fusion.1782
  1001.4 0.7 slice.3523
  1128.2 0.4 convolution_negate_fusion.33
  1159.0 0.3 fusion.104
  1159.6 17.2 %fusion.28 = f32[16384,128]{1,0:T(8,128)} fusion(f32[16384,128]{1,0:T(8,128)} %copy-done, f32[1,1]{0,1:T(1,128)} %constant.46.clone.1, f32[64,64]{0,1:T(8,128)S(1)} %fusion.116, f32[64,64]{0,1:T(8,128)S(1)} %convolution_negate_fusion, f32[32,64]{0,1:T(8,128)S(1)} %concatenate.2854, f32[32,32]{0,1:T(8,128)S(1)} %convolution_negate_fusion.3, ...), kind=kOutput, calls=%fused_computation.185 | convolution fusion | flops 3221504000 | bytes 16826368 | tf_op jit(solution)/shard_map/dot_general | solution.py:8
  (462 shorter events, 60.5 us)
Async XLA Ops:
  7.2 18.1 %copy-start.2 = (s32[16384,8]{0,1:T(8,128)S(1)}, s32[16384,8]{0,1:T(8,128)}, u32[]{:S(2)}) copy-start(s32[16384,8]{0,1:T(8,128)} %param.7) | copy-start | bytes 1572868
  7.2 18.9 %copy-start.3 = (f32[16384,8]{0,1:T(8,128)S(1)}, f32[16384,8]{0,1:T(8,128)}, u32[]{:S(2)}) copy-start(f32[16384,8]{0,1:T(8,128)} %param.8) | copy-start | bytes 1572868
  17.9 33.5 %all-to-all-start = ((f32[32,64,128]{2,1,0:T(8,128)}), f32[32,64,128]{2,1,0:T(8,128)S(1)}, u32[]{:S(2)}, u32[]{:S(2)}) async-start(f32[32,64,128]{2,1,0:T(8,128)} %bitcast.1), calls=%async_computation | async-start | bytes 2097152 | tf_op jit(solution)/shard_map/all_to_all | solution.py:37
  25.2 625.4 %all-reduce.129.cloned.1.call-start = ((), (), s32[]{:S(2)}) async-start(), calls=%async_computation.1 | async-start | bytes 131072 | tf_op jit(solution)/shard_map/psum | solution.py:27
  434.8 54.9 %copy-start.4 = (f32[16384,1]{0,1:T(1,128)S(1)}, f32[16384,1]{0,1:T(1,128)}, u32[]{:S(2)}) copy-start(f32[16384,1]{0,1:T(1,128)} %get-tuple-element.3) | copy-start | bytes 196612
  434.9 54.9 %copy-start.5 = (f32[16384,1]{0,1:T(1,128)S(1)}, f32[16384,1]{0,1:T(1,128)}, u32[]{:S(2)}) copy-start(f32[16384,1]{0,1:T(1,128)} %get-tuple-element.4) | copy-start | bytes 196612
  434.9 54.9 %copy-start.6 = (f32[16384,1]{0,1:T(1,128)S(1)}, f32[16384,1]{0,1:T(1,128)}, u32[]{:S(2)}) copy-start(f32[16384,1]{0,1:T(1,128)} %get-tuple-element.5) | copy-start | bytes 196612
  434.9 54.9 %copy-start.7 = (f32[16384,1]{0,1:T(1,128)S(1)}, f32[16384,1]{0,1:T(1,128)}, u32[]{:S(2)}) copy-start(f32[16384,1]{0,1:T(1,128)} %get-tuple-element.6) | copy-start | bytes 196612
  434.9 54.9 %copy-start.8 = (f32[16384,1]{0,1:T(1,128)S(1)}, f32[16384,1]{0,1:T(1,128)}, u32[]{:S(2)}) copy-start(f32[16384,1]{0,1:T(1,128)} %get-tuple-element.7) | copy-start | bytes 196612
  434.9 54.9 %copy-start.9 = (f32[16384,1]{0,1:T(1,128)S(1)}, f32[16384,1]{0,1:T(1,128)}, u32[]{:S(2)}) copy-start(f32[16384,1]{0,1:T(1,128)} %get-tuple-element.8) | copy-start | bytes 196612
  434.9 54.9 %copy-start.10 = (f32[16384,1]{0,1:T(1,128)S(1)}, f32[16384,1]{0,1:T(1,128)}, u32[]{:S(2)}) copy-start(f32[16384,1]{0,1:T(1,128)} %get-tuple-element.9) | copy-start | bytes 196612
  434.9 54.9 %copy-start.11 = (f32[16384,1]{0,1:T(1,128)S(1)}, f32[16384,1]{0,1:T(1,128)}, u32[]{:S(2)}) copy-start(f32[16384,1]{0,1:T(1,128)} %get-tuple-element.10) | copy-start | bytes 196612
  515.6 3.4 copy-start.1
  533.9 442.6 %all-reduce.131.cloned.1.call-start = ((), (), s32[]{:S(2)}) async-start(), calls=%async_computation.2 | async-start | bytes 131072 | tf_op jit(solution)/shard_map/psum | solution.py:27
  840.1 3.3 copy-start
Sparse Core Ops, SparseCore 0:
  534.0 116.5 all-reduce.128
  858.1 118.3 all-reduce.130
where the time goes:
time: 1190 us; the launch traced here: 1180 us
  local copies, waits for them, and re-layouts  474 us (40%)
  between operations  267 us (22%)
  waiting for transfers between devices  259 us (22%)
  matrix products  111 us (9%)
  other arithmetic  66.1 us (6%)
    gather x8, local copies, waits for them, and re-layouts, body(): field = field + weights[:, s][:, None] * flat[stencil[:, s]]  438 us
    psum x2, waiting for transfers between devices, normed_factor(): gram = lax.psum(local, 'rows')  235 us
    dot_general x257, matrix products, product(): jnp.dot(left, right, precision=lax.Precision.HIGHEST, preferred_element_t...  111 us
    add x1, other arithmetic, body(): field = field + weights[:, s][:, None] * flat[stencil[:, s]]  25.8 us
    another operation x6, other arithmetic, normed_factor(): upper = jnp.linalg.cholesky(gram / total_rows).T  24.8 us
    all_to_all x1, waiting for transfers between devices, body(): lax.all_to_all(outgoing, 'rows', split_axis=0, concat_axis=0, tiled=True)  24.3 us
  transfers between devices with their start and end apart: 3, of which 3 were waited for; matrix products, arithmetic and copies ran while one was open for 0% of the time, Pallas kernels for 0%

commit v1 on v0

v1 whole, which is shorter than its diff:
```python
import functools
import math

import jax
import jax.numpy as jnp
from jax import lax
from jax.experimental import pallas as pl
from jax.experimental.pallas import tpu as pltpu
from jax.sharding import PartitionSpec as P

F32 = jnp.float32
BF16 = jnp.bfloat16
TILE = 8
VMEM_LIMIT = 56 * 1024 * 1024


def exact(left, right, dims=((1,), (0,))):
    return lax.dot_general(left, right, (dims, ((), ())), precision=lax.Precision.HIGHEST, preferred_element_type=F32)


def rough(left, right, dims=((1,), (0,))):
    return lax.dot_general(left.astype(BF16), right.astype(BF16), (dims, ((), ())), preferred_element_type=F32)


def pick_kernel(send_ref, snap_ref, out_ref):
    peers, cap = send_ref.shape

    def one_peer(peer, carry):
        base = peer * cap
        for slot in range(cap):
            node = send_ref[peer, slot]
            out_ref[pl.ds(base + slot, 1), :] = snap_ref[pl.ds(node, 1), :]
        return carry

    lax.fori_loop(0, peers, one_peer, 0)


def pick_donors(snapshots, send_list):
    peers, cap = send_list.shape
    return pl.pallas_call(
        pick_kernel,
        out_shape=jax.ShapeDtypeStruct((peers * cap, snapshots.shape[1]), F32),
        in_specs=[pl.BlockSpec(memory_space=pltpu.SMEM), pl.BlockSpec(memory_space=pltpu.VMEM)],
        out_specs=pl.BlockSpec(memory_space=pltpu.VMEM),
        compiler_params=pltpu.CompilerParams(vmem_limit_bytes=VMEM_LIMIT),
        name="pick_donors",
    )(send_list, snapshots)


def weave_kernel(runs, run_rows, cap, peers, me_ref, sten_ref, wt_ref, mat_ref, slot_ref):
    step = pl.program_id(0)
    iota = lax.broadcasted_iota(jnp.int32, (cap, run_rows), 0)
    for sub in range(runs):
        run = step * runs + sub
        peer = lax.rem(me_ref[0] + run, peers)
        cols = slice(sub * run_rows, (sub + 1) * run_rows)
        dense = jnp.zeros((cap, run_rows), F32)
        for s in range(sten_ref.shape[0]):
            place = jnp.broadcast_to(sten_ref[s : s + 1, cols] - peer * cap, (cap, run_rows))
            value = jnp.broadcast_to(wt_ref[s : s + 1, cols], (cap, run_rows))
            dense = dense + jnp.where(iota == place, value, 0.0)
        high = dense.astype(BF16)
        high_f = high.astype(F32)
        low_f = (dense - high_f).astype(BF16).astype(F32)
        pair = jnp.concatenate([high_f, low_f], axis=0)
        mat = pair.T.astype(BF16)
        mat_ref[cols, :] = mat
        gram = jnp.dot(pair.astype(BF16), mat, preferred_element_type=F32)
        half = gram[:cap] + gram[cap:]
        slot_ref[sub * cap : (sub + 1) * cap, :] = half[:, :cap] + half[:, cap:]


def weave(me, stencil, weights, peers, cap):
    rows = stencil.shape[0]
    run_rows = rows // peers
    runs = max(1, 2048 // run_rows)
    block = runs * run_rows
    grid_spec = pltpu.PrefetchScalarGridSpec(
        num_scalar_prefetch=1,
        grid=(peers // runs,),
        in_specs=[
            pl.BlockSpec((stencil.shape[1], block), lambda i, m: (0, i)),
            pl.BlockSpec((stencil.shape[1], block), lambda i, m: (0, i)),
        ],
        out_specs=[
            pl.BlockSpec((block, 2 * cap), lambda i, m: (i, 0)),
            pl.BlockSpec((runs * cap, cap), lambda i, m: (i, 0)),
        ],
    )
    return pl.pallas_call(
        functools.partial(weave_kernel, runs, run_rows, cap, peers),
        out_shape=[jax.ShapeDtypeStruct((rows, 2 * cap), BF16), jax.ShapeDtypeStruct((peers * cap, cap), F32)],
        grid_spec=grid_spec,
        compiler_params=pltpu.CompilerParams(vmem_limit_bytes=VMEM_LIMIT),
        cost_estimate=pl.CostEstimate(flops=8 * 10**9, bytes_accessed=40 * 10**6, transcendentals=0),
        name="weave",
    )(me, stencil.T, weights.T)


def two_sum(a, b):
    s = a + b
    t = s - a
    return s, (a - (s - t)) + (b - t)


def merge(a, b):
    s, e = two_sum(a[0], b[0])
    low = (a[1] + b[1]) + e
    high = s + low
    return high, low - (high - s)


def gram_kernel(peers, cap, me_ref, x_ref, slot_ref, keep_ref, give_ref, z_ref):
    snaps = x_ref.shape[1]

    def one_run(run, carry):
        peer = lax.rem(me_ref[0] + run, peers)
        at = pl.ds(pl.multiple_of(peer * cap, cap), cap)
        frm = pl.ds(pl.multiple_of(run * cap, cap), cap)
        z_ref[at, :] = exact(slot_ref[frm, :], x_ref[at, :])
        return carry

    lax.fori_loop(0, peers, one_run, 0, unroll=4)
    chunk = 256

    def one_chunk(i, carry):
        at = pl.ds(pl.multiple_of(i * chunk, chunk), chunk)
        part = exact(x_ref[at, :], z_ref[at, :], ((0,), (0,)))
        s, e = two_sum(carry[0], part)
        return s, carry[1] + e

    zero = jnp.zeros((snaps, snaps), F32)
    high, low = lax.fori_loop(0, peers * cap // chunk, one_chunk, (zero, zero), unroll=2)
    half = snaps // 2
    core = lax.rem(me_ref[0], 2)
    for ref, want in ((keep_ref, 0), (give_ref, 1)):
        for i, part in enumerate((high, low)):
            ref[i] = jnp.where(core == want, part[:half], part[half:])


def local_gram(me, x, slots, peers, cap):
    snaps = x.shape[1]
    shape = jax.ShapeDtypeStruct((2, snaps // 2, snaps), F32)
    vmem = pl.BlockSpec(memory_space=pltpu.VMEM)
    return pl.pallas_call(
        functools.partial(gram_kernel, peers, cap),
        out_shape=[shape, shape],
        in_specs=[pl.BlockSpec(memory_space=pltpu.SMEM), vmem, vmem],
        out_specs=[vmem, vmem],
        scratch_shapes=[pltpu.VMEM(x.shape, F32)],
        compiler_params=pltpu.CompilerParams(vmem_limit_bytes=VMEM_LIMIT),
        name="local_gram",
    )(me, x, slots)


def hop(value, mask, peers):
    return lax.ppermute(value, "rows", [(i, i ^ mask) for i in range(peers)])


def sum_pairs(keep, give, peers):
    other = hop(give, 1, peers)
    mine = merge((keep[0], keep[1]), (other[0], other[1]))
    bit = 2
    while bit < peers:
        now = jnp.stack(mine)
        if bit * 2 < peers:
            a = hop(now, bit, peers)
            b = hop(now, 2 * bit, peers)
            c = hop(now, 3 * bit, peers)
            mine = merge(merge(mine, (a[0], a[1])), merge((b[0], b[1]), (c[0], c[1])))
            bit *= 4
        else:
            a = hop(now, bit, peers)
            mine = merge(mine, (a[0], a[1]))
            bit *= 2
    now = jnp.stack(mine)
    return now, hop(now, 1, peers)


def power_scale(value):
    scale = jnp.ones_like(value)
    for k in (32, 16, 8, 4, 2, 1):
        small = value < 2.0 ** (2 - 2 * k)
        value = jnp.where(small, value * 2.0 ** (2 * k), value)
        scale = jnp.where(small, scale * 2.0**k, scale)
    for k in (32, 16, 8, 4, 2, 1):
        large = value >= 2.0 ** (2 * k)
        value = jnp.where(large, value * 2.0 ** (-2 * k), value)
        scale = jnp.where(large, scale * 2.0**-k, scale)
    return scale


def factor(gram):
    size = gram.shape[0]
    sub = lax.broadcasted_iota(jnp.int32, (TILE, size), 0)
    lane = lax.broadcasted_iota(jnp.int32, (TILE, size), 1)
    left = gram
    right = (lax.broadcasted_iota(jnp.int32, (size, size), 0) == lax.broadcasted_iota(jnp.int32, (size, size), 1)).astype(F32)
    tops, inverses = [], []
    for j in range(size // TILE):
        head, tail = left[:TILE], left[TILE:]
        ihead, itail = right[:TILE], right[TILE:]
        pivots = jnp.ones((TILE, size), F32)
        for k in range(TILE):
            col = j * TILE + k
            row = jnp.broadcast_to(head[k : k + 1, :], (TILE, size))
            irow = jnp.broadcast_to(ihead[k : k + 1, :], (TILE, size))
            pivot = jnp.broadcast_to(row[:, col : col + 1], (TILE, size))
            pivots = jnp.where(sub == k, pivot, pivots)
            over = 1.0 / pivot
            row = row * over
            irow = irow * over
            coef = jnp.where(sub > k, jnp.broadcast_to(head[:, col : col + 1], (TILE, size)), 0.0)
            head = head - coef * row
            ihead = ihead - coef * irow
            rest = tail.shape[0]
            if rest:
                coef = jnp.broadcast_to(tail[:, col : col + 1], (rest, size))
                many = rest // TILE
                tail = tail - coef * jnp.concatenate([row] * many, axis=0)
                itail = itail - coef * jnp.concatenate([irow] * many, axis=0)
        root = lax.rsqrt(pivots)
        tops.append(jnp.where(lane >= sub + j * TILE, head * root, 0.0))
        inverses.append(ihead * root)
        left, right = tail, itail
    return jnp.concatenate(tops, axis=0), jnp.concatenate(inverses, axis=0)


def slices(value):
    out = []
    for bits in (6, 14, 22, 30):
        big = 1.5 * 2.0 ** (23 - bits)
        piece = (value + big) - big
        value = value - piece
        out.append(piece.astype(BF16))
    return out


def triangular(high, low):
    size = high.shape[0]
    rows = lax.broadcasted_iota(jnp.int32, (size, size), 0)
    cols = lax.broadcasted_iota(jnp.int32, (size, size), 1)
    diagonal = jnp.where(rows == cols, high, 0.0)
    across = power_scale(jnp.sum(diagonal, axis=0, keepdims=True))
    down = power_scale(jnp.sum(diagonal, axis=1, keepdims=True))
    high = high * across * down
    low = low * across * down
    upper, inv_t = factor(high)
    up = slices(upper)
    lo = slices(upper.T)
    first = jnp.dot(lo[0], jnp.concatenate(up, axis=1), preferred_element_type=F32)
    second = jnp.dot(lo[1], jnp.concatenate(up[:3], axis=1), preferred_element_type=F32)
    third = jnp.dot(lo[2], jnp.concatenate(up[:2], axis=1), preferred_element_type=F32)
    fourth = jnp.dot(lo[3], up[0], preferred_element_type=F32)
    rest = high - first[:, :size]
    rest = rest - (first[:, size : 2 * size] + second[:, :size])
    rest = rest - second[:, size : 2 * size]
    rest = rest - (first[:, 2 * size : 3 * size] + third[:, :size])
    rest = rest + low
    rest = rest - ((first[:, 3 * size :] + fourth) + (second[:, 2 * size :] + third[:, size:]))
    inv = inv_t.T
    error = exact(exact(inv_t, rest), inv)
    weight = jnp.where(rows < cols, 1.0, jnp.where(rows == cols, 0.5, 0.0))
    shift = error * weight
    for _ in range(2):
        shift = (error - rough(shift, shift, ((0,), (0,)))) * weight
    square = rough(shift, shift)
    minus = square - shift
    minus = minus + rough(square, minus)
    inv = inv + exact(inv, minus)
    upper = upper + exact(shift, upper)
    return upper * (1.0 / across), inv * down


def basis_kernel(runs, run_rows, cap, peers, scale, me_ref, mine_ref, other_ref, x_ref, mat_ref, out_ref, r_ref, inv_ref):
    step = pl.program_id(0)

    @pl.when(step == 0)
    def _():
        core = lax.rem(me_ref[0], 2)
        parts = []
        for i in range(2):
            mine, other = mine_ref[i], other_ref[i]
            top = jnp.where(core == 0, mine, other)
            low = jnp.where(core == 0, other, mine)
            parts.append(jnp.concatenate([top, low], axis=0))
        upper, inv = triangular(parts[0], parts[1])
        r_ref[...] = upper * (1.0 / scale)
        inv_ref[...] = inv * scale

    for sub in range(runs):
        peer = lax.rem(me_ref[0] + step * runs + sub, peers)
        at = pl.ds(pl.multiple_of(peer * cap, cap), cap)
        y = exact(x_ref[at, :], inv_ref[...])
        high = y.astype(BF16)
        low = (y - high.astype(F32)).astype(BF16)
        both = jnp.concatenate([high, low], axis=1)
        both = jnp.concatenate([both, both], axis=0)
        rows = slice(sub * run_rows, (sub + 1) * run_rows)
        twice = jnp.dot(mat_ref[rows, :], both, preferred_element_type=F32)
        snaps = y.shape[1]
        out_ref[rows, :] = twice[:, :snaps] + twice[:, snaps:]


def make_basis(me, mine, other, x, mat, peers, cap, total_rows):
    rows = mat.shape[0]
    snaps = x.shape[1]
    run_rows = rows // peers
    runs = max(1, 1024 // run_rows)
    block = runs * run_rows
    whole = lambda *dims: pl.BlockSpec(dims, lambda i, m: (0,) * len(dims))
    grid_spec = pltpu.PrefetchScalarGridSpec(
        num_scalar_prefetch=1,
        grid=(peers // runs,),
        in_specs=[whole(*mine.shape), whole(*other.shape), whole(*x.shape), pl.BlockSpec((block, 2 * cap), lambda i, m: (i, 0))],
        out_specs=[pl.BlockSpec((block, snaps), lambda i, m: (i, 0)), whole(snaps, snaps)],
        scratch_shapes=[pltpu.VMEM((snaps, snaps), F32)],
    )
    return pl.pallas_call(
        functools.partial(basis_kernel, runs, run_rows, cap, peers, math.sqrt(total_rows)),
        out_shape=[jax.ShapeDtypeStruct((rows, snaps), F32), jax.ShapeDtypeStruct((snaps, snaps), F32)],
        grid_spec=grid_spec,
        compiler_params=pltpu.CompilerParams(vmem_limit_bytes=VMEM_LIMIT),
        name="make_basis",
    )(me, mine, other, x, mat)


def body(snapshots, send_list, stencil, weights):
    peers, cap = send_list.shape
    total_rows = stencil.shape[0] * peers
    me = lax.axis_index("rows").astype(jnp.int32).reshape(1)
    outgoing = pick_donors(snapshots, send_list)
    x = lax.all_to_all(outgoing, "rows", split_axis=0, concat_axis=0, tiled=True)
    mat, slots = weave(me, stencil, weights, peers, cap)
    keep, give = local_gram(me, x, slots, peers, cap)
    mine, other = sum_pairs(keep, give, peers)
    basis, r_factor = make_basis(me, mine, other, x, mat, peers, cap, total_rows)
    return (basis, r_factor)


def solution(mesh):
    return jax.shard_map(
        body,
        mesh=mesh,
        in_specs=(P("rows", None), P("rows", None), P("rows", None), P("rows", None)),
        out_specs=(P("rows", None), P()),
        check_vma=False,
    )
```

time: 1190 us -> 102 us (0.09)
  local copies, waits for them, and re-layouts: 474 us -> 1.59 us
  between operations: 267 us -> 0.71 us
  waiting for transfers between devices: 259 us -> 26.3 us
  matrix products: 111 us -> 0 us
  other arithmetic: 66.1 us -> 0.93 us
  Pallas kernels: 0 us -> 56.7 us
    gather x9 -> x0, local copies, waits for them, and re-layouts: 448 us -> none  [the longest x8 438 us: body(): field = field + weights[:, s][:, None] * flat[stencil[:, s]]]
    psum x2 -> x0, waiting for transfers between devices: 235 us -> none  [normed_factor(): gram = lax.psum(local, 'rows')]
    dot_general x257 -> x0, matrix products: 111 us -> none  [product(): jnp.dot(left, right, precision=lax.Precision.HIGHEST, preferred_element_t...]
    pallas_call x0 -> x4, Pallas kernels: none -> 56.7 us  [the longest x1 36.1 us: make_basis(): pl.pallas_call(functools.partial(basis_kernel, runs, run_rows, cap, peers...]
    add x1 -> x2, other arithmetic: 25.8 us -> 0.09 us  [merge(): low = a[1] + b[1] + e]
    another operation x6 -> x3, other arithmetic: 24.8 us -> 0.02 us  [sum_pairs(): now = jnp.stack(mine)]
    slice x25 -> x0, local copies, waits for them, and re-layouts: 18.1 us -> none  [the longest x8 5.83 us: upper_inverse(): top_inv = upper_inverse(upper[:half, :half])]
  transfers between devices with their start and end apart: 3 -> 9, of which waited for: 3 -> 8; matrix products, arithmetic and copies ran while one was open for 0% -> 0% of each run, Pallas kernels for 0% -> 10%
where the time goes in v1:
time: 102 us
  Pallas kernels  56.7 us (56%)
  waiting for transfers between devices  26.3 us (26%)
  starting transfers between devices  15.4 us (15%)
  local copies, waits for them, and re-layouts  1.59 us (2%)
    pallas_call x1, Pallas kernels, make_basis(): pl.pallas_call(functools.partial(basis_kernel, runs, run_rows, cap, peers...  36.1 us
    all_to_all x1, waiting for transfers between devices, body(): lax.all_to_all(outgoing, 'rows', split_axis=0, concat_axis=0, tiled=True)  16.5 us
    ppermute x8, waiting for transfers between devices, hop(): return lax.ppermute(value, 'rows', [(i, i ^ mask) for i in range(peers)])  9.83 us
    pallas_call x1, Pallas kernels, weave(): pl.pallas_call(functools.partial(weave_kernel, runs, run_rows, cap, peers...  9.74 us
    ppermute x8, starting transfers between devices, hop(): return lax.ppermute(value, 'rows', [(i, i ^ mask) for i in range(peers)])  8.08 us
    all_to_all x1, starting transfers between devices, body(): lax.all_to_all(outgoing, 'rows', split_axis=0, concat_axis=0, tiled=True)  7.3 us
    pallas_call x1, Pallas kernels, local_gram(): pl.pallas_call(functools.partial(gram_kernel, peers, cap), out_shape=[sha...  5.92 us
    pallas_call x1, Pallas kernels, pick_donors(): pl.pallas_call(pick_kernel, out_shape=jax.ShapeDtypeStruct((peers * cap,...  4.95 us
  transfers between devices with their start and end apart: 9, of which 8 were waited for; matrix products, arithmetic and copies ran while one was open for 0% of the time, Pallas kernels for 10%

profile of v1, /device:TPU:0, one launch (start us, length us, event | category | flops | bytes accessed | tf_op | source)
XLA Modules:
  0.0 101.6 jit_solution(7084947641065468917)
XLA Ops:
  0.6 5.0 %pick_donors.1 = f32[2048,128]{1,0:T(8,128)} custom-call(s32[32,64]{1,0:T(8,128)} %send_ref.1, f32[8192,128]{1,0:T(8,128)} %snap_ref.1), custom_call_target="tpu_custom_call" | custom-call | tf_op jit(solution)/shard_map/pick_donors/pallas_call | solution.py:40
  5.6 7.3 %all-to-all-start = ((f32[32,64,128]{2,1,0:T(8,128)}), f32[32,64,128]{2,1,0:T(8,128)S(1)}, u32[]{:S(2)}, u32[]{:S(2)}) async-start(f32[32,64,128]{2,1,0:T(8,128)} %bitcast.7), calls=%async_computation | async-start | bytes 2097152 | tf_op jit(solution)/shard_map/all_to_all | solution.py:333
  12.9 9.7 %weave.1 = (bf16[16384,128]{1,0:T(8,128)(2,1)}, f32[2048,64]{1,0:T(8,128)}) custom-call(s32[1]{0:T(128)} %bitcast.me_ref, s32[8,16384]{1,0:T(8,128)} %bitcast.8, f32[8,16384]{1,0:T(8,128)} %bitcast.9), custom_call_target="tpu_custom_call" | custom-call | flops 8000000000 | bytes 40000000 | tf_op jit(solution)/shard_map/weave/pallas_call | solution.py:90
  22.6 16.5 %all-to-all-done = f32[32,64,128]{2,1,0:T(8,128)S(1)} async-done(((f32[32,64,128]{2,1,0:T(8,128)}), f32[32,64,128]{2,1,0:T(8,128)S(1)}, u32[]{:S(2)}, u32[]{:S(2)}) %all-to-all-start) | async-done | bytes 1048608 | tf_op jit(solution)/shard_map/all_to_all | solution.py:333
  39.1 0.0 copy-start
  39.1 1.0 copy-done
  40.1 5.9 %local_gram.1 = (f32[2,64,128]{2,1,0:T(8,128)}, f32[2,64,128]{2,1,0:T(8,128)}) custom-call(s32[1]{0:T(128)} %bitcast.me_ref, f32[2048,128]{1,0:T(8,128)} %bitcast.5, f32[2048,64]{1,0:T(8,128)} %get-tuple-element.6.slot_ref), custom_call_target="tpu_custom_call" | custom-call | tf_op jit(solution)/shard_map/local_gram/pallas_call | solution.py:145
  46.0 0.0 collective-permute-start
  46.0 1.5 %collective-permute-done = f32[2,64,128]{2,1,0:T(8,128)S(1)} collective-permute-done((f32[2,64,128]{2,1,0:T(8,128)}, f32[2,64,128]{2,1,0:T(8,128)S(1)}, u32[]{:S(2)}, u32[]{:S(2)}) %collective-permute-start) | collective-permute-done | bytes 65568 | tf_op jit(solution)/shard_map/ppermute | solution.py:157
  47.5 0.8 subtract_subtract_fusion.2
  48.3 2.5 %collective-permute-start.3 = (f32[2,64,128]{2,1,0:T(8,128)S(1)}, f32[2,64,128]{2,1,0:T(8,128)S(1)}, u32[]{:S(2)}, u32[]{:S(2)}) collective-permute-start(f32[2,64,128]{2,1,0:T(8,128)S(1)} %pad_maximum_fusion), channel_id=1, source_target_pairs={{0,6},{1,7},{2,4},{3,5},{4,2},{5,3},{6,0},{7,1},{8,14},{9,15},{10,... | collective-permute-start | bytes 196616 | tf_op jit(solution)/shard_map/ppermute | solution.py:157
  50.8 0.5 collective-permute-start.2
  51.3 0.6 collective-permute-start.1
  51.8 1.7 %collective-permute-done.3 = f32[2,64,128]{2,1,0:T(8,128)S(1)} collective-permute-done((f32[2,64,128]{2,1,0:T(8,128)S(1)}, f32[2,64,128]{2,1,0:T(8,128)S(1)}, u32[]{:S(2)}, u32[]{:S(2)}) %collective-permute-start.3) | collective-permute-done | bytes 65568 | tf_op jit(solution)/shard_map/ppermute | solution.py:157
  53.6 1.5 %collective-permute-done.2 = f32[2,64,128]{2,1,0:T(8,128)S(1)} collective-permute-done((f32[2,64,128]{2,1,0:T(8,128)S(1)}, f32[2,64,128]{2,1,0:T(8,128)S(1)}, u32[]{:S(2)}, u32[]{:S(2)}) %collective-permute-start.2) | collective-permute-done | bytes 65568 | tf_op jit(solution)/shard_map/ppermute | solution.py:157
  55.0 0.5 collective-permute-done.1
  55.6 1.5 %collective-permute-start.6 = (f32[2,64,128]{2,1,0:T(8,128)S(1)}, f32[2,64,128]{2,1,0:T(8,128)S(1)}, u32[]{:S(2)}, u32[]{:S(2)}) collective-permute-start(f32[2,64,128]{2,1,0:T(8,128)S(1)} %pad_maximum_fusion.1), channel_id=1, source_target_pairs={{0,24},{1,25},{2,26},{3,27},{4,28},{5,29},{6,30},{7,31},{8,16},{9,... | collective-permute-start | bytes 196616 | tf_op jit(solution)/shard_map/ppermute | solution.py:157
  57.2 0.6 collective-permute-start.5
  57.8 2.3 %collective-permute-start.4 = (f32[2,64,128]{2,1,0:T(8,128)S(1)}, f32[2,64,128]{2,1,0:T(8,128)S(1)}, u32[]{:S(2)}, u32[]{:S(2)}) collective-permute-start(f32[2,64,128]{2,1,0:T(8,128)S(1)} %pad_maximum_fusion.1), channel_id=1, source_target_pairs={{0,8},{1,9},{2,10},{3,11},{4,12},{5,13},{6,14},{7,15},{8,0},{9,1},... | collective-permute-start | bytes 196616 | tf_op jit(solution)/shard_map/ppermute | solution.py:157
  60.1 1.8 %collective-permute-done.6 = f32[2,64,128]{2,1,0:T(8,128)S(1)} collective-permute-done((f32[2,64,128]{2,1,0:T(8,128)S(1)}, f32[2,64,128]{2,1,0:T(8,128)S(1)}, u32[]{:S(2)}, u32[]{:S(2)}) %collective-permute-start.6) | collective-permute-done | bytes 65568 | tf_op jit(solution)/shard_map/ppermute | solution.py:157
  61.9 1.6 %collective-permute-done.5 = f32[2,64,128]{2,1,0:T(8,128)S(1)} collective-permute-done((f32[2,64,128]{2,1,0:T(8,128)S(1)}, f32[2,64,128]{2,1,0:T(8,128)S(1)}, u32[]{:S(2)}, u32[]{:S(2)}) %collective-permute-start.5) | collective-permute-done | bytes 65568 | tf_op jit(solution)/shard_map/ppermute | solution.py:157
  63.5 0.0 collective-permute-done.4
  63.6 0.0 copy-start.1
  63.6 0.1 collective-permute-start.7
  63.7 1.2 %collective-permute-done.7.other_ref = f32[2,64,128]{2,1,0:T(8,128)S(1)} collective-permute-done((f32[2,64,128]{2,1,0:T(8,128)S(1)}, f32[2,64,128]{2,1,0:T(8,128)S(1)}, u32[]{:S(2)}, u32[]{:S(2)}) %collective-permute-start.7) | collective-permute-done | bytes 65568 | tf_op jit(solution)/shard_map/ppermute | solution.py:157
  64.9 0.0 copy-start.2
  64.9 0.0 copy-done.1
  64.9 0.6 copy-done.2
  65.5 36.1 %make_basis.1 = (f32[16384,128]{1,0:T(8,128)}, f32[128,128]{1,0:T(8,128)}) custom-call(s32[1]{0:T(128)} %bitcast.me_ref, f32[2,64,128]{2,1,0:T(8,128)} %copy-done.1, f32[2,64,128]{2,1,0:T(8,128)} %copy-done.2, f32[2048,128]{1,0:T(8,128)} %bitcast.6, bf16[16384,128]{1,0:T(8,128)(2,1)} %get-tuple-element.9.mat_ref), custom_call_target="tpu_custom_call" | custom-call | tf_op jit(solution)/shard_map/make_basis/pallas_call | solution.py:319
  (7 shorter events, 0.1 us)
Async XLA Ops:
  5.6 33.5 %all-to-all-start = ((f32[32,64,128]{2,1,0:T(8,128)}), f32[32,64,128]{2,1,0:T(8,128)S(1)}, u32[]{:S(2)}, u32[]{:S(2)}) async-start(f32[32,64,128]{2,1,0:T(8,128)} %bitcast.7), calls=%async_computation | async-start | bytes 2097152 | tf_op jit(solution)/shard_map/all_to_all | solution.py:333
  39.1 1.0 copy-start
  46.0 1.5 %collective-permute-start = (f32[2,64,128]{2,1,0:T(8,128)}, f32[2,64,128]{2,1,0:T(8,128)S(1)}, u32[]{:S(2)}, u32[]{:S(2)}) collective-permute-start(f32[2,64,128]{2,1,0:T(8,128)} %get-tuple-element.8), channel_id=1, source_target_pairs={{0,1},{1,0},{2,3},{3,2},{4,5},{5,4},{6,7},{7,6},{8,9},{9,8},{10,11... | collective-permute-start | bytes 196616 | tf_op jit(solution)/shard_map/ppermute | solution.py:157
  48.3 5.3 %collective-permute-start.3 = (f32[2,64,128]{2,1,0:T(8,128)S(1)}, f32[2,64,128]{2,1,0:T(8,128)S(1)}, u32[]{:S(2)}, u32[]{:S(2)}) collective-permute-start(f32[2,64,128]{2,1,0:T(8,128)S(1)} %pad_maximum_fusion), channel_id=1, source_target_pairs={{0,6},{1,7},{2,4},{3,5},{4,2},{5,3},{6,0},{7,1},{8,14},{9,15},{10,... | collective-permute-start | bytes 196616 | tf_op jit(solution)/shard_map/ppermute | solution.py:157
  50.8 4.3 %collective-permute-start.2 = (f32[2,64,128]{2,1,0:T(8,128)S(1)}, f32[2,64,128]{2,1,0:T(8,128)S(1)}, u32[]{:S(2)}, u32[]{:S(2)}) collective-permute-start(f32[2,64,128]{2,1,0:T(8,128)S(1)} %pad_maximum_fusion), channel_id=1, source_target_pairs={{0,4},{1,5},{2,6},{3,7},{4,0},{5,1},{6,2},{7,3},{8,12},{9,13},{10,... | collective-permute-start | bytes 196616 | tf_op jit(solution)/shard_map/ppermute | solution.py:157
  51.3 4.3 %collective-permute-start.1 = (f32[2,64,128]{2,1,0:T(8,128)S(1)}, f32[2,64,128]{2,1,0:T(8,128)S(1)}, u32[]{:S(2)}, u32[]{:S(2)}) collective-permute-start(f32[2,64,128]{2,1,0:T(8,128)S(1)} %pad_maximum_fusion), channel_id=1, source_target_pairs={{0,2},{1,3},{2,0},{3,1},{4,6},{5,7},{6,4},{7,5},{8,10},{9,11},{10,... | collective-permute-start | bytes 196616 | tf_op jit(solution)/shard_map/ppermute | solution.py:157
  55.6 6.3 %collective-permute-start.6 = (f32[2,64,128]{2,1,0:T(8,128)S(1)}, f32[2,64,128]{2,1,0:T(8,128)S(1)}, u32[]{:S(2)}, u32[]{:S(2)}) collective-permute-start(f32[2,64,128]{2,1,0:T(8,128)S(1)} %pad_maximum_fusion.1), channel_id=1, source_target_pairs={{0,24},{1,25},{2,26},{3,27},{4,28},{5,29},{6,30},{7,31},{8,16},{9,... | collective-permute-start | bytes 196616 | tf_op jit(solution)/shard_map/ppermute | solution.py:157
  57.2 6.4 %collective-permute-start.5 = (f32[2,64,128]{2,1,0:T(8,128)S(1)}, f32[2,64,128]{2,1,0:T(8,128)S(1)}, u32[]{:S(2)}, u32[]{:S(2)}) collective-permute-start(f32[2,64,128]{2,1,0:T(8,128)S(1)} %pad_maximum_fusion.1), channel_id=1, source_target_pairs={{0,16},{1,17},{2,18},{3,19},{4,20},{5,21},{6,22},{7,23},{8,24},{9,... | collective-permute-start | bytes 196616 | tf_op jit(solution)/shard_map/ppermute | solution.py:157
  57.8 5.7 %collective-permute-start.4 = (f32[2,64,128]{2,1,0:T(8,128)S(1)}, f32[2,64,128]{2,1,0:T(8,128)S(1)}, u32[]{:S(2)}, u32[]{:S(2)}) collective-permute-start(f32[2,64,128]{2,1,0:T(8,128)S(1)} %pad_maximum_fusion.1), channel_id=1, source_target_pairs={{0,8},{1,9},{2,10},{3,11},{4,12},{5,13},{6,14},{7,15},{8,0},{9,1},... | collective-permute-start | bytes 196616 | tf_op jit(solution)/shard_map/ppermute | solution.py:157
  63.6 1.3 %copy-start.1 = (f32[2,64,128]{2,1,0:T(8,128)}, f32[2,64,128]{2,1,0:T(8,128)S(1)}, u32[]{:S(2)}) copy-start(f32[2,64,128]{2,1,0:T(8,128)S(1)} %pad_maximum_fusion.2.mine_ref) | copy-start | bytes 196612
  63.6 1.3 %collective-permute-start.7 = (f32[2,64,128]{2,1,0:T(8,128)S(1)}, f32[2,64,128]{2,1,0:T(8,128)S(1)}, u32[]{:S(2)}, u32[]{:S(2)}) collective-permute-start(f32[2,64,128]{2,1,0:T(8,128)S(1)} %pad_maximum_fusion.2.mine_ref), channel_id=1, source_target_pairs={{0,1},{1,0},{2,3},{3,2},{4,5},{5,4},{6,7},{7,6},{8,9},{9,8},{10,11... | collective-permute-start | bytes 196616 | tf_op jit(solution)/shard_map/ppermute | solution.py:157
  64.9 0.6 copy-start.2

commit v2 on v1

--- a/solution.py
+++ b/solution.py
@@ -11,7 +11,6 @@
 F32 = jnp.float32
 BF16 = jnp.bfloat16
 TILE = 8
-VMEM_LIMIT = 56 * 1024 * 1024
 
 
 def exact(left, right, dims=((1,), (0,))):
@@ -22,14 +21,35 @@
     return lax.dot_general(left.astype(BF16), right.astype(BF16), (dims, ((), ())), preferred_element_type=F32)
 
 
-def pick_kernel(send_ref, snap_ref, out_ref):
+PIECES = 8
+MOST_VMEM = 60 * 1024 * 1024
+
+
+def limit(*arrays):
+    total = 0
+    for shape, dtype in arrays:
+        lanes = -(-shape[-1] // 128) * 128
+        total += math.prod(shape[:-1]) * lanes * jnp.dtype(dtype).itemsize
+    return total + 8 * 1024 * 1024
+
+
+def pick_kernel(send_ref, snap_ref, out_ref, held_ref, sems):
     peers, cap = send_ref.shape
+    part = snap_ref.shape[0] // PIECES
+    copies = []
+    for i in range(PIECES):
+        at = pl.ds(i * part, part)
+        copy = pltpu.make_async_copy(snap_ref.at[at, :], held_ref.at[at, :], sems.at[i])
+        copy.start()
+        copies.append(copy)
+    for copy in copies:
+        copy.wait()
 
     def one_peer(peer, carry):
         base = peer * cap
         for slot in range(cap):
             node = send_ref[peer, slot]
-            out_ref[pl.ds(base + slot, 1), :] = snap_ref[pl.ds(node, 1), :]
+            out_ref[pl.ds(base + slot, 1), :] = held_ref[pl.ds(node, 1), :]
         return carry
 
     lax.fori_loop(0, peers, one_peer, 0)
@@ -37,12 +57,14 @@
 
 def pick_donors(snapshots, send_list):
     peers, cap = send_list.shape
+    snaps = snapshots.shape[1]
     return pl.pallas_call(
         pick_kernel,
-        out_shape=jax.ShapeDtypeStruct((peers * cap, snapshots.shape[1]), F32),
-        in_specs=[pl.BlockSpec(memory_space=pltpu.SMEM), pl.BlockSpec(memory_space=pltpu.VMEM)],
+        out_shape=jax.ShapeDtypeStruct((peers * cap, snaps), F32),
+        in_specs=[pl.BlockSpec(memory_space=pltpu.SMEM), pl.BlockSpec(memory_space=pltpu.HBM)],
         out_specs=pl.BlockSpec(memory_space=pltpu.VMEM),
-        compiler_params=pltpu.CompilerParams(vmem_limit_bytes=VMEM_LIMIT),
+        scratch_shapes=[pltpu.VMEM(snapshots.shape, F32), pltpu.SemaphoreType.DMA((PIECES,))],
+        compiler_params=pltpu.CompilerParams(vmem_limit_bytes=MOST_VMEM),
         name="pick_donors",
     )(send_list, snapshots)
 
@@ -91,7 +113,7 @@
         functools.partial(weave_kernel, runs, run_rows, cap, peers),
         out_shape=[jax.ShapeDtypeStruct((rows, 2 * cap), BF16), jax.ShapeDtypeStruct((peers * cap, cap), F32)],
         grid_spec=grid_spec,
-        compiler_params=pltpu.CompilerParams(vmem_limit_bytes=VMEM_LIMIT),
+        compiler_params=pltpu.CompilerParams(vmem_limit_bytes=16 * 1024 * 1024),
         cost_estimate=pl.CostEstimate(flops=8 * 10**9, bytes_accessed=40 * 10**6, transcendentals=0),
         name="weave",
     )(me, stencil.T, weights.T)
@@ -120,7 +142,7 @@
         z_ref[at, :] = exact(slot_ref[frm, :], x_ref[at, :])
         return carry
 
-    lax.fori_loop(0, peers, one_run, 0, unroll=4)
+    lax.fori_loop(0, peers, one_run, 0, unroll=16)
     chunk = 256
 
     def one_chunk(i, carry):
@@ -130,7 +152,7 @@
         return s, carry[1] + e
 
     zero = jnp.zeros((snaps, snaps), F32)
-    high, low = lax.fori_loop(0, peers * cap // chunk, one_chunk, (zero, zero), unroll=2)
+    high, low = lax.fori_loop(0, peers * cap // chunk, one_chunk, (zero, zero), unroll=8)
     half = snaps // 2
     core = lax.rem(me_ref[0], 2)
     for ref, want in ((keep_ref, 0), (give_ref, 1)):
@@ -148,7 +170,7 @@
         in_specs=[pl.BlockSpec(memory_space=pltpu.SMEM), vmem, vmem],
         out_specs=[vmem, vmem],
         scratch_shapes=[pltpu.VMEM(x.shape, F32)],
-        compiler_params=pltpu.CompilerParams(vmem_limit_bytes=VMEM_LIMIT),
+        compiler_params=pltpu.CompilerParams(vmem_limit_bytes=limit((x.shape, F32), (x.shape, F32), (slots.shape, F32))),
         name="local_gram",
     )(me, x, slots)
 
@@ -192,37 +214,49 @@
 
 def factor(gram):
     size = gram.shape[0]
-    sub = lax.broadcasted_iota(jnp.int32, (TILE, size), 0)
-    lane = lax.broadcasted_iota(jnp.int32, (TILE, size), 1)
+    tile = (TILE, size)
+    sub = lax.broadcasted_iota(jnp.int32, tile, 0)
+    lane = lax.broadcasted_iota(jnp.int32, tile, 1)
     left = gram
     right = (lax.broadcasted_iota(jnp.int32, (size, size), 0) == lax.broadcasted_iota(jnp.int32, (size, size), 1)).astype(F32)
     tops, inverses = [], []
     for j in range(size // TILE):
-        head, tail = left[:TILE], left[TILE:]
-        ihead, itail = right[:TILE], right[TILE:]
-        pivots = jnp.ones((TILE, size), F32)
+        rest = left.shape[0] - TILE
+        many = rest // TILE
+        columns = [left[:, j * TILE + k : j * TILE + k + 1] for k in range(TILE)]
+        heads = [jnp.broadcast_to(column[:TILE], tile) for column in columns]
+        tails = [jnp.broadcast_to(column[TILE:], (rest, size)) for column in columns] if rest else []
+        block = [[jnp.broadcast_to(heads[k][i : i + 1, :], tile) for k in range(i + 1)] for i in range(TILE)]
+        rows = [jnp.broadcast_to(left[k : k + 1, :], tile) for k in range(TILE)]
+        irows = [jnp.broadcast_to(right[k : k + 1, :], tile) for k in range(TILE)]
+        over, coef = [], {}
         for k in range(TILE):
-            col = j * TILE + k
-            row = jnp.broadcast_to(head[k : k + 1, :], (TILE, size))
-            irow = jnp.broadcast_to(ihead[k : k + 1, :], (TILE, size))
-            pivot = jnp.broadcast_to(row[:, col : col + 1], (TILE, size))
-            pivots = jnp.where(sub == k, pivot, pivots)
-            over = 1.0 / pivot
-            row = row * over
-            irow = irow * over
-            coef = jnp.where(sub > k, jnp.broadcast_to(head[:, col : col + 1], (TILE, size)), 0.0)
-            head = head - coef * row
-            ihead = ihead - coef * irow
-            rest = tail.shape[0]
-            if rest:
-                coef = jnp.broadcast_to(tail[:, col : col + 1], (rest, size))
-                many = rest // TILE
-                tail = tail - coef * jnp.concatenate([row] * many, axis=0)
-                itail = itail - coef * jnp.concatenate([irow] * many, axis=0)
+            over.append(1.0 / block[k][k])
+            for i in range(k + 1, TILE):
+                coef[i, k] = block[i][k] * over[k]
+                for c in range(k + 1, i + 1):
+                    block[i][c] = block[i][c] - (block[i][k] * block[c][k]) * over[k]
+                rows[i] = rows[i] - coef[i, k] * rows[k]
+                irows[i] = irows[i] - coef[i, k] * irows[k]
+        top, inverse, pivots = rows[0], irows[0], block[0][0]
+        for k in range(1, TILE):
+            top = jnp.where(sub == k, rows[k], top)
+            inverse = jnp.where(sub == k, irows[k], inverse)
+            pivots = jnp.where(sub == k, block[k][k], pivots)
         root = lax.rsqrt(pivots)
-        tops.append(jnp.where(lane >= sub + j * TILE, head * root, 0.0))
-        inverses.append(ihead * root)
-        left, right = tail, itail
+        tops.append(jnp.where(lane >= sub + j * TILE, top * root, 0.0))
+        inverses.append(inverse * root)
+        if rest:
+            solved = [rows[k] * over[k] for k in range(TILE)]
+            isolved = [irows[k] * over[k] for k in range(TILE)]
+            for k in reversed(range(TILE)):
+                for i in range(k):
+                    solved[i] = solved[i] - coef[k, i] * solved[k]
+                    isolved[i] = isolved[i] - coef[k, i] * isolved[k]
+            left, right = left[TILE:], right[TILE:]
+            for k in range(TILE):
+                left = left - tails[k] * jnp.concatenate([solved[k]] * many, axis=0)
+                right = right - tails[k] * jnp.concatenate([isolved[k]] * many, axis=0)
     return jnp.concatenate(tops, axis=0), jnp.concatenate(inverses, axis=0)
 
 
@@ -259,68 +293,107 @@
     rest = rest + low
     rest = rest - ((first[:, 3 * size :] + fourth) + (second[:, 2 * size :] + third[:, size:]))
     inv = inv_t.T
-    error = exact(exact(inv_t, rest), inv)
+    slip = jnp.where(rows <= cols, exact(upper, inv) - (rows == cols).astype(F32), 0.0)
     weight = jnp.where(rows < cols, 1.0, jnp.where(rows == cols, 0.5, 0.0))
-    shift = error * weight
+    error = exact(exact(inv_t, rest), inv) + rough(slip, slip, ((0,), (0,)))
+    shift = error * weight + slip
     for _ in range(2):
-        shift = (error - rough(shift, shift, ((0,), (0,)))) * weight
+        shift = (error - rough(shift, shift, ((0,), (0,)))) * weight + slip
     square = rough(shift, shift)
     minus = square - shift
     minus = minus + rough(square, minus)
     inv = inv + exact(inv, minus)
-    upper = upper + exact(shift, upper)
+    upper = upper + exact(shift - slip - rough(shift, slip), upper)
     return upper * (1.0 / across), inv * down
 
 
-def basis_kernel(runs, run_rows, cap, peers, scale, me_ref, mine_ref, other_ref, x_ref, mat_ref, out_ref, r_ref, inv_ref):
-    step = pl.program_id(0)
-
-    @pl.when(step == 0)
-    def _():
-        core = lax.rem(me_ref[0], 2)
-        parts = []
-        for i in range(2):
-            mine, other = mine_ref[i], other_ref[i]
-            top = jnp.where(core == 0, mine, other)
-            low = jnp.where(core == 0, other, mine)
-            parts.append(jnp.concatenate([top, low], axis=0))
-        upper, inv = triangular(parts[0], parts[1])
-        r_ref[...] = upper * (1.0 / scale)
-        inv_ref[...] = inv * scale
-
-    for sub in range(runs):
-        peer = lax.rem(me_ref[0] + step * runs + sub, peers)
-        at = pl.ds(pl.multiple_of(peer * cap, cap), cap)
-        y = exact(x_ref[at, :], inv_ref[...])
-        high = y.astype(BF16)
-        low = (y - high.astype(F32)).astype(BF16)
-        both = jnp.concatenate([high, low], axis=1)
-        both = jnp.concatenate([both, both], axis=0)
-        rows = slice(sub * run_rows, (sub + 1) * run_rows)
-        twice = jnp.dot(mat_ref[rows, :], both, preferred_element_type=F32)
-        snaps = y.shape[1]
-        out_ref[rows, :] = twice[:, :snaps] + twice[:, snaps:]
+def thirds(value):
+    high = value.astype(BF16)
+    rest = value - high.astype(F32)
+    middle = rest.astype(BF16)
+    return high, middle, (rest - middle.astype(F32)).astype(BF16)
+
+
+CHUNKS = 16
+
+
+def basis_kernel(
+    cap, peers, scale, me_ref, mine_ref, other_ref, x_ref, mat_hbm, out_hbm, r_ref, y_ref, mat_ref, out_ref, sems, in_sem
+):
+    slots, snaps = x_ref.shape
+    fetch = pltpu.make_async_copy(mat_hbm, mat_ref, in_sem)
+    fetch.start()
+    core = lax.rem(me_ref[0], 2)
+    parts = []
+    for i in range(2):
+        mine, other = mine_ref[i], other_ref[i]
+        top = jnp.where(core == 0, mine, other)
+        low = jnp.where(core == 0, other, mine)
+        parts.append(jnp.concatenate([top, low], axis=0))
+    upper, inv = triangular(parts[0], parts[1])
+    r_ref[...] = upper * (1.0 / scale)
+    high, middle, low = thirds(inv * scale)
+    wide = jnp.concatenate([high, middle], axis=1)
+    wide = jnp.concatenate([wide, wide], axis=0)
+    tall = jnp.concatenate([low, high], axis=0)
+    chunk = 512
+
+    def one_chunk(i, carry):
+        at = pl.ds(pl.multiple_of(i * chunk, chunk), chunk)
+        high, middle, low = thirds(x_ref[at, :])
+        first = jnp.dot(jnp.concatenate([high, middle], axis=1), wide, preferred_element_type=F32)
+        second = jnp.dot(jnp.concatenate([high, low], axis=1), tall, preferred_element_type=F32)
+        y = first[:, :snaps] + (first[:, snaps:] + second)
+        y_high = y.astype(BF16)
+        y_ref[at, :snaps] = y_high
+        y_ref[at, snaps:] = (y - y_high.astype(F32)).astype(BF16)
+        return carry
+
+    lax.fori_loop(0, slots // chunk, one_chunk, 0)
+    fetch.wait()
+    rows = mat_ref.shape[0]
+    block = rows // CHUNKS
+    run_rows = rows // peers
+    runs = block // run_rows
+
+    def send(i):
+        at = pl.ds(pl.multiple_of(i * block, block), block)
+        return pltpu.make_async_copy(out_ref.at[at, :], out_hbm.at[at, :], sems.at[i])
+
+    def one_block(i, carry):
+        for sub in range(runs):
+            run = i * runs + sub
+            peer = lax.rem(me_ref[0] + run, peers)
+            both = y_ref[pl.ds(pl.multiple_of(peer * cap, cap), cap), :]
+            both = jnp.concatenate([both, both], axis=0)
+            at = pl.ds(pl.multiple_of(run * run_rows, run_rows), run_rows)
+            twice = jnp.dot(mat_ref[at, :], both, preferred_element_type=F32)
+            out_ref[at, :] = twice[:, :snaps] + twice[:, snaps:]
+        send(i).start()
+        return carry
+
+    lax.fori_loop(0, CHUNKS, one_block, 0)
+
+    def one_wait(i, carry):
+        send(i).wait()
+        return carry
+
+    lax.fori_loop(0, CHUNKS, one_wait, 0)
 
 
 def make_basis(me, mine, other, x, mat, peers, cap, total_rows):
     rows = mat.shape[0]
-    snaps = x.shape[1]
-    run_rows = rows // peers
-    runs = max(1, 1024 // run_rows)
-    block = runs * run_rows
-    whole = lambda *dims: pl.BlockSpec(dims, lambda i, m: (0,) * len(dims))
-    grid_spec = pltpu.PrefetchScalarGridSpec(
-        num_scalar_prefetch=1,
-        grid=(peers // runs,),
-        in_specs=[whole(*mine.shape), whole(*other.shape), whole(*x.shape), pl.BlockSpec((block, 2 * cap), lambda i, m: (i, 0))],
-        out_specs=[pl.BlockSpec((block, snaps), lambda i, m: (i, 0)), whole(snaps, snaps)],
-        scratch_shapes=[pltpu.VMEM((snaps, snaps), F32)],
-    )
+    slots, snaps = x.shape
+    vmem = pl.BlockSpec(memory_space=pltpu.VMEM)
+    hbm = pl.BlockSpec(memory_space=pltpu.HBM)
+    held = [((slots, 2 * snaps), BF16), (mat.shape, BF16), ((rows, snaps), F32)]
     return pl.pallas_call(
-        functools.partial(basis_kernel, runs, run_rows, cap, peers, math.sqrt(total_rows)),
+        functools.partial(basis_kernel, cap, peers, math.sqrt(total_rows)),
         out_shape=[jax.ShapeDtypeStruct((rows, snaps), F32), jax.ShapeDtypeStruct((snaps, snaps), F32)],
-        grid_spec=grid_spec,
-        compiler_params=pltpu.CompilerParams(vmem_limit_bytes=VMEM_LIMIT),
+        in_specs=[pl.BlockSpec(memory_space=pltpu.SMEM), vmem, vmem, vmem, hbm],
+        out_specs=[hbm, vmem],
+        scratch_shapes=[pltpu.VMEM(*h) for h in held] + [pltpu.SemaphoreType.DMA((CHUNKS,)), pltpu.SemaphoreType.DMA(())],
+        compiler_params=pltpu.CompilerParams(vmem_limit_bytes=MOST_VMEM),
         name="make_basis",
     )(me, mine, other, x, mat)
 

time: 102 us -> 77.5 us (0.76)
  Pallas kernels: 56.7 us -> 32.6 us
    pallas_call x1, Pallas kernels: 36.1 us -> 16.2 us  [make_basis(): pl.pallas_call(functools.partial(basis_kernel, cap, peers, math.sqrt(tota...]
    pallas_call x1, Pallas kernels: 5.92 us -> 2.23 us  [local_gram(): pl.pallas_call(functools.partial(gram_kernel, peers, cap), out_shape=[sha...]
    pallas_call x1, Pallas kernels: 9.74 us -> 8.15 us  [weave(): pl.pallas_call(functools.partial(weave_kernel, runs, run_rows, cap, peers...]
    pallas_call x1, Pallas kernels: 4.95 us -> 6.02 us  [pick_donors(): pl.pallas_call(pick_kernel, out_shape=jax.ShapeDtypeStruct((peers * cap,...]
    unnamed x6 -> x12, local copies, waits for them, and re-layouts: 1.59 us -> 2.57 us
  transfers between devices with their start and end apart: 9 -> 9, of which waited for: 8 -> 8; matrix products, arithmetic and copies ran while one was open for 0% -> 0% of each run, Pallas kernels for 10% -> 11%
where the time goes in v2:
time: 77.5 us; the launch traced here: 77.2 us
  Pallas kernels  32.6 us (42%)
  waiting for transfers between devices  25.7 us (33%)
  starting transfers between devices  15.5 us (20%)
  local copies, waits for them, and re-layouts  2.57 us (3%)
  between operations  0.78 us (1%)
    pallas_call x1, Pallas kernels, make_basis(): pl.pallas_call(functools.partial(basis_kernel, cap, peers, math.sqrt(tota...  16.2 us
    all_to_all x1, waiting for transfers between devices, body(): lax.all_to_all(outgoing, 'rows', split_axis=0, concat_axis=0, tiled=True)  16.1 us
    ppermute x8, waiting for transfers between devices, hop(): return lax.ppermute(value, 'rows', [(i, i ^ mask) for i in range(peers)])  9.61 us
    pallas_call x1, Pallas kernels, weave(): pl.pallas_call(functools.partial(weave_kernel, runs, run_rows, cap, peers...  8.15 us
    ppermute x8, starting transfers between devices, hop(): return lax.ppermute(value, 'rows', [(i, i ^ mask) for i in range(peers)])  8.15 us
    all_to_all x1, starting transfers between devices, body(): lax.all_to_all(outgoing, 'rows', split_axis=0, concat_axis=0, tiled=True)  7.3 us
    pallas_call x1, Pallas kernels, pick_donors(): pl.pallas_call(pick_kernel, out_shape=jax.ShapeDtypeStruct((peers * cap,...  6.02 us
    unnamed x12, local copies, waits for them, and re-layouts  2.57 us
  transfers between devices with their start and end apart: 9, of which 8 were waited for; matrix products, arithmetic and copies ran while one was open for 0% of the time, Pallas kernels for 11%

profile of v2, /device:TPU:0, one launch (start us, length us, event | category | flops | bytes accessed | tf_op | source)
XLA Modules:
  0.0 77.2 jit_solution(2526348259676520802)
XLA Ops:
  0.6 0.0 copy-start.3
  0.6 0.0 copy-start.2
  0.7 6.0 %pick_donors.1 = f32[2048,128]{1,0:T(8,128)} custom-call(s32[32,64]{1,0:T(8,128)} %send_ref.1, f32[8192,128]{1,0:T(8,128)} %snap_ref.1), custom_call_target="tpu_custom_call" | custom-call | tf_op jit(solution)/shard_map/pick_donors/pallas_call | solution.py:61
  6.7 7.3 %all-to-all-start = ((f32[32,64,128]{2,1,0:T(8,128)}), f32[32,64,128]{2,1,0:T(8,128)S(1)}, u32[]{:S(2)}, u32[]{:S(2)}) async-start(f32[32,64,128]{2,1,0:T(8,128)} %bitcast.9), calls=%async_computation | async-start | bytes 2097152 | tf_op jit(solution)/shard_map/all_to_all | solution.py:406
  14.0 0.0 copy-done.3
  14.0 0.0 copy-done.2
  14.0 8.2 %weave.1 = (bf16[16384,128]{1,0:T(8,128)(2,1)S(1)}, f32[2048,64]{1,0:T(8,128)S(1)}) custom-call(s32[1]{0:T(128)} %bitcast.me_ref, s32[8,16384]{1,0:T(8,128)S(1)} %bitcast.7, f32[8,16384]{1,0:T(8,128)S(1)} %bitcast.8), custom_call_target="tpu_custom_call" | custom-call | flops 8000000000 | bytes 40000000 | tf_op jit(solution)/shard_map/weave/pallas_call | solution.py:112
  22.2 0.0 copy-start.1
  22.2 1.9 %copy-done.1 = bf16[16384,128]{1,0:T(8,128)(2,1)} copy-done((bf16[16384,128]{1,0:T(8,128)(2,1)}, bf16[16384,128]{1,0:T(8,128)(2,1)S(1)}, u32[]{:S(2)}) %copy-start.1) | copy-done | bytes 4194328
  24.1 16.1 %all-to-all-done = f32[32,64,128]{2,1,0:T(8,128)S(1)} async-done(((f32[32,64,128]{2,1,0:T(8,128)}), f32[32,64,128]{2,1,0:T(8,128)S(1)}, u32[]{:S(2)}, u32[]{:S(2)}) %all-to-all-start) | async-done | bytes 1048608 | tf_op jit(solution)/shard_map/all_to_all | solution.py:406
  40.2 0.0 copy-start
  40.2 2.2 %local_gram.1 = (f32[2,64,128]{2,1,0:T(8,128)S(1)}, f32[2,64,128]{2,1,0:T(8,128)S(1)}) custom-call(s32[1]{0:T(128)} %bitcast.me_ref, f32[2048,128]{1,0:T(8,128)S(1)} %bitcast.5, f32[2048,64]{1,0:T(8,128)S(1)} %get-tuple-element.6.slot_ref), custom_call_target="tpu_custom_call" | custom-call | tf_op jit(solution)/shard_map/local_gram/pallas_call | solution.py:167
  42.5 0.1 collective-permute-start
  42.5 1.2 %collective-permute-done = f32[2,64,128]{2,1,0:T(8,128)S(1)} collective-permute-done((f32[2,64,128]{2,1,0:T(8,128)S(1)}, f32[2,64,128]{2,1,0:T(8,128)S(1)}, u32[]{:S(2)}, u32[]{:S(2)}) %collective-permute-start) | collective-permute-done | bytes 65568 | tf_op jit(solution)/shard_map/ppermute | solution.py:179
  43.8 2.5 %collective-permute-start.3 = (f32[2,64,128]{2,1,0:T(8,128)S(1)}, f32[2,64,128]{2,1,0:T(8,128)S(1)}, u32[]{:S(2)}, u32[]{:S(2)}) collective-permute-start(f32[2,64,128]{2,1,0:T(8,128)S(1)} %pad_maximum_fusion), channel_id=1, source_target_pairs={{0,6},{1,7},{2,4},{3,5},{4,2},{5,3},{6,0},{7,1},{8,14},{9,15},{10,... | collective-permute-start | bytes 196616 | tf_op jit(solution)/shard_map/ppermute | solution.py:179
  46.3 0.5 collective-permute-start.2
  46.8 0.6 collective-permute-start.1
  47.4 1.7 %collective-permute-done.3 = f32[2,64,128]{2,1,0:T(8,128)S(1)} collective-permute-done((f32[2,64,128]{2,1,0:T(8,128)S(1)}, f32[2,64,128]{2,1,0:T(8,128)S(1)}, u32[]{:S(2)}, u32[]{:S(2)}) %collective-permute-start.3) | collective-permute-done | bytes 65568 | tf_op jit(solution)/shard_map/ppermute | solution.py:179
  49.1 1.5 %collective-permute-done.2 = f32[2,64,128]{2,1,0:T(8,128)S(1)} collective-permute-done((f32[2,64,128]{2,1,0:T(8,128)S(1)}, f32[2,64,128]{2,1,0:T(8,128)S(1)}, u32[]{:S(2)}, u32[]{:S(2)}) %collective-permute-start.2) | collective-permute-done | bytes 65568 | tf_op jit(solution)/shard_map/ppermute | solution.py:179
  50.5 0.5 collective-permute-done.1
  51.2 1.5 %collective-permute-start.6 = (f32[2,64,128]{2,1,0:T(8,128)S(1)}, f32[2,64,128]{2,1,0:T(8,128)S(1)}, u32[]{:S(2)}, u32[]{:S(2)}) collective-permute-start(f32[2,64,128]{2,1,0:T(8,128)S(1)} %pad_maximum_fusion.1), channel_id=1, source_target_pairs={{0,24},{1,25},{2,26},{3,27},{4,28},{5,29},{6,30},{7,31},{8,16},{9,... | collective-permute-start | bytes 196616 | tf_op jit(solution)/shard_map/ppermute | solution.py:179
  52.7 0.6 collective-permute-start.5
  53.3 2.3 %collective-permute-start.4 = (f32[2,64,128]{2,1,0:T(8,128)S(1)}, f32[2,64,128]{2,1,0:T(8,128)S(1)}, u32[]{:S(2)}, u32[]{:S(2)}) collective-permute-start(f32[2,64,128]{2,1,0:T(8,128)S(1)} %pad_maximum_fusion.1), channel_id=1, source_target_pairs={{0,8},{1,9},{2,10},{3,11},{4,12},{5,13},{6,14},{7,15},{8,0},{9,1},... | collective-permute-start | bytes 196616 | tf_op jit(solution)/shard_map/ppermute | solution.py:179
  55.6 1.8 %collective-permute-done.6 = f32[2,64,128]{2,1,0:T(8,128)S(1)} collective-permute-done((f32[2,64,128]{2,1,0:T(8,128)S(1)}, f32[2,64,128]{2,1,0:T(8,128)S(1)}, u32[]{:S(2)}, u32[]{:S(2)}) %collective-permute-start.6) | collective-permute-done | bytes 65568 | tf_op jit(solution)/shard_map/ppermute | solution.py:179
  57.4 1.6 %collective-permute-done.5 = f32[2,64,128]{2,1,0:T(8,128)S(1)} collective-permute-done((f32[2,64,128]{2,1,0:T(8,128)S(1)}, f32[2,64,128]{2,1,0:T(8,128)S(1)}, u32[]{:S(2)}, u32[]{:S(2)}) %collective-permute-start.5) | collective-permute-done | bytes 65568 | tf_op jit(solution)/shard_map/ppermute | solution.py:179
  59.0 0.0 collective-permute-done.4
  59.1 0.0 copy-start.4
  59.1 0.1 collective-permute-start.7
  59.2 1.2 %collective-permute-done.7.other_ref = f32[2,64,128]{2,1,0:T(8,128)S(1)} collective-permute-done((f32[2,64,128]{2,1,0:T(8,128)S(1)}, f32[2,64,128]{2,1,0:T(8,128)S(1)}, u32[]{:S(2)}, u32[]{:S(2)}) %collective-permute-start.7) | collective-permute-done | bytes 65568 | tf_op jit(solution)/shard_map/ppermute | solution.py:179
  60.4 0.0 copy-start.5
  60.4 0.0 copy-done
  60.5 0.0 copy-done.4
  60.5 0.6 copy-done.5
  61.1 16.2 %make_basis.1 = (f32[16384,128]{1,0:T(8,128)}, f32[128,128]{1,0:T(8,128)}) custom-call(s32[1]{0:T(128)} %bitcast.me_ref, f32[2,64,128]{2,1,0:T(8,128)} %copy-done.4, f32[2,64,128]{2,1,0:T(8,128)} %copy-done.5, f32[2048,128]{1,0:T(8,128)} %bitcast.6, bf16[16384,128]{1,0:T(8,128)(2,1)} %copy-done.1), custom_call_target="tpu_custom_call" | custom-call | tf_op jit(solution)/shard_map/make_basis/pallas_call | solution.py:390
  (8 shorter events, 0.1 us)
Async XLA Ops:
  0.6 13.4 %copy-start.3 = (f32[16384,8]{0,1:T(8,128)S(1)}, f32[16384,8]{0,1:T(8,128)}, u32[]{:S(2)}) copy-start(f32[16384,8]{0,1:T(8,128)} %param.7) | copy-start | bytes 1572868
  0.6 13.4 %copy-start.2 = (s32[16384,8]{0,1:T(8,128)S(1)}, s32[16384,8]{0,1:T(8,128)}, u32[]{:S(2)}) copy-start(s32[16384,8]{0,1:T(8,128)} %param.6) | copy-start | bytes 1572868
  6.7 33.5 %all-to-all-start = ((f32[32,64,128]{2,1,0:T(8,128)}), f32[32,64,128]{2,1,0:T(8,128)S(1)}, u32[]{:S(2)}, u32[]{:S(2)}) async-start(f32[32,64,128]{2,1,0:T(8,128)} %bitcast.9), calls=%async_computation | async-start | bytes 2097152 | tf_op jit(solution)/shard_map/all_to_all | solution.py:406
  22.2 1.9 %copy-start.1 = (bf16[16384,128]{1,0:T(8,128)(2,1)}, bf16[16384,128]{1,0:T(8,128)(2,1)S(1)}, u32[]{:S(2)}) copy-start(bf16[16384,128]{1,0:T(8,128)(2,1)S(1)} %get-tuple-element.9.mat_hbm) | copy-start | bytes 12582916
  40.2 20.2 %copy-start = (f32[32,64,128]{2,1,0:T(8,128)}, f32[32,64,128]{2,1,0:T(8,128)S(1)}, u32[]{:S(2)}) copy-start(f32[32,64,128]{2,1,0:T(8,128)S(1)} %all-to-all-done) | copy-start | bytes 3145732
  42.5 1.3 %collective-permute-start = (f32[2,64,128]{2,1,0:T(8,128)S(1)}, f32[2,64,128]{2,1,0:T(8,128)S(1)}, u32[]{:S(2)}, u32[]{:S(2)}) collective-permute-start(f32[2,64,128]{2,1,0:T(8,128)S(1)} %get-tuple-element.8), channel_id=1, source_target_pairs={{0,1},{1,0},{2,3},{3,2},{4,5},{5,4},{6,7},{7,6},{8,9},{9,8},{10,11... | collective-permute-start | bytes 196616 | tf_op jit(solution)/shard_map/ppermute | solution.py:179
  43.8 5.3 %collective-permute-start.3 = (f32[2,64,128]{2,1,0:T(8,128)S(1)}, f32[2,64,128]{2,1,0:T(8,128)S(1)}, u32[]{:S(2)}, u32[]{:S(2)}) collective-permute-start(f32[2,64,128]{2,1,0:T(8,128)S(1)} %pad_maximum_fusion), channel_id=1, source_target_pairs={{0,6},{1,7},{2,4},{3,5},{4,2},{5,3},{6,0},{7,1},{8,14},{9,15},{10,... | collective-permute-start | bytes 196616 | tf_op jit(solution)/shard_map/ppermute | solution.py:179
  46.3 4.3 %collective-permute-start.2 = (f32[2,64,128]{2,1,0:T(8,128)S(1)}, f32[2,64,128]{2,1,0:T(8,128)S(1)}, u32[]{:S(2)}, u32[]{:S(2)}) collective-permute-start(f32[2,64,128]{2,1,0:T(8,128)S(1)} %pad_maximum_fusion), channel_id=1, source_target_pairs={{0,4},{1,5},{2,6},{3,7},{4,0},{5,1},{6,2},{7,3},{8,12},{9,13},{10,... | collective-permute-start | bytes 196616 | tf_op jit(solution)/shard_map/ppermute | solution.py:179
  46.8 4.3 %collective-permute-start.1 = (f32[2,64,128]{2,1,0:T(8,128)S(1)}, f32[2,64,128]{2,1,0:T(8,128)S(1)}, u32[]{:S(2)}, u32[]{:S(2)}) collective-permute-start(f32[2,64,128]{2,1,0:T(8,128)S(1)} %pad_maximum_fusion), channel_id=1, source_target_pairs={{0,2},{1,3},{2,0},{3,1},{4,6},{5,7},{6,4},{7,5},{8,10},{9,11},{10,... | collective-permute-start | bytes 196616 | tf_op jit(solution)/shard_map/ppermute | solution.py:179
  51.2 6.3 %collective-permute-start.6 = (f32[2,64,128]{2,1,0:T(8,128)S(1)}, f32[2,64,128]{2,1,0:T(8,128)S(1)}, u32[]{:S(2)}, u32[]{:S(2)}) collective-permute-start(f32[2,64,128]{2,1,0:T(8,128)S(1)} %pad_maximum_fusion.1), channel_id=1, source_target_pairs={{0,24},{1,25},{2,26},{3,27},{4,28},{5,29},{6,30},{7,31},{8,16},{9,... | collective-permute-start | bytes 196616 | tf_op jit(solution)/shard_map/ppermute | solution.py:179
  52.7 6.4 %collective-permute-start.5 = (f32[2,64,128]{2,1,0:T(8,128)S(1)}, f32[2,64,128]{2,1,0:T(8,128)S(1)}, u32[]{:S(2)}, u32[]{:S(2)}) collective-permute-start(f32[2,64,128]{2,1,0:T(8,128)S(1)} %pad_maximum_fusion.1), channel_id=1, source_target_pairs={{0,16},{1,17},{2,18},{3,19},{4,20},{5,21},{6,22},{7,23},{8,24},{9,... | collective-permute-start | bytes 196616 | tf_op jit(solution)/shard_map/ppermute | solution.py:179
  53.3 5.8 %collective-permute-start.4 = (f32[2,64,128]{2,1,0:T(8,128)S(1)}, f32[2,64,128]{2,1,0:T(8,128)S(1)}, u32[]{:S(2)}, u32[]{:S(2)}) collective-permute-start(f32[2,64,128]{2,1,0:T(8,128)S(1)} %pad_maximum_fusion.1), channel_id=1, source_target_pairs={{0,8},{1,9},{2,10},{3,11},{4,12},{5,13},{6,14},{7,15},{8,0},{9,1},... | collective-permute-start | bytes 196616 | tf_op jit(solution)/shard_map/ppermute | solution.py:179
  59.1 1.3 %copy-start.4 = (f32[2,64,128]{2,1,0:T(8,128)}, f32[2,64,128]{2,1,0:T(8,128)S(1)}, u32[]{:S(2)}) copy-start(f32[2,64,128]{2,1,0:T(8,128)S(1)} %pad_maximum_fusion.2.mine_ref) | copy-start | bytes 196612
  59.1 1.3 %collective-permute-start.7 = (f32[2,64,128]{2,1,0:T(8,128)S(1)}, f32[2,64,128]{2,1,0:T(8,128)S(1)}, u32[]{:S(2)}, u32[]{:S(2)}) collective-permute-start(f32[2,64,128]{2,1,0:T(8,128)S(1)} %pad_maximum_fusion.2.mine_ref), channel_id=1, source_target_pairs={{0,1},{1,0},{2,3},{3,2},{4,5},{5,4},{6,7},{7,6},{8,9},{9,8},{10,11... | collective-permute-start | bytes 196616 | tf_op jit(solution)/shard_map/ppermute | solution.py:179
  60.4 0.6 copy-start.5

commit v3 on v2

--- a/solution.py
+++ b/solution.py
@@ -22,7 +22,9 @@
 
 
 PIECES = 8
-MOST_VMEM = 60 * 1024 * 1024
+GROUPS = 4
+MOST_VMEM = 58 * 1024 * 1024
+BASIS_VMEM = 50 * 1024 * 1024
 
 
 def limit(*arrays):
@@ -33,17 +35,21 @@
     return total + 8 * 1024 * 1024
 
 
-def pick_kernel(send_ref, snap_ref, out_ref, held_ref, sems):
-    peers, cap = send_ref.shape
-    part = snap_ref.shape[0] // PIECES
+def pick_kernel(send_hbm, snap_hbm, out_hbm, held_ref, out_ref, send_ref, sems, out_sems, list_sem):
+    peers, cap = send_hbm.shape
+    part = snap_hbm.shape[0] // PIECES
+    listed = pltpu.make_async_copy(send_hbm, send_ref, list_sem)
+    listed.start()
     copies = []
     for i in range(PIECES):
         at = pl.ds(i * part, part)
-        copy = pltpu.make_async_copy(snap_ref.at[at, :], held_ref.at[at, :], sems.at[i])
+        copy = pltpu.make_async_copy(snap_hbm.at[at, :], held_ref.at[at, :], sems.at[i])
         copy.start()
         copies.append(copy)
+    listed.wait()
     for copy in copies:
         copy.wait()
+    group = peers // GROUPS
 
     def one_peer(peer, carry):
         base = peer * cap
@@ -52,18 +58,35 @@
             out_ref[pl.ds(base + slot, 1), :] = held_ref[pl.ds(node, 1), :]
         return carry
 
-    lax.fori_loop(0, peers, one_peer, 0)
+    leaving = []
+    for i in range(GROUPS):
+        lax.fori_loop(i * group, (i + 1) * group, one_peer, 0, unroll=2)
+        at = pl.ds(i * group * cap, group * cap)
+        copy = pltpu.make_async_copy(out_ref.at[at, :], out_hbm.at[at, :], out_sems.at[i])
+        copy.start()
+        leaving.append(copy)
+    for copy in leaving:
+        copy.wait()
 
 
 def pick_donors(snapshots, send_list):
     peers, cap = send_list.shape
     snaps = snapshots.shape[1]
+    hbm = pl.BlockSpec(memory_space=pltpu.HBM)
+    dma = pltpu.SemaphoreType.DMA
     return pl.pallas_call(
         pick_kernel,
         out_shape=jax.ShapeDtypeStruct((peers * cap, snaps), F32),
-        in_specs=[pl.BlockSpec(memory_space=pltpu.SMEM), pl.BlockSpec(memory_space=pltpu.HBM)],
-        out_specs=pl.BlockSpec(memory_space=pltpu.VMEM),
-        scratch_shapes=[pltpu.VMEM(snapshots.shape, F32), pltpu.SemaphoreType.DMA((PIECES,))],
+        in_specs=[hbm, hbm],
+        out_specs=hbm,
+        scratch_shapes=[
+            pltpu.VMEM(snapshots.shape, F32),
+            pltpu.VMEM((peers * cap, snaps), F32),
+            pltpu.SMEM(send_list.shape, jnp.int32),
+            dma((PIECES,)),
+            dma((GROUPS,)),
+            dma(()),
+        ],
         compiler_params=pltpu.CompilerParams(vmem_limit_bytes=MOST_VMEM),
         name="pick_donors",
     )(send_list, snapshots)
@@ -132,6 +155,24 @@
     return high, low - (high - s)
 
 
+def pack(full):
+    size = full.shape[0]
+    half, low = size // 2, 3 * size // 4
+    lane = lax.broadcasted_iota(jnp.int32, (size // 4, size), 1)
+    fold = jnp.where(lane < half, pltpu.roll(full[low:], half, 1), full[half:low])
+    return jnp.concatenate([full[:half], fold], axis=0)
+
+
+def unpack(packed):
+    size = packed.shape[1]
+    half = size // 2
+    top, fold = packed[:half], packed[half:]
+    lane = lax.broadcasted_iota(jnp.int32, (half, size), 1)
+    corner = jnp.concatenate([fold, pltpu.roll(fold, half, 1)], axis=0)
+    mirror = jnp.concatenate([top, top], axis=0).T[half:]
+    return jnp.concatenate([top, jnp.where(lane < half, mirror, corner)], axis=0)
+
+
 def gram_kernel(peers, cap, me_ref, x_ref, slot_ref, keep_ref, give_ref, z_ref):
     snaps = x_ref.shape[1]
 
@@ -153,16 +194,16 @@
 
     zero = jnp.zeros((snaps, snaps), F32)
     high, low = lax.fori_loop(0, peers * cap // chunk, one_chunk, (zero, zero), unroll=8)
-    half = snaps // 2
     core = lax.rem(me_ref[0], 2)
-    for ref, want in ((keep_ref, 0), (give_ref, 1)):
-        for i, part in enumerate((high, low)):
-            ref[i] = jnp.where(core == want, part[:half], part[half:])
+    half = keep_ref.shape[1]
+    for i, part in enumerate((pack(high), pack(low))):
+        keep_ref[i] = jnp.where(core == 0, part[:half], part[half:])
+        give_ref[i] = jnp.where(core == 0, part[half:], part[:half])
 
 
 def local_gram(me, x, slots, peers, cap):
     snaps = x.shape[1]
-    shape = jax.ShapeDtypeStruct((2, snaps // 2, snaps), F32)
+    shape = jax.ShapeDtypeStruct((2, 3 * snaps // 8, snaps), F32)
     vmem = pl.BlockSpec(memory_space=pltpu.VMEM)
     return pl.pallas_call(
         functools.partial(gram_kernel, peers, cap),
@@ -218,7 +259,6 @@
     sub = lax.broadcasted_iota(jnp.int32, tile, 0)
     lane = lax.broadcasted_iota(jnp.int32, tile, 1)
     left = gram
-    right = (lax.broadcasted_iota(jnp.int32, (size, size), 0) == lax.broadcasted_iota(jnp.int32, (size, size), 1)).astype(F32)
     tops, inverses = [], []
     for j in range(size // TILE):
         rest = left.shape[0] - TILE
@@ -228,16 +268,37 @@
         tails = [jnp.broadcast_to(column[TILE:], (rest, size)) for column in columns] if rest else []
         block = [[jnp.broadcast_to(heads[k][i : i + 1, :], tile) for k in range(i + 1)] for i in range(TILE)]
         rows = [jnp.broadcast_to(left[k : k + 1, :], tile) for k in range(TILE)]
-        irows = [jnp.broadcast_to(right[k : k + 1, :], tile) for k in range(TILE)]
+        irows = [jnp.where(lane < j * TILE, rows[k], (lane == j * TILE + k).astype(F32)) for k in range(TILE)]
         over, coef = [], {}
-        for k in range(TILE):
-            over.append(1.0 / block[k][k])
-            for i in range(k + 1, TILE):
-                coef[i, k] = block[i][k] * over[k]
-                for c in range(k + 1, i + 1):
-                    block[i][c] = block[i][c] - (block[i][k] * block[c][k]) * over[k]
-                rows[i] = rows[i] - coef[i, k] * rows[k]
-                irows[i] = irows[i] - coef[i, k] * irows[k]
+        if rest:
+            ahead = [tail[:TILE] for tail in tails]
+            kept = (lane < j * TILE) | (lane >= (j + 1) * TILE)
+            near = jnp.where(kept, left[TILE : 2 * TILE], 0.0)
+            solved = []
+        for k in range(0, TILE, 2):
+            n = k + 1
+            first, cross = block[k][k], block[n][k]
+            det = first * block[n][n] - cross * cross
+            over_first, over_det = 1.0 / first, 1.0 / det
+            over += [over_first, first * over_det]
+            block[n][n] = det * over_first
+            both = over_first * over_det
+            coef[n, k] = cross * over_first
+            moved = {i: block[i][n] * first - block[i][k] * cross for i in range(n + 1, TILE)}
+            for i in range(n + 1, TILE):
+                for c in range(n + 1, i + 1):
+                    block[i][c] = (block[i][c] - (block[i][k] * block[c][k]) * over_first) - (moved[i] * moved[c]) * both
+            for i in range(n + 1, TILE):
+                coef[i, k] = block[i][k] * over_first
+                coef[i, n] = moved[i] * over_det
+            for many_rows in (rows, irows, ahead) if rest else (rows, irows):
+                many_rows[n] = many_rows[n] - coef[n, k] * many_rows[k]
+                for i in range(n + 1, TILE):
+                    many_rows[i] = many_rows[i] - (coef[i, k] * many_rows[k] + coef[i, n] * many_rows[n])
+            if rest:
+                for c in (k, n):
+                    solved.append(jnp.where(lane < (j + 1) * TILE, irows[c], rows[c]) * over[c])
+                    near = near - ahead[c] * solved[c]
         top, inverse, pivots = rows[0], irows[0], block[0][0]
         for k in range(1, TILE):
             top = jnp.where(sub == k, rows[k], top)
@@ -246,17 +307,17 @@
         root = lax.rsqrt(pivots)
         tops.append(jnp.where(lane >= sub + j * TILE, top * root, 0.0))
         inverses.append(inverse * root)
-        if rest:
-            solved = [rows[k] * over[k] for k in range(TILE)]
-            isolved = [irows[k] * over[k] for k in range(TILE)]
+        if many == 1:
+            left = near
+        elif rest:
             for k in reversed(range(TILE)):
                 for i in range(k):
                     solved[i] = solved[i] - coef[k, i] * solved[k]
-                    isolved[i] = isolved[i] - coef[k, i] * isolved[k]
-            left, right = left[TILE:], right[TILE:]
+            more = many - 1
+            left = jnp.where(jnp.concatenate([kept] * more, axis=0), left[2 * TILE :], 0.0)
             for k in range(TILE):
-                left = left - tails[k] * jnp.concatenate([solved[k]] * many, axis=0)
-                right = right - tails[k] * jnp.concatenate([isolved[k]] * many, axis=0)
+                left = left - tails[k][TILE:] * jnp.concatenate([solved[k]] * more, axis=0)
+            left = jnp.concatenate([near, left], axis=0)
     return jnp.concatenate(tops, axis=0), jnp.concatenate(inverses, axis=0)
 
 
@@ -297,9 +358,9 @@
     weight = jnp.where(rows < cols, 1.0, jnp.where(rows == cols, 0.5, 0.0))
     error = exact(exact(inv_t, rest), inv) + rough(slip, slip, ((0,), (0,)))
     shift = error * weight + slip
-    for _ in range(2):
-        shift = (error - rough(shift, shift, ((0,), (0,)))) * weight + slip
+    shift = (error - rough(shift, shift, ((0,), (0,)))) * weight + slip
     square = rough(shift, shift)
+    shift = (error - rough(shift, shift, ((0,), (0,)))) * weight + slip
     minus = square - shift
     minus = minus + rough(square, minus)
     inv = inv + exact(inv, minus)
@@ -314,7 +375,7 @@
     return high, middle, (rest - middle.astype(F32)).astype(BF16)
 
 
-CHUNKS = 16
+CHUNKS = 8
 
 
 def basis_kernel(
@@ -329,7 +390,7 @@
         mine, other = mine_ref[i], other_ref[i]
         top = jnp.where(core == 0, mine, other)
         low = jnp.where(core == 0, other, mine)
-        parts.append(jnp.concatenate([top, low], axis=0))
+        parts.append(unpack(jnp.concatenate([top, low], axis=0)))
     upper, inv = triangular(parts[0], parts[1])
     r_ref[...] = upper * (1.0 / scale)
     high, middle, low = thirds(inv * scale)
@@ -372,13 +433,13 @@
         send(i).start()
         return carry
 
-    lax.fori_loop(0, CHUNKS, one_block, 0)
+    lax.fori_loop(0, CHUNKS, one_block, 0, unroll=True)
 
     def one_wait(i, carry):
         send(i).wait()
         return carry
 
-    lax.fori_loop(0, CHUNKS, one_wait, 0)
+    lax.fori_loop(0, CHUNKS, one_wait, 0, unroll=True)
 
 
 def make_basis(me, mine, other, x, mat, peers, cap, total_rows):
@@ -393,7 +454,7 @@
         in_specs=[pl.BlockSpec(memory_space=pltpu.SMEM), vmem, vmem, vmem, hbm],
         out_specs=[hbm, vmem],
         scratch_shapes=[pltpu.VMEM(*h) for h in held] + [pltpu.SemaphoreType.DMA((CHUNKS,)), pltpu.SemaphoreType.DMA(())],
-        compiler_params=pltpu.CompilerParams(vmem_limit_bytes=MOST_VMEM),
+        compiler_params=pltpu.CompilerParams(vmem_limit_bytes=BASIS_VMEM),
         name="make_basis",
     )(me, mine, other, x, mat)
 

time: 77.5 us -> 69.9 us (0.902)
  Pallas kernels: 32.6 us -> 26.7 us
  waiting for transfers between devices: 25.7 us -> 24.7 us
    pallas_call x1, Pallas kernels: 16.2 us -> 11.6 us  [make_basis(): pl.pallas_call(functools.partial(basis_kernel, cap, peers, math.sqrt(tota...]
    pallas_call x1, Pallas kernels: 6.02 us -> 4.72 us  [pick_donors(): pl.pallas_call(pick_kernel, out_shape=jax.ShapeDtypeStruct((peers * cap,...]
    ppermute x8, waiting for transfers between devices: 9.61 us -> 8.55 us  [hop(): return lax.ppermute(value, 'rows', [(i, i ^ mask) for i in range(peers)])]
    unnamed x12 -> x6, local copies, waits for them, and re-layouts: 2.57 us -> 1.95 us
  transfers between devices with their start and end apart: 9 -> 9, of which waited for: 8 -> 8; matrix products, arithmetic and copies ran while one was open for 0% -> 0% of each run, Pallas kernels for 11% -> 12%
where the time goes in v3:
time: 69.9 us; the launch traced here: 69.7 us
  Pallas kernels  26.7 us (38%)
  waiting for transfers between devices  24.7 us (35%)
  starting transfers between devices  15.5 us (22%)
  local copies, waits for them, and re-layouts  1.95 us (3%)
  between operations  0.78 us (1%)
    all_to_all x1, waiting for transfers between devices, body(): lax.all_to_all(outgoing, 'rows', split_axis=0, concat_axis=0, tiled=True)  16.1 us
    pallas_call x1, Pallas kernels, make_basis(): pl.pallas_call(functools.partial(basis_kernel, cap, peers, math.sqrt(tota...  11.6 us
    ppermute x8, waiting for transfers between devices, hop(): return lax.ppermute(value, 'rows', [(i, i ^ mask) for i in range(peers)])  8.55 us
    pallas_call x1, Pallas kernels, weave(): pl.pallas_call(functools.partial(weave_kernel, runs, run_rows, cap, peers...  8.15 us
    ppermute x8, starting transfers between devices, hop(): return lax.ppermute(value, 'rows', [(i, i ^ mask) for i in range(peers)])  8.15 us
    all_to_all x1, starting transfers between devices, body(): lax.all_to_all(outgoing, 'rows', split_axis=0, concat_axis=0, tiled=True)  7.3 us
    pallas_call x1, Pallas kernels, pick_donors(): pl.pallas_call(pick_kernel, out_shape=jax.ShapeDtypeStruct((peers * cap,...  4.72 us
    pallas_call x1, Pallas kernels, local_gram(): pl.pallas_call(functools.partial(gram_kernel, peers, cap), out_shape=[sha...  2.29 us
  transfers between devices with their start and end apart: 9, of which 8 were waited for; matrix products, arithmetic and copies ran while one was open for 0% of the time, Pallas kernels for 12%

profile of v3, /device:TPU:0, one launch (start us, length us, event | category | flops | bytes accessed | tf_op | source)
XLA Modules:
  0.0 69.7 jit_solution(14768729788762555246)
XLA Ops:
  0.6 0.0 copy-start.2
  0.6 0.0 copy-start.1
  0.7 4.7 %pick_donors.1 = f32[2048,128]{1,0:T(8,128)} custom-call(s32[32,64]{1,0:T(8,128)} %send_hbm.1, f32[8192,128]{1,0:T(8,128)} %snap_hbm.1), custom_call_target="tpu_custom_call" | custom-call | tf_op jit(solution)/shard_map/pick_donors/pallas_call | solution.py:77
  5.4 7.3 %all-to-all-start = ((f32[32,64,128]{2,1,0:T(8,128)}), f32[32,64,128]{2,1,0:T(8,128)S(1)}, u32[]{:S(2)}, u32[]{:S(2)}) async-start(f32[32,64,128]{2,1,0:T(8,128)} %bitcast.9), calls=%async_computation | async-start | bytes 2097152 | tf_op jit(solution)/shard_map/all_to_all | solution.py:467
  12.7 0.0 copy-done.2
  12.7 0.0 copy-done.1
  12.7 8.2 %weave.1 = (bf16[16384,128]{1,0:T(8,128)(2,1)S(1)}, f32[2048,64]{1,0:T(8,128)S(1)}) custom-call(s32[1]{0:T(128)} %bitcast.me_ref, s32[8,16384]{1,0:T(8,128)S(1)} %bitcast.7, f32[8,16384]{1,0:T(8,128)S(1)} %bitcast.8), custom_call_target="tpu_custom_call" | custom-call | flops 8000000000 | bytes 40000000 | tf_op jit(solution)/shard_map/weave/pallas_call | solution.py:135
  20.9 0.0 copy-start
  20.9 1.9 %copy-done = bf16[16384,128]{1,0:T(8,128)(2,1)} copy-done((bf16[16384,128]{1,0:T(8,128)(2,1)}, bf16[16384,128]{1,0:T(8,128)(2,1)S(1)}, u32[]{:S(2)}) %copy-start) | copy-done | bytes 4194328
  22.8 16.1 %all-to-all-done = f32[32,64,128]{2,1,0:T(8,128)S(1)} async-done(((f32[32,64,128]{2,1,0:T(8,128)}), f32[32,64,128]{2,1,0:T(8,128)S(1)}, u32[]{:S(2)}, u32[]{:S(2)}) %all-to-all-start) | async-done | bytes 1048608 | tf_op jit(solution)/shard_map/all_to_all | solution.py:467
  38.9 2.3 %local_gram.1 = (f32[2,48,128]{2,1,0:T(8,128)S(1)}, f32[2,48,128]{2,1,0:T(8,128)S(1)}) custom-call(s32[1]{0:T(128)} %bitcast.me_ref, f32[2048,128]{1,0:T(8,128)S(1)} %bitcast.5, f32[2048,64]{1,0:T(8,128)S(1)} %get-tuple-element.6.slot_ref), custom_call_target="tpu_custom_call" | custom-call | tf_op jit(solution)/shard_map/local_gram/pallas_call | solution.py:208
  41.2 0.1 collective-permute-start
  41.3 1.2 %collective-permute-done = f32[2,48,128]{2,1,0:T(8,128)S(1)} collective-permute-done((f32[2,48,128]{2,1,0:T(8,128)S(1)}, f32[2,48,128]{2,1,0:T(8,128)S(1)}, u32[]{:S(2)}, u32[]{:S(2)}) %collective-permute-start) | collective-permute-done | bytes 49184 | tf_op jit(solution)/shard_map/ppermute | solution.py:220
  42.6 2.5 %collective-permute-start.3 = (f32[2,48,128]{2,1,0:T(8,128)S(1)}, f32[2,48,128]{2,1,0:T(8,128)S(1)}, u32[]{:S(2)}, u32[]{:S(2)}) collective-permute-start(f32[2,48,128]{2,1,0:T(8,128)S(1)} %pad_maximum_fusion), channel_id=1, source_target_pairs={{0,6},{1,7},{2,4},{3,5},{4,2},{5,3},{6,0},{7,1},{8,14},{9,15},{10,... | collective-permute-start | bytes 147464 | tf_op jit(solution)/shard_map/ppermute | solution.py:220
  45.0 0.5 collective-permute-start.2
  45.6 0.6 collective-permute-start.1
  46.1 1.5 %collective-permute-done.3 = f32[2,48,128]{2,1,0:T(8,128)S(1)} collective-permute-done((f32[2,48,128]{2,1,0:T(8,128)S(1)}, f32[2,48,128]{2,1,0:T(8,128)S(1)}, u32[]{:S(2)}, u32[]{:S(2)}) %collective-permute-start.3) | collective-permute-done | bytes 49184 | tf_op jit(solution)/shard_map/ppermute | solution.py:220
  47.6 1.5 %collective-permute-done.2 = f32[2,48,128]{2,1,0:T(8,128)S(1)} collective-permute-done((f32[2,48,128]{2,1,0:T(8,128)S(1)}, f32[2,48,128]{2,1,0:T(8,128)S(1)}, u32[]{:S(2)}, u32[]{:S(2)}) %collective-permute-start.2) | collective-permute-done | bytes 49184 | tf_op jit(solution)/shard_map/ppermute | solution.py:220
  49.1 0.5 collective-permute-done.1
  49.7 1.5 %collective-permute-start.6 = (f32[2,48,128]{2,1,0:T(8,128)S(1)}, f32[2,48,128]{2,1,0:T(8,128)S(1)}, u32[]{:S(2)}, u32[]{:S(2)}) collective-permute-start(f32[2,48,128]{2,1,0:T(8,128)S(1)} %pad_maximum_fusion.1), channel_id=1, source_target_pairs={{0,24},{1,25},{2,26},{3,27},{4,28},{5,29},{6,30},{7,31},{8,16},{9,... | collective-permute-start | bytes 147464 | tf_op jit(solution)/shard_map/ppermute | solution.py:220
  51.2 0.6 collective-permute-start.5
  51.9 2.3 %collective-permute-start.4 = (f32[2,48,128]{2,1,0:T(8,128)S(1)}, f32[2,48,128]{2,1,0:T(8,128)S(1)}, u32[]{:S(2)}, u32[]{:S(2)}) collective-permute-start(f32[2,48,128]{2,1,0:T(8,128)S(1)} %pad_maximum_fusion.1), channel_id=1, source_target_pairs={{0,8},{1,9},{2,10},{3,11},{4,12},{5,13},{6,14},{7,15},{8,0},{9,1},... | collective-permute-start | bytes 147464 | tf_op jit(solution)/shard_map/ppermute | solution.py:220
  54.2 1.5 %collective-permute-done.6 = f32[2,48,128]{2,1,0:T(8,128)S(1)} collective-permute-done((f32[2,48,128]{2,1,0:T(8,128)S(1)}, f32[2,48,128]{2,1,0:T(8,128)S(1)}, u32[]{:S(2)}, u32[]{:S(2)}) %collective-permute-start.6) | collective-permute-done | bytes 49184 | tf_op jit(solution)/shard_map/ppermute | solution.py:220
  55.7 1.1 %collective-permute-done.5 = f32[2,48,128]{2,1,0:T(8,128)S(1)} collective-permute-done((f32[2,48,128]{2,1,0:T(8,128)S(1)}, f32[2,48,128]{2,1,0:T(8,128)S(1)}, u32[]{:S(2)}, u32[]{:S(2)}) %collective-permute-start.5) | collective-permute-done | bytes 49184 | tf_op jit(solution)/shard_map/ppermute | solution.py:220
  56.8 0.0 collective-permute-done.4
  56.8 0.1 collective-permute-start.7
  56.9 1.2 %collective-permute-done.7.other_ref = f32[2,48,128]{2,1,0:T(8,128)S(1)} collective-permute-done((f32[2,48,128]{2,1,0:T(8,128)S(1)}, f32[2,48,128]{2,1,0:T(8,128)S(1)}, u32[]{:S(2)}, u32[]{:S(2)}) %collective-permute-start.7) | collective-permute-done | bytes 49184 | tf_op jit(solution)/shard_map/ppermute | solution.py:220
  58.1 11.6 %make_basis.1 = (f32[16384,128]{1,0:T(8,128)}, f32[128,128]{1,0:T(8,128)}) custom-call(s32[1]{0:T(128)} %bitcast.me_ref, f32[2,48,128]{2,1,0:T(8,128)S(1)} %pad_maximum_fusion.2.mine_ref, f32[2,48,128]{2,1,0:T(8,128)S(1)} %collective-permute-done.7.other_ref, f32[2048,128]{1,0:T(8,128)S(1)} %bitcast.6, bf16[16384,128]{1,0:T(8,128)(2,1)} %copy-done), custom_call_target="tpu_custom_call" | custom-call | tf_op jit(solution)/shard_map/make_basis/pallas_call | solution.py:451
  (8 shorter events, 0.1 us)
Async XLA Ops:
  0.6 12.1 %copy-start.2 = (f32[16384,8]{0,1:T(8,128)S(1)}, f32[16384,8]{0,1:T(8,128)}, u32[]{:S(2)}) copy-start(f32[16384,8]{0,1:T(8,128)} %param.7) | copy-start | bytes 1572868
  0.6 12.1 %copy-start.1 = (s32[16384,8]{0,1:T(8,128)S(1)}, s32[16384,8]{0,1:T(8,128)}, u32[]{:S(2)}) copy-start(s32[16384,8]{0,1:T(8,128)} %param.6) | copy-start | bytes 1572868
  5.4 33.5 %all-to-all-start = ((f32[32,64,128]{2,1,0:T(8,128)}), f32[32,64,128]{2,1,0:T(8,128)S(1)}, u32[]{:S(2)}, u32[]{:S(2)}) async-start(f32[32,64,128]{2,1,0:T(8,128)} %bitcast.9), calls=%async_computation | async-start | bytes 2097152 | tf_op jit(solution)/shard_map/all_to_all | solution.py:467
  20.9 2.0 %copy-start = (bf16[16384,128]{1,0:T(8,128)(2,1)}, bf16[16384,128]{1,0:T(8,128)(2,1)S(1)}, u32[]{:S(2)}) copy-start(bf16[16384,128]{1,0:T(8,128)(2,1)S(1)} %get-tuple-element.9.mat_hbm) | copy-start | bytes 12582916
  41.2 1.3 %collective-permute-start = (f32[2,48,128]{2,1,0:T(8,128)S(1)}, f32[2,48,128]{2,1,0:T(8,128)S(1)}, u32[]{:S(2)}, u32[]{:S(2)}) collective-permute-start(f32[2,48,128]{2,1,0:T(8,128)S(1)} %get-tuple-element.8), channel_id=1, source_target_pairs={{0,1},{1,0},{2,3},{3,2},{4,5},{5,4},{6,7},{7,6},{8,9},{9,8},{10,11... | collective-permute-start | bytes 147464 | tf_op jit(solution)/shard_map/ppermute | solution.py:220
  42.6 5.1 %collective-permute-start.3 = (f32[2,48,128]{2,1,0:T(8,128)S(1)}, f32[2,48,128]{2,1,0:T(8,128)S(1)}, u32[]{:S(2)}, u32[]{:S(2)}) collective-permute-start(f32[2,48,128]{2,1,0:T(8,128)S(1)} %pad_maximum_fusion), channel_id=1, source_target_pairs={{0,6},{1,7},{2,4},{3,5},{4,2},{5,3},{6,0},{7,1},{8,14},{9,15},{10,... | collective-permute-start | bytes 147464 | tf_op jit(solution)/shard_map/ppermute | solution.py:220
  45.0 4.1 %collective-permute-start.2 = (f32[2,48,128]{2,1,0:T(8,128)S(1)}, f32[2,48,128]{2,1,0:T(8,128)S(1)}, u32[]{:S(2)}, u32[]{:S(2)}) collective-permute-start(f32[2,48,128]{2,1,0:T(8,128)S(1)} %pad_maximum_fusion), channel_id=1, source_target_pairs={{0,4},{1,5},{2,6},{3,7},{4,0},{5,1},{6,2},{7,3},{8,12},{9,13},{10,... | collective-permute-start | bytes 147464 | tf_op jit(solution)/shard_map/ppermute | solution.py:220
  45.6 4.1 %collective-permute-start.1 = (f32[2,48,128]{2,1,0:T(8,128)S(1)}, f32[2,48,128]{2,1,0:T(8,128)S(1)}, u32[]{:S(2)}, u32[]{:S(2)}) collective-permute-start(f32[2,48,128]{2,1,0:T(8,128)S(1)} %pad_maximum_fusion), channel_id=1, source_target_pairs={{0,2},{1,3},{2,0},{3,1},{4,6},{5,7},{6,4},{7,5},{8,10},{9,11},{10,... | collective-permute-start | bytes 147464 | tf_op jit(solution)/shard_map/ppermute | solution.py:220
  49.7 6.0 %collective-permute-start.6 = (f32[2,48,128]{2,1,0:T(8,128)S(1)}, f32[2,48,128]{2,1,0:T(8,128)S(1)}, u32[]{:S(2)}, u32[]{:S(2)}) collective-permute-start(f32[2,48,128]{2,1,0:T(8,128)S(1)} %pad_maximum_fusion.1), channel_id=1, source_target_pairs={{0,24},{1,25},{2,26},{3,27},{4,28},{5,29},{6,30},{7,31},{8,16},{9,... | collective-permute-start | bytes 147464 | tf_op jit(solution)/shard_map/ppermute | solution.py:220
  51.2 5.5 %collective-permute-start.5 = (f32[2,48,128]{2,1,0:T(8,128)S(1)}, f32[2,48,128]{2,1,0:T(8,128)S(1)}, u32[]{:S(2)}, u32[]{:S(2)}) collective-permute-start(f32[2,48,128]{2,1,0:T(8,128)S(1)} %pad_maximum_fusion.1), channel_id=1, source_target_pairs={{0,16},{1,17},{2,18},{3,19},{4,20},{5,21},{6,22},{7,23},{8,24},{9,... | collective-permute-start | bytes 147464 | tf_op jit(solution)/shard_map/ppermute | solution.py:220
  51.9 4.9 %collective-permute-start.4 = (f32[2,48,128]{2,1,0:T(8,128)S(1)}, f32[2,48,128]{2,1,0:T(8,128)S(1)}, u32[]{:S(2)}, u32[]{:S(2)}) collective-permute-start(f32[2,48,128]{2,1,0:T(8,128)S(1)} %pad_maximum_fusion.1), channel_id=1, source_target_pairs={{0,8},{1,9},{2,10},{3,11},{4,12},{5,13},{6,14},{7,15},{8,0},{9,1},... | collective-permute-start | bytes 147464 | tf_op jit(solution)/shard_map/ppermute | solution.py:220
  56.8 1.3 %collective-permute-start.7 = (f32[2,48,128]{2,1,0:T(8,128)S(1)}, f32[2,48,128]{2,1,0:T(8,128)S(1)}, u32[]{:S(2)}, u32[]{:S(2)}) collective-permute-start(f32[2,48,128]{2,1,0:T(8,128)S(1)} %pad_maximum_fusion.2.mine_ref), channel_id=1, source_target_pairs={{0,1},{1,0},{2,3},{3,2},{4,5},{5,4},{6,7},{7,6},{8,9},{9,8},{10,11... | collective-permute-start | bytes 147464 | tf_op jit(solution)/shard_map/ppermute | solution.py:220

commit v4 on v3

--- a/solution.py
+++ b/solution.py
@@ -258,23 +258,31 @@
     tile = (TILE, size)
     sub = lax.broadcasted_iota(jnp.int32, tile, 0)
     lane = lax.broadcasted_iota(jnp.int32, tile, 1)
-    left = gram
+    panels = size // TILE
+    left = [gram[i * TILE : (i + 1) * TILE] for i in range(panels)]
+
+    def across(value, col):
+        return jnp.broadcast_to(value[:, col : col + 1], tile)
+
+    def down(value, row):
+        return jnp.broadcast_to(value[row : row + 1, :], tile)
+
     tops, inverses = [], []
-    for j in range(size // TILE):
-        rest = left.shape[0] - TILE
-        many = rest // TILE
-        columns = [left[:, j * TILE + k : j * TILE + k + 1] for k in range(TILE)]
-        heads = [jnp.broadcast_to(column[:TILE], tile) for column in columns]
-        tails = [jnp.broadcast_to(column[TILE:], (rest, size)) for column in columns] if rest else []
-        block = [[jnp.broadcast_to(heads[k][i : i + 1, :], tile) for k in range(i + 1)] for i in range(TILE)]
-        rows = [jnp.broadcast_to(left[k : k + 1, :], tile) for k in range(TILE)]
-        irows = [jnp.where(lane < j * TILE, rows[k], (lane == j * TILE + k).astype(F32)) for k in range(TILE)]
-        over, coef = [], {}
-        if rest:
-            ahead = [tail[:TILE] for tail in tails]
-            kept = (lane < j * TILE) | (lane >= (j + 1) * TILE)
-            near = jnp.where(kept, left[TILE : 2 * TILE], 0.0)
-            solved = []
+    heads = [across(left[0], k) for k in range(TILE)]
+    ahead = [across(left[1], k) for k in range(TILE)]
+    for j in range(panels):
+        start, stop = j * TILE, (j + 1) * TILE
+        later = range(j + 1, panels)
+        tails = {i: [across(left[i], start + k) for k in range(TILE)] for i in later if i > j + 1}
+        near_heads = [across(left[j + 1], stop + c) for c in range(TILE)] if j + 1 < panels else []
+        near_ahead = [across(left[j + 2], stop + c) for c in range(TILE)] if j + 2 < panels else []
+        second = list(tails[j + 2]) if j + 2 < panels else []
+        block = [[down(heads[k], i) for k in range(i + 1)] for i in range(TILE)]
+        rows = [down(left[j], k) for k in range(TILE)]
+        irows = [jnp.where(lane < start, rows[k], (lane == start + k).astype(F32)) for k in range(TILE)]
+        kept = (lane < start) | (lane >= stop)
+        groups = [g for g in (ahead, second, rows, irows) if g]
+        over, coef, solved = [], {}, []
         for k in range(0, TILE, 2):
             n = k + 1
             first, cross = block[k][k], block[n][k]
@@ -291,33 +299,44 @@
             for i in range(n + 1, TILE):
                 coef[i, k] = block[i][k] * over_first
                 coef[i, n] = moved[i] * over_det
-            for many_rows in (rows, irows, ahead) if rest else (rows, irows):
-                many_rows[n] = many_rows[n] - coef[n, k] * many_rows[k]
+            for group in groups:
+                group[n] = group[n] - coef[n, k] * group[k]
                 for i in range(n + 1, TILE):
-                    many_rows[i] = many_rows[i] - (coef[i, k] * many_rows[k] + coef[i, n] * many_rows[n])
-            if rest:
-                for c in (k, n):
-                    solved.append(jnp.where(lane < (j + 1) * TILE, irows[c], rows[c]) * over[c])
-                    near = near - ahead[c] * solved[c]
+                    group[i] = group[i] - (coef[i, k] * group[k] + coef[i, n] * group[n])
+            shrunk = {p: ahead[p] * over[p] for p in (k, n)} if near_heads else {}
+            for c in range(TILE):
+                for p in (k, n):
+                    if near_heads:
+                        scaled = down(shrunk[p], c)
+                        near_heads[c] = near_heads[c] - ahead[p] * scaled
+                    if near_ahead:
+                        near_ahead[c] = near_ahead[c] - second[p] * scaled
+            for p in (k, n):
+                solved.append(jnp.where(lane < stop, irows[p], rows[p]) * over[p])
         top, inverse, pivots = rows[0], irows[0], block[0][0]
         for k in range(1, TILE):
             top = jnp.where(sub == k, rows[k], top)
             inverse = jnp.where(sub == k, irows[k], inverse)
             pivots = jnp.where(sub == k, block[k][k], pivots)
         root = lax.rsqrt(pivots)
-        tops.append(jnp.where(lane >= sub + j * TILE, top * root, 0.0))
+        tops.append(jnp.where(lane >= sub + start, top * root, 0.0))
         inverses.append(inverse * root)
-        if many == 1:
-            left = near
-        elif rest:
+        for i, columns in ((j + 1, ahead), (j + 2, second)):
+            if columns:
+                value = jnp.where(kept, left[i], 0.0)
+                for k in range(TILE):
+                    value = value - columns[k] * solved[k]
+                left[i] = value
+        if j + 3 < panels:
             for k in reversed(range(TILE)):
                 for i in range(k):
                     solved[i] = solved[i] - coef[k, i] * solved[k]
-            more = many - 1
-            left = jnp.where(jnp.concatenate([kept] * more, axis=0), left[2 * TILE :], 0.0)
-            for k in range(TILE):
-                left = left - tails[k][TILE:] * jnp.concatenate([solved[k]] * more, axis=0)
-            left = jnp.concatenate([near, left], axis=0)
+            for i in range(j + 3, panels):
+                value = jnp.where(kept, left[i], 0.0)
+                for k in range(TILE):
+                    value = value - tails[i][k] * solved[k]
+                left[i] = value
+        heads, ahead = near_heads, near_ahead
     return jnp.concatenate(tops, axis=0), jnp.concatenate(inverses, axis=0)
 
 
@@ -344,15 +363,17 @@
     up = slices(upper)
     lo = slices(upper.T)
     first = jnp.dot(lo[0], jnp.concatenate(up, axis=1), preferred_element_type=F32)
-    second = jnp.dot(lo[1], jnp.concatenate(up[:3], axis=1), preferred_element_type=F32)
-    third = jnp.dot(lo[2], jnp.concatenate(up[:2], axis=1), preferred_element_type=F32)
-    fourth = jnp.dot(lo[3], up[0], preferred_element_type=F32)
-    rest = high - first[:, :size]
-    rest = rest - (first[:, size : 2 * size] + second[:, :size])
-    rest = rest - second[:, size : 2 * size]
-    rest = rest - (first[:, 2 * size : 3 * size] + third[:, :size])
+    second = jnp.dot(lo[1], jnp.concatenate(up, axis=1), preferred_element_type=F32)
+    third = jnp.dot(lo[2], jnp.concatenate(up[:3], axis=1), preferred_element_type=F32)
+    fourth = jnp.dot(lo[3], jnp.concatenate(up[:2], axis=1), preferred_element_type=F32)
+    part = lambda value, i: value[:, i * size : (i + 1) * size]
+    rest = high - part(first, 0)
+    rest = rest - (part(first, 1) + part(second, 0))
+    rest = rest - part(second, 1)
+    rest = rest - (part(first, 2) + part(third, 0))
     rest = rest + low
-    rest = rest - ((first[:, 3 * size :] + fourth) + (second[:, 2 * size :] + third[:, size:]))
+    rest = rest - ((part(first, 3) + part(fourth, 0)) + (part(second, 2) + part(third, 1)))
+    rest = rest - ((part(second, 3) + part(fourth, 1)) + part(third, 2))
     inv = inv_t.T
     slip = jnp.where(rows <= cols, exact(upper, inv) - (rows == cols).astype(F32), 0.0)
     weight = jnp.where(rows < cols, 1.0, jnp.where(rows == cols, 0.5, 0.0))

time: 69.9 us -> 69.1 us (0.989)
  Pallas kernels: 26.7 us -> 25.9 us
    pallas_call x1, Pallas kernels: 11.6 us -> 10.8 us  [make_basis(): pl.pallas_call(functools.partial(basis_kernel, cap, peers, math.sqrt(tota...]
where the time goes in v4:
time: 69.1 us; the launch traced here: 68.9 us
  Pallas kernels  25.9 us (37%)
  waiting for transfers between devices  24.7 us (36%)
  starting transfers between devices  15.5 us (22%)
  local copies, waits for them, and re-layouts  1.95 us (3%)
  between operations  0.78 us (1%)
    all_to_all x1, waiting for transfers between devices, body(): lax.all_to_all(outgoing, 'rows', split_axis=0, concat_axis=0, tiled=True)  16.1 us
    pallas_call x1, Pallas kernels, make_basis(): pl.pallas_call(functools.partial(basis_kernel, cap, peers, math.sqrt(tota...  10.8 us
    ppermute x8, waiting for transfers between devices, hop(): return lax.ppermute(value, 'rows', [(i, i ^ mask) for i in range(peers)])  8.55 us
    pallas_call x1, Pallas kernels, weave(): pl.pallas_call(functools.partial(weave_kernel, runs, run_rows, cap, peers...  8.15 us
    ppermute x8, starting transfers between devices, hop(): return lax.ppermute(value, 'rows', [(i, i ^ mask) for i in range(peers)])  8.15 us
    all_to_all x1, starting transfers between devices, body(): lax.all_to_all(outgoing, 'rows', split_axis=0, concat_axis=0, tiled=True)  7.3 us
    pallas_call x1, Pallas kernels, pick_donors(): pl.pallas_call(pick_kernel, out_shape=jax.ShapeDtypeStruct((peers * cap,...  4.72 us
    pallas_call x1, Pallas kernels, local_gram(): pl.pallas_call(functools.partial(gram_kernel, peers, cap), out_shape=[sha...  2.29 us
  transfers between devices with their start and end apart: 9, of which 8 were waited for; matrix products, arithmetic and copies ran while one was open for 0% of the time, Pallas kernels for 12%

profile of v4, /device:TPU:0, one launch (start us, length us, event | category | flops | bytes accessed | tf_op | source)
XLA Modules:
  0.0 68.9 jit_solution(4251450409118714386)
XLA Ops:
  0.6 0.0 copy-start.2
  0.6 0.0 copy-start.1
  0.7 4.7 %pick_donors.1 = f32[2048,128]{1,0:T(8,128)} custom-call(s32[32,64]{1,0:T(8,128)} %send_hbm.1, f32[8192,128]{1,0:T(8,128)} %snap_hbm.1), custom_call_target="tpu_custom_call" | custom-call | tf_op jit(solution)/shard_map/pick_donors/pallas_call | solution.py:77
  5.4 7.3 %all-to-all-start = ((f32[32,64,128]{2,1,0:T(8,128)}), f32[32,64,128]{2,1,0:T(8,128)S(1)}, u32[]{:S(2)}, u32[]{:S(2)}) async-start(f32[32,64,128]{2,1,0:T(8,128)} %bitcast.9), calls=%async_computation | async-start | bytes 2097152 | tf_op jit(solution)/shard_map/all_to_all | solution.py:488
  12.7 0.0 copy-done.2
  12.7 0.0 copy-done.1
  12.7 8.2 %weave.1 = (bf16[16384,128]{1,0:T(8,128)(2,1)S(1)}, f32[2048,64]{1,0:T(8,128)S(1)}) custom-call(s32[1]{0:T(128)} %bitcast.me_ref, s32[8,16384]{1,0:T(8,128)S(1)} %bitcast.7, f32[8,16384]{1,0:T(8,128)S(1)} %bitcast.8), custom_call_target="tpu_custom_call" | custom-call | flops 8000000000 | bytes 40000000 | tf_op jit(solution)/shard_map/weave/pallas_call | solution.py:135
  20.9 0.0 copy-start
  20.9 1.9 %copy-done = bf16[16384,128]{1,0:T(8,128)(2,1)} copy-done((bf16[16384,128]{1,0:T(8,128)(2,1)}, bf16[16384,128]{1,0:T(8,128)(2,1)S(1)}, u32[]{:S(2)}) %copy-start) | copy-done | bytes 4194328
  22.8 16.1 %all-to-all-done = f32[32,64,128]{2,1,0:T(8,128)S(1)} async-done(((f32[32,64,128]{2,1,0:T(8,128)}), f32[32,64,128]{2,1,0:T(8,128)S(1)}, u32[]{:S(2)}, u32[]{:S(2)}) %all-to-all-start) | async-done | bytes 1048608 | tf_op jit(solution)/shard_map/all_to_all | solution.py:488
  38.9 2.3 %local_gram.1 = (f32[2,48,128]{2,1,0:T(8,128)S(1)}, f32[2,48,128]{2,1,0:T(8,128)S(1)}) custom-call(s32[1]{0:T(128)} %bitcast.me_ref, f32[2048,128]{1,0:T(8,128)S(1)} %bitcast.5, f32[2048,64]{1,0:T(8,128)S(1)} %get-tuple-element.6.slot_ref), custom_call_target="tpu_custom_call" | custom-call | tf_op jit(solution)/shard_map/local_gram/pallas_call | solution.py:208
  41.2 0.1 collective-permute-start
  41.3 1.2 %collective-permute-done = f32[2,48,128]{2,1,0:T(8,128)S(1)} collective-permute-done((f32[2,48,128]{2,1,0:T(8,128)S(1)}, f32[2,48,128]{2,1,0:T(8,128)S(1)}, u32[]{:S(2)}, u32[]{:S(2)}) %collective-permute-start) | collective-permute-done | bytes 49184 | tf_op jit(solution)/shard_map/ppermute | solution.py:220
  42.6 2.5 %collective-permute-start.3 = (f32[2,48,128]{2,1,0:T(8,128)S(1)}, f32[2,48,128]{2,1,0:T(8,128)S(1)}, u32[]{:S(2)}, u32[]{:S(2)}) collective-permute-start(f32[2,48,128]{2,1,0:T(8,128)S(1)} %pad_maximum_fusion), channel_id=1, source_target_pairs={{0,6},{1,7},{2,4},{3,5},{4,2},{5,3},{6,0},{7,1},{8,14},{9,15},{10,... | collective-permute-start | bytes 147464 | tf_op jit(solution)/shard_map/ppermute | solution.py:220
  45.0 0.5 collective-permute-start.2
  45.6 0.6 collective-permute-start.1
  46.1 1.5 %collective-permute-done.3 = f32[2,48,128]{2,1,0:T(8,128)S(1)} collective-permute-done((f32[2,48,128]{2,1,0:T(8,128)S(1)}, f32[2,48,128]{2,1,0:T(8,128)S(1)}, u32[]{:S(2)}, u32[]{:S(2)}) %collective-permute-start.3) | collective-permute-done | bytes 49184 | tf_op jit(solution)/shard_map/ppermute | solution.py:220
  47.6 1.5 %collective-permute-done.2 = f32[2,48,128]{2,1,0:T(8,128)S(1)} collective-permute-done((f32[2,48,128]{2,1,0:T(8,128)S(1)}, f32[2,48,128]{2,1,0:T(8,128)S(1)}, u32[]{:S(2)}, u32[]{:S(2)}) %collective-permute-start.2) | collective-permute-done | bytes 49184 | tf_op jit(solution)/shard_map/ppermute | solution.py:220
  49.1 0.5 collective-permute-done.1
  49.7 1.5 %collective-permute-start.6 = (f32[2,48,128]{2,1,0:T(8,128)S(1)}, f32[2,48,128]{2,1,0:T(8,128)S(1)}, u32[]{:S(2)}, u32[]{:S(2)}) collective-permute-start(f32[2,48,128]{2,1,0:T(8,128)S(1)} %pad_maximum_fusion.1), channel_id=1, source_target_pairs={{0,24},{1,25},{2,26},{3,27},{4,28},{5,29},{6,30},{7,31},{8,16},{9,... | collective-permute-start | bytes 147464 | tf_op jit(solution)/shard_map/ppermute | solution.py:220
  51.2 0.6 collective-permute-start.5
  51.9 2.3 %collective-permute-start.4 = (f32[2,48,128]{2,1,0:T(8,128)S(1)}, f32[2,48,128]{2,1,0:T(8,128)S(1)}, u32[]{:S(2)}, u32[]{:S(2)}) collective-permute-start(f32[2,48,128]{2,1,0:T(8,128)S(1)} %pad_maximum_fusion.1), channel_id=1, source_target_pairs={{0,8},{1,9},{2,10},{3,11},{4,12},{5,13},{6,14},{7,15},{8,0},{9,1},... | collective-permute-start | bytes 147464 | tf_op jit(solution)/shard_map/ppermute | solution.py:220
  54.2 1.5 %collective-permute-done.6 = f32[2,48,128]{2,1,0:T(8,128)S(1)} collective-permute-done((f32[2,48,128]{2,1,0:T(8,128)S(1)}, f32[2,48,128]{2,1,0:T(8,128)S(1)}, u32[]{:S(2)}, u32[]{:S(2)}) %collective-permute-start.6) | collective-permute-done | bytes 49184 | tf_op jit(solution)/shard_map/ppermute | solution.py:220
  55.7 1.1 %collective-permute-done.5 = f32[2,48,128]{2,1,0:T(8,128)S(1)} collective-permute-done((f32[2,48,128]{2,1,0:T(8,128)S(1)}, f32[2,48,128]{2,1,0:T(8,128)S(1)}, u32[]{:S(2)}, u32[]{:S(2)}) %collective-permute-start.5) | collective-permute-done | bytes 49184 | tf_op jit(solution)/shard_map/ppermute | solution.py:220
  56.8 0.0 collective-permute-done.4
  56.8 0.1 collective-permute-start.7
  56.9 1.2 %collective-permute-done.7.other_ref = f32[2,48,128]{2,1,0:T(8,128)S(1)} collective-permute-done((f32[2,48,128]{2,1,0:T(8,128)S(1)}, f32[2,48,128]{2,1,0:T(8,128)S(1)}, u32[]{:S(2)}, u32[]{:S(2)}) %collective-permute-start.7) | collective-permute-done | bytes 49184 | tf_op jit(solution)/shard_map/ppermute | solution.py:220
  58.1 10.8 %make_basis.1 = (f32[16384,128]{1,0:T(8,128)}, f32[128,128]{1,0:T(8,128)}) custom-call(s32[1]{0:T(128)} %bitcast.me_ref, f32[2,48,128]{2,1,0:T(8,128)S(1)} %pad_maximum_fusion.2.mine_ref, f32[2,48,128]{2,1,0:T(8,128)S(1)} %collective-permute-done.7.other_ref, f32[2048,128]{1,0:T(8,128)S(1)} %bitcast.6, bf16[16384,128]{1,0:T(8,128)(2,1)} %copy-done), custom_call_target="tpu_custom_call" | custom-call | tf_op jit(solution)/shard_map/make_basis/pallas_call | solution.py:472
  (8 shorter events, 0.1 us)
Async XLA Ops:
  0.6 12.1 %copy-start.2 = (f32[16384,8]{0,1:T(8,128)S(1)}, f32[16384,8]{0,1:T(8,128)}, u32[]{:S(2)}) copy-start(f32[16384,8]{0,1:T(8,128)} %param.7) | copy-start | bytes 1572868
  0.6 12.1 %copy-start.1 = (s32[16384,8]{0,1:T(8,128)S(1)}, s32[16384,8]{0,1:T(8,128)}, u32[]{:S(2)}) copy-start(s32[16384,8]{0,1:T(8,128)} %param.6) | copy-start | bytes 1572868
  5.4 33.5 %all-to-all-start = ((f32[32,64,128]{2,1,0:T(8,128)}), f32[32,64,128]{2,1,0:T(8,128)S(1)}, u32[]{:S(2)}, u32[]{:S(2)}) async-start(f32[32,64,128]{2,1,0:T(8,128)} %bitcast.9), calls=%async_computation | async-start | bytes 2097152 | tf_op jit(solution)/shard_map/all_to_all | solution.py:488
  20.9 2.0 %copy-start = (bf16[16384,128]{1,0:T(8,128)(2,1)}, bf16[16384,128]{1,0:T(8,128)(2,1)S(1)}, u32[]{:S(2)}) copy-start(bf16[16384,128]{1,0:T(8,128)(2,1)S(1)} %get-tuple-element.9.mat_hbm) | copy-start | bytes 12582916
  41.2 1.3 %collective-permute-start = (f32[2,48,128]{2,1,0:T(8,128)S(1)}, f32[2,48,128]{2,1,0:T(8,128)S(1)}, u32[]{:S(2)}, u32[]{:S(2)}) collective-permute-start(f32[2,48,128]{2,1,0:T(8,128)S(1)} %get-tuple-element.8), channel_id=1, source_target_pairs={{0,1},{1,0},{2,3},{3,2},{4,5},{5,4},{6,7},{7,6},{8,9},{9,8},{10,11... | collective-permute-start | bytes 147464 | tf_op jit(solution)/shard_map/ppermute | solution.py:220
  42.6 5.1 %collective-permute-start.3 = (f32[2,48,128]{2,1,0:T(8,128)S(1)}, f32[2,48,128]{2,1,0:T(8,128)S(1)}, u32[]{:S(2)}, u32[]{:S(2)}) collective-permute-start(f32[2,48,128]{2,1,0:T(8,128)S(1)} %pad_maximum_fusion), channel_id=1, source_target_pairs={{0,6},{1,7},{2,4},{3,5},{4,2},{5,3},{6,0},{7,1},{8,14},{9,15},{10,... | collective-permute-start | bytes 147464 | tf_op jit(solution)/shard_map/ppermute | solution.py:220
  45.0 4.1 %collective-permute-start.2 = (f32[2,48,128]{2,1,0:T(8,128)S(1)}, f32[2,48,128]{2,1,0:T(8,128)S(1)}, u32[]{:S(2)}, u32[]{:S(2)}) collective-permute-start(f32[2,48,128]{2,1,0:T(8,128)S(1)} %pad_maximum_fusion), channel_id=1, source_target_pairs={{0,4},{1,5},{2,6},{3,7},{4,0},{5,1},{6,2},{7,3},{8,12},{9,13},{10,... | collective-permute-start | bytes 147464 | tf_op jit(solution)/shard_map/ppermute | solution.py:220
  45.6 4.1 %collective-permute-start.1 = (f32[2,48,128]{2,1,0:T(8,128)S(1)}, f32[2,48,128]{2,1,0:T(8,128)S(1)}, u32[]{:S(2)}, u32[]{:S(2)}) collective-permute-start(f32[2,48,128]{2,1,0:T(8,128)S(1)} %pad_maximum_fusion), channel_id=1, source_target_pairs={{0,2},{1,3},{2,0},{3,1},{4,6},{5,7},{6,4},{7,5},{8,10},{9,11},{10,... | collective-permute-start | bytes 147464 | tf_op jit(solution)/shard_map/ppermute | solution.py:220
  49.7 6.0 %collective-permute-start.6 = (f32[2,48,128]{2,1,0:T(8,128)S(1)}, f32[2,48,128]{2,1,0:T(8,128)S(1)}, u32[]{:S(2)}, u32[]{:S(2)}) collective-permute-start(f32[2,48,128]{2,1,0:T(8,128)S(1)} %pad_maximum_fusion.1), channel_id=1, source_target_pairs={{0,24},{1,25},{2,26},{3,27},{4,28},{5,29},{6,30},{7,31},{8,16},{9,... | collective-permute-start | bytes 147464 | tf_op jit(solution)/shard_map/ppermute | solution.py:220
  51.2 5.5 %collective-permute-start.5 = (f32[2,48,128]{2,1,0:T(8,128)S(1)}, f32[2,48,128]{2,1,0:T(8,128)S(1)}, u32[]{:S(2)}, u32[]{:S(2)}) collective-permute-start(f32[2,48,128]{2,1,0:T(8,128)S(1)} %pad_maximum_fusion.1), channel_id=1, source_target_pairs={{0,16},{1,17},{2,18},{3,19},{4,20},{5,21},{6,22},{7,23},{8,24},{9,... | collective-permute-start | bytes 147464 | tf_op jit(solution)/shard_map/ppermute | solution.py:220
  51.9 4.9 %collective-permute-start.4 = (f32[2,48,128]{2,1,0:T(8,128)S(1)}, f32[2,48,128]{2,1,0:T(8,128)S(1)}, u32[]{:S(2)}, u32[]{:S(2)}) collective-permute-start(f32[2,48,128]{2,1,0:T(8,128)S(1)} %pad_maximum_fusion.1), channel_id=1, source_target_pairs={{0,8},{1,9},{2,10},{3,11},{4,12},{5,13},{6,14},{7,15},{8,0},{9,1},... | collective-permute-start | bytes 147464 | tf_op jit(solution)/shard_map/ppermute | solution.py:220
  56.8 1.3 %collective-permute-start.7 = (f32[2,48,128]{2,1,0:T(8,128)S(1)}, f32[2,48,128]{2,1,0:T(8,128)S(1)}, u32[]{:S(2)}, u32[]{:S(2)}) collective-permute-start(f32[2,48,128]{2,1,0:T(8,128)S(1)} %pad_maximum_fusion.2.mine_ref), channel_id=1, source_target_pairs={{0,1},{1,0},{2,3},{3,2},{4,5},{5,4},{6,7},{7,6},{8,9},{9,8},{10,11... | collective-permute-start | bytes 147464 | tf_op jit(solution)/shard_map/ppermute | solution.py:220

commit v5 on v4

--- a/solution.py
+++ b/solution.py
@@ -19,6 +19,16 @@
 
 def rough(left, right, dims=((1,), (0,))):
     return lax.dot_general(left.astype(BF16), right.astype(BF16), (dims, ((), ())), preferred_element_type=F32)
+
+
+def thirds(value):
+    high = value.astype(BF16)
+    rest = value - high.astype(F32)
+    middle = rest.astype(BF16)
+    return high, middle, (rest - middle.astype(F32)).astype(BF16)
+
+
+CHUNKS = 8
 
 
 PIECES = 8
@@ -112,7 +122,8 @@
         mat_ref[cols, :] = mat
         gram = jnp.dot(pair.astype(BF16), mat, preferred_element_type=F32)
         half = gram[:cap] + gram[cap:]
-        slot_ref[sub * cap : (sub + 1) * cap, :] = half[:, :cap] + half[:, cap:]
+        s_high, s_middle, s_low = thirds(half[:, :cap] + half[:, cap:])
+        slot_ref[sub * cap : (sub + 1) * cap, :] = jnp.concatenate([s_high, s_middle, s_low, s_high], axis=1)
 
 
 def weave(me, stencil, weights, peers, cap):
@@ -129,12 +140,12 @@
         ],
         out_specs=[
             pl.BlockSpec((block, 2 * cap), lambda i, m: (i, 0)),
-            pl.BlockSpec((runs * cap, cap), lambda i, m: (i, 0)),
+            pl.BlockSpec((runs * cap, 4 * cap), lambda i, m: (i, 0)),
         ],
     )
     return pl.pallas_call(
         functools.partial(weave_kernel, runs, run_rows, cap, peers),
-        out_shape=[jax.ShapeDtypeStruct((rows, 2 * cap), BF16), jax.ShapeDtypeStruct((peers * cap, cap), F32)],
+        out_shape=[jax.ShapeDtypeStruct((rows, 2 * cap), BF16), jax.ShapeDtypeStruct((peers * cap, 4 * cap), BF16)],
         grid_spec=grid_spec,
         compiler_params=pltpu.CompilerParams(vmem_limit_bytes=16 * 1024 * 1024),
         cost_estimate=pl.CostEstimate(flops=8 * 10**9, bytes_accessed=40 * 10**6, transcendentals=0),
@@ -180,7 +191,15 @@
         peer = lax.rem(me_ref[0] + run, peers)
         at = pl.ds(pl.multiple_of(peer * cap, cap), cap)
         frm = pl.ds(pl.multiple_of(run * cap, cap), cap)
-        z_ref[at, :] = exact(slot_ref[frm, :], x_ref[at, :])
+        high, middle, low = thirds(x_ref[at, :])
+        wide = jnp.concatenate([high, middle], axis=1)
+        last = jnp.concatenate([low, jnp.zeros_like(low)], axis=1)
+        many = jnp.dot(
+            slot_ref[frm, :],
+            jnp.concatenate([wide, wide, wide, last], axis=0),
+            preferred_element_type=F32,
+        )
+        z_ref[at, :] = many[:, :snaps] + many[:, snaps:]
         return carry
 
     lax.fori_loop(0, peers, one_run, 0, unroll=16)
@@ -211,7 +230,7 @@
         in_specs=[pl.BlockSpec(memory_space=pltpu.SMEM), vmem, vmem],
         out_specs=[vmem, vmem],
         scratch_shapes=[pltpu.VMEM(x.shape, F32)],
-        compiler_params=pltpu.CompilerParams(vmem_limit_bytes=limit((x.shape, F32), (x.shape, F32), (slots.shape, F32))),
+        compiler_params=pltpu.CompilerParams(vmem_limit_bytes=limit((x.shape, F32), (x.shape, F32), (slots.shape, BF16))),
         name="local_gram",
     )(me, x, slots)
 
@@ -269,19 +288,17 @@
 
     tops, inverses = [], []
     heads = [across(left[0], k) for k in range(TILE)]
-    ahead = [across(left[1], k) for k in range(TILE)]
     for j in range(panels):
         start, stop = j * TILE, (j + 1) * TILE
         later = range(j + 1, panels)
         tails = {i: [across(left[i], start + k) for k in range(TILE)] for i in later if i > j + 1}
         near_heads = [across(left[j + 1], stop + c) for c in range(TILE)] if j + 1 < panels else []
-        near_ahead = [across(left[j + 2], stop + c) for c in range(TILE)] if j + 2 < panels else []
-        second = list(tails[j + 2]) if j + 2 < panels else []
+        ahead = [across(left[j + 1], start + k) for k in range(TILE)] if j + 1 < panels else []
         block = [[down(heads[k], i) for k in range(i + 1)] for i in range(TILE)]
         rows = [down(left[j], k) for k in range(TILE)]
         irows = [jnp.where(lane < start, rows[k], (lane == start + k).astype(F32)) for k in range(TILE)]
         kept = (lane < start) | (lane >= stop)
-        groups = [g for g in (ahead, second, rows, irows) if g]
+        groups = [g for g in (ahead, rows, irows) if g]
         over, coef, solved = [], {}, []
         for k in range(0, TILE, 2):
             n = k + 1
@@ -309,8 +326,6 @@
                     if near_heads:
                         scaled = down(shrunk[p], c)
                         near_heads[c] = near_heads[c] - ahead[p] * scaled
-                    if near_ahead:
-                        near_ahead[c] = near_ahead[c] - second[p] * scaled
             for p in (k, n):
                 solved.append(jnp.where(lane < stop, irows[p], rows[p]) * over[p])
         top, inverse, pivots = rows[0], irows[0], block[0][0]
@@ -321,22 +336,21 @@
         root = lax.rsqrt(pivots)
         tops.append(jnp.where(lane >= sub + start, top * root, 0.0))
         inverses.append(inverse * root)
-        for i, columns in ((j + 1, ahead), (j + 2, second)):
-            if columns:
-                value = jnp.where(kept, left[i], 0.0)
-                for k in range(TILE):
-                    value = value - columns[k] * solved[k]
-                left[i] = value
-        if j + 3 < panels:
+        if ahead:
+            value = jnp.where(kept, left[j + 1], 0.0)
+            for k in range(TILE):
+                value = value - ahead[k] * solved[k]
+            left[j + 1] = value
+        if j + 2 < panels:
             for k in reversed(range(TILE)):
                 for i in range(k):
                     solved[i] = solved[i] - coef[k, i] * solved[k]
-            for i in range(j + 3, panels):
+            for i in range(j + 2, panels):
                 value = jnp.where(kept, left[i], 0.0)
                 for k in range(TILE):
                     value = value - tails[i][k] * solved[k]
                 left[i] = value
-        heads, ahead = near_heads, near_ahead
+        heads = near_heads
     return jnp.concatenate(tops, axis=0), jnp.concatenate(inverses, axis=0)
 
 
@@ -389,16 +403,6 @@
     return upper * (1.0 / across), inv * down
 
 
-def thirds(value):
-    high = value.astype(BF16)
-    rest = value - high.astype(F32)
-    middle = rest.astype(BF16)
-    return high, middle, (rest - middle.astype(F32)).astype(BF16)
-
-
-CHUNKS = 8
-
-
 def basis_kernel(
     cap, peers, scale, me_ref, mine_ref, other_ref, x_ref, mat_hbm, out_hbm, r_ref, y_ref, mat_ref, out_ref, sems, in_sem
 ):

time: 69.1 us -> 69 us (level)
  transfers between devices with their start and end apart: 9 -> 9, of which waited for: 8 -> 8; matrix products, arithmetic and copies ran while one was open for 0% -> 0% of each run, Pallas kernels for 12% -> 13%
where the time goes in v5:
time: 69 us; the launch traced here: 68.8 us
  Pallas kernels  26.4 us (38%)
  waiting for transfers between devices  24.1 us (35%)
  starting transfers between devices  15.5 us (22%)
  local copies, waits for them, and re-layouts  1.95 us (3%)
  between operations  0.78 us (1%)
    all_to_all x1, waiting for transfers between devices, body(): lax.all_to_all(outgoing, 'rows', split_axis=0, concat_axis=0, tiled=True)  15.5 us
    pallas_call x1, Pallas kernels, make_basis(): pl.pallas_call(functools.partial(basis_kernel, cap, peers, math.sqrt(tota...  10.8 us
    pallas_call x1, Pallas kernels, weave(): pl.pallas_call(functools.partial(weave_kernel, runs, run_rows, cap, peers...  8.75 us
    ppermute x8, waiting for transfers between devices, hop(): return lax.ppermute(value, 'rows', [(i, i ^ mask) for i in range(peers)])  8.56 us
    ppermute x8, starting transfers between devices, hop(): return lax.ppermute(value, 'rows', [(i, i ^ mask) for i in range(peers)])  8.15 us
    all_to_all x1, starting transfers between devices, body(): lax.all_to_all(outgoing, 'rows', split_axis=0, concat_axis=0, tiled=True)  7.3 us
    pallas_call x1, Pallas kernels, pick_donors(): pl.pallas_call(pick_kernel, out_shape=jax.ShapeDtypeStruct((peers * cap,...  4.72 us
    pallas_call x1, Pallas kernels, local_gram(): pl.pallas_call(functools.partial(gram_kernel, peers, cap), out_shape=[sha...  2.13 us
  transfers between devices with their start and end apart: 9, of which 8 were waited for; matrix products, arithmetic and copies ran while one was open for 0% of the time, Pallas kernels for 13%

profile of v5, /device:TPU:0, one launch (start us, length us, event | category | flops | bytes accessed | tf_op | source)
XLA Modules:
  0.0 68.8 jit_solution(4455423661126091885)
XLA Ops:
  0.6 0.0 copy-start.2
  0.6 0.0 copy-start.1
  0.7 4.7 %pick_donors.1 = f32[2048,128]{1,0:T(8,128)} custom-call(s32[32,64]{1,0:T(8,128)} %send_hbm.1, f32[8192,128]{1,0:T(8,128)} %snap_hbm.1), custom_call_target="tpu_custom_call" | custom-call | tf_op jit(solution)/shard_map/pick_donors/pallas_call | solution.py:87
  5.4 7.3 %all-to-all-start = ((f32[32,64,128]{2,1,0:T(8,128)}), f32[32,64,128]{2,1,0:T(8,128)S(1)}, u32[]{:S(2)}, u32[]{:S(2)}) async-start(f32[32,64,128]{2,1,0:T(8,128)} %bitcast.9), calls=%async_computation | async-start | bytes 2097152 | tf_op jit(solution)/shard_map/all_to_all | solution.py:492
  12.7 0.0 copy-done.2
  12.7 0.0 copy-done.1
  12.7 8.7 %weave.1 = (bf16[16384,128]{1,0:T(8,128)(2,1)S(1)}, bf16[2048,256]{1,0:T(8,128)(2,1)S(1)}) custom-call(s32[1]{0:T(128)} %bitcast.me_ref, s32[8,16384]{1,0:T(8,128)S(1)} %bitcast.7, f32[8,16384]{1,0:T(8,128)S(1)} %bitcast.8), custom_call_target="tpu_custom_call" | custom-call | flops 8000000000 | bytes 40000000 | tf_op jit(solution)/shard_map/weave/pallas_call | solution.py:146
  21.5 0.0 copy-start
  21.5 1.9 %copy-done = bf16[16384,128]{1,0:T(8,128)(2,1)} copy-done((bf16[16384,128]{1,0:T(8,128)(2,1)}, bf16[16384,128]{1,0:T(8,128)(2,1)S(1)}, u32[]{:S(2)}) %copy-start) | copy-done | bytes 4194328
  23.4 15.5 %all-to-all-done = f32[32,64,128]{2,1,0:T(8,128)S(1)} async-done(((f32[32,64,128]{2,1,0:T(8,128)}), f32[32,64,128]{2,1,0:T(8,128)S(1)}, u32[]{:S(2)}, u32[]{:S(2)}) %all-to-all-start) | async-done | bytes 1048608 | tf_op jit(solution)/shard_map/all_to_all | solution.py:492
  38.9 2.1 %local_gram.1 = (f32[2,48,128]{2,1,0:T(8,128)S(1)}, f32[2,48,128]{2,1,0:T(8,128)S(1)}) custom-call(s32[1]{0:T(128)} %bitcast.me_ref, f32[2048,128]{1,0:T(8,128)S(1)} %bitcast.5, bf16[2048,256]{1,0:T(8,128)(2,1)S(1)} %get-tuple-element.6.slot_ref), custom_call_target="tpu_custom_call" | custom-call | tf_op jit(solution)/shard_map/local_gram/pallas_call | solution.py:227
  41.1 0.1 collective-permute-start
  41.1 1.2 %collective-permute-done = f32[2,48,128]{2,1,0:T(8,128)S(1)} collective-permute-done((f32[2,48,128]{2,1,0:T(8,128)S(1)}, f32[2,48,128]{2,1,0:T(8,128)S(1)}, u32[]{:S(2)}, u32[]{:S(2)}) %collective-permute-start) | collective-permute-done | bytes 49184 | tf_op jit(solution)/shard_map/ppermute | solution.py:239
  42.4 2.5 %collective-permute-start.3 = (f32[2,48,128]{2,1,0:T(8,128)S(1)}, f32[2,48,128]{2,1,0:T(8,128)S(1)}, u32[]{:S(2)}, u32[]{:S(2)}) collective-permute-start(f32[2,48,128]{2,1,0:T(8,128)S(1)} %pad_maximum_fusion), channel_id=1, source_target_pairs={{0,6},{1,7},{2,4},{3,5},{4,2},{5,3},{6,0},{7,1},{8,14},{9,15},{10,... | collective-permute-start | bytes 147464 | tf_op jit(solution)/shard_map/ppermute | solution.py:239
  44.9 0.5 collective-permute-start.2
  45.4 0.6 collective-permute-start.1
  46.0 1.5 %collective-permute-done.3 = f32[2,48,128]{2,1,0:T(8,128)S(1)} collective-permute-done((f32[2,48,128]{2,1,0:T(8,128)S(1)}, f32[2,48,128]{2,1,0:T(8,128)S(1)}, u32[]{:S(2)}, u32[]{:S(2)}) %collective-permute-start.3) | collective-permute-done | bytes 49184 | tf_op jit(solution)/shard_map/ppermute | solution.py:239
  47.5 1.5 %collective-permute-done.2 = f32[2,48,128]{2,1,0:T(8,128)S(1)} collective-permute-done((f32[2,48,128]{2,1,0:T(8,128)S(1)}, f32[2,48,128]{2,1,0:T(8,128)S(1)}, u32[]{:S(2)}, u32[]{:S(2)}) %collective-permute-start.2) | collective-permute-done | bytes 49184 | tf_op jit(solution)/shard_map/ppermute | solution.py:239
  48.9 0.5 collective-permute-done.1
  49.6 1.5 %collective-permute-start.6 = (f32[2,48,128]{2,1,0:T(8,128)S(1)}, f32[2,48,128]{2,1,0:T(8,128)S(1)}, u32[]{:S(2)}, u32[]{:S(2)}) collective-permute-start(f32[2,48,128]{2,1,0:T(8,128)S(1)} %pad_maximum_fusion.1), channel_id=1, source_target_pairs={{0,24},{1,25},{2,26},{3,27},{4,28},{5,29},{6,30},{7,31},{8,16},{9,... | collective-permute-start | bytes 147464 | tf_op jit(solution)/shard_map/ppermute | solution.py:239
  51.1 0.6 collective-permute-start.5
  51.7 2.3 %collective-permute-start.4 = (f32[2,48,128]{2,1,0:T(8,128)S(1)}, f32[2,48,128]{2,1,0:T(8,128)S(1)}, u32[]{:S(2)}, u32[]{:S(2)}) collective-permute-start(f32[2,48,128]{2,1,0:T(8,128)S(1)} %pad_maximum_fusion.1), channel_id=1, source_target_pairs={{0,8},{1,9},{2,10},{3,11},{4,12},{5,13},{6,14},{7,15},{8,0},{9,1},... | collective-permute-start | bytes 147464 | tf_op jit(solution)/shard_map/ppermute | solution.py:239
  54.0 1.5 %collective-permute-done.6 = f32[2,48,128]{2,1,0:T(8,128)S(1)} collective-permute-done((f32[2,48,128]{2,1,0:T(8,128)S(1)}, f32[2,48,128]{2,1,0:T(8,128)S(1)}, u32[]{:S(2)}, u32[]{:S(2)}) %collective-permute-start.6) | collective-permute-done | bytes 49184 | tf_op jit(solution)/shard_map/ppermute | solution.py:239
  55.5 1.1 %collective-permute-done.5 = f32[2,48,128]{2,1,0:T(8,128)S(1)} collective-permute-done((f32[2,48,128]{2,1,0:T(8,128)S(1)}, f32[2,48,128]{2,1,0:T(8,128)S(1)}, u32[]{:S(2)}, u32[]{:S(2)}) %collective-permute-start.5) | collective-permute-done | bytes 49184 | tf_op jit(solution)/shard_map/ppermute | solution.py:239
  56.6 0.0 collective-permute-done.4
  56.7 0.1 collective-permute-start.7
  56.8 1.2 %collective-permute-done.7.other_ref = f32[2,48,128]{2,1,0:T(8,128)S(1)} collective-permute-done((f32[2,48,128]{2,1,0:T(8,128)S(1)}, f32[2,48,128]{2,1,0:T(8,128)S(1)}, u32[]{:S(2)}, u32[]{:S(2)}) %collective-permute-start.7) | collective-permute-done | bytes 49184 | tf_op jit(solution)/shard_map/ppermute | solution.py:239
  58.0 10.8 %make_basis.1 = (f32[16384,128]{1,0:T(8,128)}, f32[128,128]{1,0:T(8,128)}) custom-call(s32[1]{0:T(128)} %bitcast.me_ref, f32[2,48,128]{2,1,0:T(8,128)S(1)} %pad_maximum_fusion.2.mine_ref, f32[2,48,128]{2,1,0:T(8,128)S(1)} %collective-permute-done.7.other_ref, f32[2048,128]{1,0:T(8,128)S(1)} %bitcast.6, bf16[16384,128]{1,0:T(8,128)(2,1)} %copy-done), custom_call_target="tpu_custom_call" | custom-call | tf_op jit(solution)/shard_map/make_basis/pallas_call | solution.py:476
  (8 shorter events, 0.1 us)
Async XLA Ops:
  0.6 12.1 %copy-start.2 = (f32[16384,8]{0,1:T(8,128)S(1)}, f32[16384,8]{0,1:T(8,128)}, u32[]{:S(2)}) copy-start(f32[16384,8]{0,1:T(8,128)} %param.7) | copy-start | bytes 1572868
  0.6 12.1 %copy-start.1 = (s32[16384,8]{0,1:T(8,128)S(1)}, s32[16384,8]{0,1:T(8,128)}, u32[]{:S(2)}) copy-start(s32[16384,8]{0,1:T(8,128)} %param.6) | copy-start | bytes 1572868
  5.4 33.5 %all-to-all-start = ((f32[32,64,128]{2,1,0:T(8,128)}), f32[32,64,128]{2,1,0:T(8,128)S(1)}, u32[]{:S(2)}, u32[]{:S(2)}) async-start(f32[32,64,128]{2,1,0:T(8,128)} %bitcast.9), calls=%async_computation | async-start | bytes 2097152 | tf_op jit(solution)/shard_map/all_to_all | solution.py:492
  21.5 2.0 %copy-start = (bf16[16384,128]{1,0:T(8,128)(2,1)}, bf16[16384,128]{1,0:T(8,128)(2,1)S(1)}, u32[]{:S(2)}) copy-start(bf16[16384,128]{1,0:T(8,128)(2,1)S(1)} %get-tuple-element.9.mat_hbm) | copy-start | bytes 12582916
  41.1 1.3 %collective-permute-start = (f32[2,48,128]{2,1,0:T(8,128)S(1)}, f32[2,48,128]{2,1,0:T(8,128)S(1)}, u32[]{:S(2)}, u32[]{:S(2)}) collective-permute-start(f32[2,48,128]{2,1,0:T(8,128)S(1)} %get-tuple-element.8), channel_id=1, source_target_pairs={{0,1},{1,0},{2,3},{3,2},{4,5},{5,4},{6,7},{7,6},{8,9},{9,8},{10,11... | collective-permute-start | bytes 147464 | tf_op jit(solution)/shard_map/ppermute | solution.py:239
  42.4 5.1 %collective-permute-start.3 = (f32[2,48,128]{2,1,0:T(8,128)S(1)}, f32[2,48,128]{2,1,0:T(8,128)S(1)}, u32[]{:S(2)}, u32[]{:S(2)}) collective-permute-start(f32[2,48,128]{2,1,0:T(8,128)S(1)} %pad_maximum_fusion), channel_id=1, source_target_pairs={{0,6},{1,7},{2,4},{3,5},{4,2},{5,3},{6,0},{7,1},{8,14},{9,15},{10,... | collective-permute-start | bytes 147464 | tf_op jit(solution)/shard_map/ppermute | solution.py:239
  44.9 4.1 %collective-permute-start.2 = (f32[2,48,128]{2,1,0:T(8,128)S(1)}, f32[2,48,128]{2,1,0:T(8,128)S(1)}, u32[]{:S(2)}, u32[]{:S(2)}) collective-permute-start(f32[2,48,128]{2,1,0:T(8,128)S(1)} %pad_maximum_fusion), channel_id=1, source_target_pairs={{0,4},{1,5},{2,6},{3,7},{4,0},{5,1},{6,2},{7,3},{8,12},{9,13},{10,... | collective-permute-start | bytes 147464 | tf_op jit(solution)/shard_map/ppermute | solution.py:239
  45.4 4.1 %collective-permute-start.1 = (f32[2,48,128]{2,1,0:T(8,128)S(1)}, f32[2,48,128]{2,1,0:T(8,128)S(1)}, u32[]{:S(2)}, u32[]{:S(2)}) collective-permute-start(f32[2,48,128]{2,1,0:T(8,128)S(1)} %pad_maximum_fusion), channel_id=1, source_target_pairs={{0,2},{1,3},{2,0},{3,1},{4,6},{5,7},{6,4},{7,5},{8,10},{9,11},{10,... | collective-permute-start | bytes 147464 | tf_op jit(solution)/shard_map/ppermute | solution.py:239
  49.6 6.0 %collective-permute-start.6 = (f32[2,48,128]{2,1,0:T(8,128)S(1)}, f32[2,48,128]{2,1,0:T(8,128)S(1)}, u32[]{:S(2)}, u32[]{:S(2)}) collective-permute-start(f32[2,48,128]{2,1,0:T(8,128)S(1)} %pad_maximum_fusion.1), channel_id=1, source_target_pairs={{0,24},{1,25},{2,26},{3,27},{4,28},{5,29},{6,30},{7,31},{8,16},{9,... | collective-permute-start | bytes 147464 | tf_op jit(solution)/shard_map/ppermute | solution.py:239
  51.1 5.5 %collective-permute-start.5 = (f32[2,48,128]{2,1,0:T(8,128)S(1)}, f32[2,48,128]{2,1,0:T(8,128)S(1)}, u32[]{:S(2)}, u32[]{:S(2)}) collective-permute-start(f32[2,48,128]{2,1,0:T(8,128)S(1)} %pad_maximum_fusion.1), channel_id=1, source_target_pairs={{0,16},{1,17},{2,18},{3,19},{4,20},{5,21},{6,22},{7,23},{8,24},{9,... | collective-permute-start | bytes 147464 | tf_op jit(solution)/shard_map/ppermute | solution.py:239
  51.7 4.9 %collective-permute-start.4 = (f32[2,48,128]{2,1,0:T(8,128)S(1)}, f32[2,48,128]{2,1,0:T(8,128)S(1)}, u32[]{:S(2)}, u32[]{:S(2)}) collective-permute-start(f32[2,48,128]{2,1,0:T(8,128)S(1)} %pad_maximum_fusion.1), channel_id=1, source_target_pairs={{0,8},{1,9},{2,10},{3,11},{4,12},{5,13},{6,14},{7,15},{8,0},{9,1},... | collective-permute-start | bytes 147464 | tf_op jit(solution)/shard_map/ppermute | solution.py:239
  56.7 1.3 %collective-permute-start.7 = (f32[2,48,128]{2,1,0:T(8,128)S(1)}, f32[2,48,128]{2,1,0:T(8,128)S(1)}, u32[]{:S(2)}, u32[]{:S(2)}) collective-permute-start(f32[2,48,128]{2,1,0:T(8,128)S(1)} %pad_maximum_fusion.2.mine_ref), channel_id=1, source_target_pairs={{0,1},{1,0},{2,3},{3,2},{4,5},{5,4},{6,7},{7,6},{8,9},{9,8},{10,11... | collective-permute-start | bytes 147464 | tf_op jit(solution)/shard_map/ppermute | solution.py:239

commit v6 on v5

--- a/solution.py
+++ b/solution.py
@@ -70,7 +70,7 @@
 
     leaving = []
     for i in range(GROUPS):
-        lax.fori_loop(i * group, (i + 1) * group, one_peer, 0, unroll=2)
+        lax.fori_loop(i * group, (i + 1) * group, one_peer, 0, unroll=8)
         at = pl.ds(i * group * cap, group * cap)
         copy = pltpu.make_async_copy(out_ref.at[at, :], out_hbm.at[at, :], out_sems.at[i])
         copy.start()
@@ -202,7 +202,7 @@
         z_ref[at, :] = many[:, :snaps] + many[:, snaps:]
         return carry
 
-    lax.fori_loop(0, peers, one_run, 0, unroll=16)
+    lax.fori_loop(0, peers, one_run, 0, unroll=32)
     chunk = 256
 
     def one_chunk(i, carry):

time: 69 us -> 68.3 us (0.990)
  Pallas kernels: 26.4 us -> 25.7 us
where the time goes in v6:
time: 68.3 us; the launch traced here: 68.1 us
  Pallas kernels  25.7 us (38%)
  waiting for transfers between devices  24.1 us (35%)
  starting transfers between devices  15.5 us (23%)
  local copies, waits for them, and re-layouts  1.95 us (3%)
  between operations  0.78 us (1%)
    all_to_all x1, waiting for transfers between devices, body(): lax.all_to_all(outgoing, 'rows', split_axis=0, concat_axis=0, tiled=True)  15.5 us
    pallas_call x1, Pallas kernels, make_basis(): pl.pallas_call(functools.partial(basis_kernel, cap, peers, math.sqrt(tota...  10.8 us
    pallas_call x1, Pallas kernels, weave(): pl.pallas_call(functools.partial(weave_kernel, runs, run_rows, cap, peers...  8.75 us
    ppermute x8, waiting for transfers between devices, hop(): return lax.ppermute(value, 'rows', [(i, i ^ mask) for i in range(peers)])  8.56 us
    ppermute x8, starting transfers between devices, hop(): return lax.ppermute(value, 'rows', [(i, i ^ mask) for i in range(peers)])  8.15 us
    all_to_all x1, starting transfers between devices, body(): lax.all_to_all(outgoing, 'rows', split_axis=0, concat_axis=0, tiled=True)  7.3 us
    pallas_call x1, Pallas kernels, pick_donors(): pl.pallas_call(pick_kernel, out_shape=jax.ShapeDtypeStruct((peers * cap,...  4.13 us
    pallas_call x1, Pallas kernels, local_gram(): pl.pallas_call(functools.partial(gram_kernel, peers, cap), out_shape=[sha...  2 us
  transfers between devices with their start and end apart: 9, of which 8 were waited for; matrix products, arithmetic and copies ran while one was open for 0% of the time, Pallas kernels for 13%

profile of v6, /device:TPU:0, one launch (start us, length us, event | category | flops | bytes accessed | tf_op | source)
XLA Modules:
  0.0 68.1 jit_solution(2706062539226088600)
XLA Ops:
  0.6 0.0 copy-start.2
  0.6 0.0 copy-start.1
  0.7 4.1 %pick_donors.1 = f32[2048,128]{1,0:T(8,128)} custom-call(s32[32,64]{1,0:T(8,128)} %send_hbm.1, f32[8192,128]{1,0:T(8,128)} %snap_hbm.1), custom_call_target="tpu_custom_call" | custom-call | tf_op jit(solution)/shard_map/pick_donors/pallas_call | solution.py:87
  4.8 7.3 %all-to-all-start = ((f32[32,64,128]{2,1,0:T(8,128)}), f32[32,64,128]{2,1,0:T(8,128)S(1)}, u32[]{:S(2)}, u32[]{:S(2)}) async-start(f32[32,64,128]{2,1,0:T(8,128)} %bitcast.9), calls=%async_computation | async-start | bytes 2097152 | tf_op jit(solution)/shard_map/all_to_all | solution.py:492
  12.1 0.0 copy-done.2
  12.1 0.0 copy-done.1
  12.1 8.8 %weave.1 = (bf16[16384,128]{1,0:T(8,128)(2,1)S(1)}, bf16[2048,256]{1,0:T(8,128)(2,1)S(1)}) custom-call(s32[1]{0:T(128)} %bitcast.me_ref, s32[8,16384]{1,0:T(8,128)S(1)} %bitcast.7, f32[8,16384]{1,0:T(8,128)S(1)} %bitcast.8), custom_call_target="tpu_custom_call" | custom-call | flops 8000000000 | bytes 40000000 | tf_op jit(solution)/shard_map/weave/pallas_call | solution.py:146
  20.9 0.0 copy-start
  20.9 1.9 %copy-done = bf16[16384,128]{1,0:T(8,128)(2,1)} copy-done((bf16[16384,128]{1,0:T(8,128)(2,1)}, bf16[16384,128]{1,0:T(8,128)(2,1)S(1)}, u32[]{:S(2)}) %copy-start) | copy-done | bytes 4194328
  22.8 15.5 %all-to-all-done = f32[32,64,128]{2,1,0:T(8,128)S(1)} async-done(((f32[32,64,128]{2,1,0:T(8,128)}), f32[32,64,128]{2,1,0:T(8,128)S(1)}, u32[]{:S(2)}, u32[]{:S(2)}) %all-to-all-start) | async-done | bytes 1048608 | tf_op jit(solution)/shard_map/all_to_all | solution.py:492
  38.3 2.0 %local_gram.1 = (f32[2,48,128]{2,1,0:T(8,128)S(1)}, f32[2,48,128]{2,1,0:T(8,128)S(1)}) custom-call(s32[1]{0:T(128)} %bitcast.me_ref, f32[2048,128]{1,0:T(8,128)S(1)} %bitcast.5, bf16[2048,256]{1,0:T(8,128)(2,1)S(1)} %get-tuple-element.6.slot_ref), custom_call_target="tpu_custom_call" | custom-call | tf_op jit(solution)/shard_map/local_gram/pallas_call | solution.py:227
  40.3 0.1 collective-permute-start
  40.4 1.2 %collective-permute-done = f32[2,48,128]{2,1,0:T(8,128)S(1)} collective-permute-done((f32[2,48,128]{2,1,0:T(8,128)S(1)}, f32[2,48,128]{2,1,0:T(8,128)S(1)}, u32[]{:S(2)}, u32[]{:S(2)}) %collective-permute-start) | collective-permute-done | bytes 49184 | tf_op jit(solution)/shard_map/ppermute | solution.py:239
  41.7 2.5 %collective-permute-start.3 = (f32[2,48,128]{2,1,0:T(8,128)S(1)}, f32[2,48,128]{2,1,0:T(8,128)S(1)}, u32[]{:S(2)}, u32[]{:S(2)}) collective-permute-start(f32[2,48,128]{2,1,0:T(8,128)S(1)} %pad_maximum_fusion), channel_id=1, source_target_pairs={{0,6},{1,7},{2,4},{3,5},{4,2},{5,3},{6,0},{7,1},{8,14},{9,15},{10,... | collective-permute-start | bytes 147464 | tf_op jit(solution)/shard_map/ppermute | solution.py:239
  44.1 0.5 collective-permute-start.2
  44.7 0.6 collective-permute-start.1
  45.2 1.5 %collective-permute-done.3 = f32[2,48,128]{2,1,0:T(8,128)S(1)} collective-permute-done((f32[2,48,128]{2,1,0:T(8,128)S(1)}, f32[2,48,128]{2,1,0:T(8,128)S(1)}, u32[]{:S(2)}, u32[]{:S(2)}) %collective-permute-start.3) | collective-permute-done | bytes 49184 | tf_op jit(solution)/shard_map/ppermute | solution.py:239
  46.7 1.5 %collective-permute-done.2 = f32[2,48,128]{2,1,0:T(8,128)S(1)} collective-permute-done((f32[2,48,128]{2,1,0:T(8,128)S(1)}, f32[2,48,128]{2,1,0:T(8,128)S(1)}, u32[]{:S(2)}, u32[]{:S(2)}) %collective-permute-start.2) | collective-permute-done | bytes 49184 | tf_op jit(solution)/shard_map/ppermute | solution.py:239
  48.2 0.5 collective-permute-done.1
  48.8 1.5 %collective-permute-start.6 = (f32[2,48,128]{2,1,0:T(8,128)S(1)}, f32[2,48,128]{2,1,0:T(8,128)S(1)}, u32[]{:S(2)}, u32[]{:S(2)}) collective-permute-start(f32[2,48,128]{2,1,0:T(8,128)S(1)} %pad_maximum_fusion.1), channel_id=1, source_target_pairs={{0,24},{1,25},{2,26},{3,27},{4,28},{5,29},{6,30},{7,31},{8,16},{9,... | collective-permute-start | bytes 147464 | tf_op jit(solution)/shard_map/ppermute | solution.py:239
  50.3 0.6 collective-permute-start.5
  51.0 2.3 %collective-permute-start.4 = (f32[2,48,128]{2,1,0:T(8,128)S(1)}, f32[2,48,128]{2,1,0:T(8,128)S(1)}, u32[]{:S(2)}, u32[]{:S(2)}) collective-permute-start(f32[2,48,128]{2,1,0:T(8,128)S(1)} %pad_maximum_fusion.1), channel_id=1, source_target_pairs={{0,8},{1,9},{2,10},{3,11},{4,12},{5,13},{6,14},{7,15},{8,0},{9,1},... | collective-permute-start | bytes 147464 | tf_op jit(solution)/shard_map/ppermute | solution.py:239
  53.3 1.5 %collective-permute-done.6 = f32[2,48,128]{2,1,0:T(8,128)S(1)} collective-permute-done((f32[2,48,128]{2,1,0:T(8,128)S(1)}, f32[2,48,128]{2,1,0:T(8,128)S(1)}, u32[]{:S(2)}, u32[]{:S(2)}) %collective-permute-start.6) | collective-permute-done | bytes 49184 | tf_op jit(solution)/shard_map/ppermute | solution.py:239
  54.8 1.1 %collective-permute-done.5 = f32[2,48,128]{2,1,0:T(8,128)S(1)} collective-permute-done((f32[2,48,128]{2,1,0:T(8,128)S(1)}, f32[2,48,128]{2,1,0:T(8,128)S(1)}, u32[]{:S(2)}, u32[]{:S(2)}) %collective-permute-start.5) | collective-permute-done | bytes 49184 | tf_op jit(solution)/shard_map/ppermute | solution.py:239
  55.9 0.0 collective-permute-done.4
  55.9 0.1 collective-permute-start.7
  56.0 1.2 %collective-permute-done.7.other_ref = f32[2,48,128]{2,1,0:T(8,128)S(1)} collective-permute-done((f32[2,48,128]{2,1,0:T(8,128)S(1)}, f32[2,48,128]{2,1,0:T(8,128)S(1)}, u32[]{:S(2)}, u32[]{:S(2)}) %collective-permute-start.7) | collective-permute-done | bytes 49184 | tf_op jit(solution)/shard_map/ppermute | solution.py:239
  57.2 10.8 %make_basis.1 = (f32[16384,128]{1,0:T(8,128)}, f32[128,128]{1,0:T(8,128)}) custom-call(s32[1]{0:T(128)} %bitcast.me_ref, f32[2,48,128]{2,1,0:T(8,128)S(1)} %pad_maximum_fusion.2.mine_ref, f32[2,48,128]{2,1,0:T(8,128)S(1)} %collective-permute-done.7.other_ref, f32[2048,128]{1,0:T(8,128)S(1)} %bitcast.6, bf16[16384,128]{1,0:T(8,128)(2,1)} %copy-done), custom_call_target="tpu_custom_call" | custom-call | tf_op jit(solution)/shard_map/make_basis/pallas_call | solution.py:476
  (8 shorter events, 0.1 us)
Async XLA Ops:
  0.6 11.5 %copy-start.2 = (f32[16384,8]{0,1:T(8,128)S(1)}, f32[16384,8]{0,1:T(8,128)}, u32[]{:S(2)}) copy-start(f32[16384,8]{0,1:T(8,128)} %param.7) | copy-start | bytes 1572868
  0.6 11.5 %copy-start.1 = (s32[16384,8]{0,1:T(8,128)S(1)}, s32[16384,8]{0,1:T(8,128)}, u32[]{:S(2)}) copy-start(s32[16384,8]{0,1:T(8,128)} %param.6) | copy-start | bytes 1572868
  4.8 33.5 %all-to-all-start = ((f32[32,64,128]{2,1,0:T(8,128)}), f32[32,64,128]{2,1,0:T(8,128)S(1)}, u32[]{:S(2)}, u32[]{:S(2)}) async-start(f32[32,64,128]{2,1,0:T(8,128)} %bitcast.9), calls=%async_computation | async-start | bytes 2097152 | tf_op jit(solution)/shard_map/all_to_all | solution.py:492
  20.9 2.0 %copy-start = (bf16[16384,128]{1,0:T(8,128)(2,1)}, bf16[16384,128]{1,0:T(8,128)(2,1)S(1)}, u32[]{:S(2)}) copy-start(bf16[16384,128]{1,0:T(8,128)(2,1)S(1)} %get-tuple-element.9.mat_hbm) | copy-start | bytes 12582916
  40.3 1.3 %collective-permute-start = (f32[2,48,128]{2,1,0:T(8,128)S(1)}, f32[2,48,128]{2,1,0:T(8,128)S(1)}, u32[]{:S(2)}, u32[]{:S(2)}) collective-permute-start(f32[2,48,128]{2,1,0:T(8,128)S(1)} %get-tuple-element.8), channel_id=1, source_target_pairs={{0,1},{1,0},{2,3},{3,2},{4,5},{5,4},{6,7},{7,6},{8,9},{9,8},{10,11... | collective-permute-start | bytes 147464 | tf_op jit(solution)/shard_map/ppermute | solution.py:239
  41.7 5.1 %collective-permute-start.3 = (f32[2,48,128]{2,1,0:T(8,128)S(1)}, f32[2,48,128]{2,1,0:T(8,128)S(1)}, u32[]{:S(2)}, u32[]{:S(2)}) collective-permute-start(f32[2,48,128]{2,1,0:T(8,128)S(1)} %pad_maximum_fusion), channel_id=1, source_target_pairs={{0,6},{1,7},{2,4},{3,5},{4,2},{5,3},{6,0},{7,1},{8,14},{9,15},{10,... | collective-permute-start | bytes 147464 | tf_op jit(solution)/shard_map/ppermute | solution.py:239
  44.1 4.1 %collective-permute-start.2 = (f32[2,48,128]{2,1,0:T(8,128)S(1)}, f32[2,48,128]{2,1,0:T(8,128)S(1)}, u32[]{:S(2)}, u32[]{:S(2)}) collective-permute-start(f32[2,48,128]{2,1,0:T(8,128)S(1)} %pad_maximum_fusion), channel_id=1, source_target_pairs={{0,4},{1,5},{2,6},{3,7},{4,0},{5,1},{6,2},{7,3},{8,12},{9,13},{10,... | collective-permute-start | bytes 147464 | tf_op jit(solution)/shard_map/ppermute | solution.py:239
  44.7 4.1 %collective-permute-start.1 = (f32[2,48,128]{2,1,0:T(8,128)S(1)}, f32[2,48,128]{2,1,0:T(8,128)S(1)}, u32[]{:S(2)}, u32[]{:S(2)}) collective-permute-start(f32[2,48,128]{2,1,0:T(8,128)S(1)} %pad_maximum_fusion), channel_id=1, source_target_pairs={{0,2},{1,3},{2,0},{3,1},{4,6},{5,7},{6,4},{7,5},{8,10},{9,11},{10,... | collective-permute-start | bytes 147464 | tf_op jit(solution)/shard_map/ppermute | solution.py:239
  48.8 6.0 %collective-permute-start.6 = (f32[2,48,128]{2,1,0:T(8,128)S(1)}, f32[2,48,128]{2,1,0:T(8,128)S(1)}, u32[]{:S(2)}, u32[]{:S(2)}) collective-permute-start(f32[2,48,128]{2,1,0:T(8,128)S(1)} %pad_maximum_fusion.1), channel_id=1, source_target_pairs={{0,24},{1,25},{2,26},{3,27},{4,28},{5,29},{6,30},{7,31},{8,16},{9,... | collective-permute-start | bytes 147464 | tf_op jit(solution)/shard_map/ppermute | solution.py:239
  50.3 5.5 %collective-permute-start.5 = (f32[2,48,128]{2,1,0:T(8,128)S(1)}, f32[2,48,128]{2,1,0:T(8,128)S(1)}, u32[]{:S(2)}, u32[]{:S(2)}) collective-permute-start(f32[2,48,128]{2,1,0:T(8,128)S(1)} %pad_maximum_fusion.1), channel_id=1, source_target_pairs={{0,16},{1,17},{2,18},{3,19},{4,20},{5,21},{6,22},{7,23},{8,24},{9,... | collective-permute-start | bytes 147464 | tf_op jit(solution)/shard_map/ppermute | solution.py:239
  51.0 4.9 %collective-permute-start.4 = (f32[2,48,128]{2,1,0:T(8,128)S(1)}, f32[2,48,128]{2,1,0:T(8,128)S(1)}, u32[]{:S(2)}, u32[]{:S(2)}) collective-permute-start(f32[2,48,128]{2,1,0:T(8,128)S(1)} %pad_maximum_fusion.1), channel_id=1, source_target_pairs={{0,8},{1,9},{2,10},{3,11},{4,12},{5,13},{6,14},{7,15},{8,0},{9,1},... | collective-permute-start | bytes 147464 | tf_op jit(solution)/shard_map/ppermute | solution.py:239
  55.9 1.3 %collective-permute-start.7 = (f32[2,48,128]{2,1,0:T(8,128)S(1)}, f32[2,48,128]{2,1,0:T(8,128)S(1)}, u32[]{:S(2)}, u32[]{:S(2)}) collective-permute-start(f32[2,48,128]{2,1,0:T(8,128)S(1)} %pad_maximum_fusion.2.mine_ref), channel_id=1, source_target_pairs={{0,1},{1,0},{2,3},{3,2},{4,5},{5,4},{6,7},{7,6},{8,9},{9,8},{10,11... | collective-permute-start | bytes 147464 | tf_op jit(solution)/shard_map/ppermute | solution.py:239

commit v7 on v6

--- a/solution.py
+++ b/solution.py
@@ -147,7 +147,7 @@
         functools.partial(weave_kernel, runs, run_rows, cap, peers),
         out_shape=[jax.ShapeDtypeStruct((rows, 2 * cap), BF16), jax.ShapeDtypeStruct((peers * cap, 4 * cap), BF16)],
         grid_spec=grid_spec,
-        compiler_params=pltpu.CompilerParams(vmem_limit_bytes=16 * 1024 * 1024),
+        compiler_params=pltpu.CompilerParams(vmem_limit_bytes=MOST_VMEM),
         cost_estimate=pl.CostEstimate(flops=8 * 10**9, bytes_accessed=40 * 10**6, transcendentals=0),
         name="weave",
     )(me, stencil.T, weights.T)

time: 68.3 us -> 69.5 us (1.018)
  Pallas kernels: 25.7 us -> 27.2 us
  local copies, waits for them, and re-layouts: 1.95 us -> 1.22 us
    pallas_call x1, Pallas kernels: 8.75 us -> 10.3 us  [weave(): pl.pallas_call(functools.partial(weave_kernel, runs, run_rows, cap, peers...]
    unnamed x6 -> x2, local copies, waits for them, and re-layouts: 1.95 us -> 1.22 us
  transfers between devices with their start and end apart: 9 -> 9, of which waited for: 8 -> 8; matrix products, arithmetic and copies ran while one was open for 0% -> 0% of each run, Pallas kernels for 13% -> 15%
where the time goes in v7:
time: 69.5 us; the launch traced here: 69.2 us
  Pallas kernels  27.2 us (39%)
  waiting for transfers between devices  24.4 us (35%)
  starting transfers between devices  15.5 us (22%)
  local copies, waits for them, and re-layouts  1.22 us (2%)
  between operations  0.73 us (1%)
    all_to_all x1, waiting for transfers between devices, body(): lax.all_to_all(outgoing, 'rows', split_axis=0, concat_axis=0, tiled=True)  15.9 us
    pallas_call x1, Pallas kernels, make_basis(): pl.pallas_call(functools.partial(basis_kernel, cap, peers, math.sqrt(tota...  10.8 us
    pallas_call x1, Pallas kernels, weave(): pl.pallas_call(functools.partial(weave_kernel, runs, run_rows, cap, peers...  10.3 us
    ppermute x8, waiting for transfers between devices, hop(): return lax.ppermute(value, 'rows', [(i, i ^ mask) for i in range(peers)])  8.56 us
    ppermute x8, starting transfers between devices, hop(): return lax.ppermute(value, 'rows', [(i, i ^ mask) for i in range(peers)])  8.15 us
    all_to_all x1, starting transfers between devices, body(): lax.all_to_all(outgoing, 'rows', split_axis=0, concat_axis=0, tiled=True)  7.3 us
    pallas_call x1, Pallas kernels, pick_donors(): pl.pallas_call(pick_kernel, out_shape=jax.ShapeDtypeStruct((peers * cap,...  4.05 us
    pallas_call x1, Pallas kernels, local_gram(): pl.pallas_call(functools.partial(gram_kernel, peers, cap), out_shape=[sha...  2 us
  transfers between devices with their start and end apart: 9, of which 8 were waited for; matrix products, arithmetic and copies ran while one was open for 0% of the time, Pallas kernels for 15%

profile of v7, /device:TPU:0, one launch (start us, length us, event | category | flops | bytes accessed | tf_op | source)
XLA Modules:
  0.0 69.2 jit_solution(8536993966171007195)
XLA Ops:
  0.6 4.0 %pick_donors.1 = f32[2048,128]{1,0:T(8,128)} custom-call(s32[32,64]{1,0:T(8,128)} %send_hbm.1, f32[8192,128]{1,0:T(8,128)} %snap_hbm.1), custom_call_target="tpu_custom_call" | custom-call | tf_op jit(solution)/shard_map/pick_donors/pallas_call | solution.py:87
  4.7 7.3 %all-to-all-start = ((f32[32,64,128]{2,1,0:T(8,128)}), f32[32,64,128]{2,1,0:T(8,128)S(1)}, u32[]{:S(2)}, u32[]{:S(2)}) async-start(f32[32,64,128]{2,1,0:T(8,128)} %bitcast.7), calls=%async_computation | async-start | bytes 2097152 | tf_op jit(solution)/shard_map/all_to_all | solution.py:492
  12.0 10.3 %weave.1 = (bf16[16384,128]{1,0:T(8,128)(2,1)}, bf16[2048,256]{1,0:T(8,128)(2,1)}) custom-call(s32[1]{0:T(128)} %bitcast.me_ref, s32[8,16384]{1,0:T(8,128)} %bitcast.8, f32[8,16384]{1,0:T(8,128)} %bitcast.9), custom_call_target="tpu_custom_call" | custom-call | flops 8000000000 | bytes 40000000 | tf_op jit(solution)/shard_map/weave/pallas_call | solution.py:146
  22.3 15.9 %all-to-all-done = f32[32,64,128]{2,1,0:T(8,128)S(1)} async-done(((f32[32,64,128]{2,1,0:T(8,128)}), f32[32,64,128]{2,1,0:T(8,128)S(1)}, u32[]{:S(2)}, u32[]{:S(2)}) %all-to-all-start) | async-done | bytes 1048608 | tf_op jit(solution)/shard_map/all_to_all | solution.py:492
  38.2 0.0 copy-start
  38.2 1.2 %copy-done = bf16[2048,256]{1,0:T(8,128)(2,1)S(1)} copy-done((bf16[2048,256]{1,0:T(8,128)(2,1)S(1)}, bf16[2048,256]{1,0:T(8,128)(2,1)}, u32[]{:S(2)}) %copy-start) | copy-done | bytes 1048600
  39.5 2.0 %local_gram.1 = (f32[2,48,128]{2,1,0:T(8,128)S(1)}, f32[2,48,128]{2,1,0:T(8,128)S(1)}) custom-call(s32[1]{0:T(128)} %bitcast.me_ref, f32[2048,128]{1,0:T(8,128)S(1)} %bitcast.5, bf16[2048,256]{1,0:T(8,128)(2,1)S(1)} %copy-done), custom_call_target="tpu_custom_call" | custom-call | tf_op jit(solution)/shard_map/local_gram/pallas_call | solution.py:227
  41.5 0.1 collective-permute-start
  41.5 1.2 %collective-permute-done = f32[2,48,128]{2,1,0:T(8,128)S(1)} collective-permute-done((f32[2,48,128]{2,1,0:T(8,128)S(1)}, f32[2,48,128]{2,1,0:T(8,128)S(1)}, u32[]{:S(2)}, u32[]{:S(2)}) %collective-permute-start) | collective-permute-done | bytes 49184 | tf_op jit(solution)/shard_map/ppermute | solution.py:239
  42.8 2.5 %collective-permute-start.3 = (f32[2,48,128]{2,1,0:T(8,128)S(1)}, f32[2,48,128]{2,1,0:T(8,128)S(1)}, u32[]{:S(2)}, u32[]{:S(2)}) collective-permute-start(f32[2,48,128]{2,1,0:T(8,128)S(1)} %pad_maximum_fusion), channel_id=1, source_target_pairs={{0,6},{1,7},{2,4},{3,5},{4,2},{5,3},{6,0},{7,1},{8,14},{9,15},{10,... | collective-permute-start | bytes 147464 | tf_op jit(solution)/shard_map/ppermute | solution.py:239
  45.3 0.5 collective-permute-start.2
  45.8 0.6 collective-permute-start.1
  46.4 1.5 %collective-permute-done.3 = f32[2,48,128]{2,1,0:T(8,128)S(1)} collective-permute-done((f32[2,48,128]{2,1,0:T(8,128)S(1)}, f32[2,48,128]{2,1,0:T(8,128)S(1)}, u32[]{:S(2)}, u32[]{:S(2)}) %collective-permute-start.3) | collective-permute-done | bytes 49184 | tf_op jit(solution)/shard_map/ppermute | solution.py:239
  47.9 1.5 %collective-permute-done.2 = f32[2,48,128]{2,1,0:T(8,128)S(1)} collective-permute-done((f32[2,48,128]{2,1,0:T(8,128)S(1)}, f32[2,48,128]{2,1,0:T(8,128)S(1)}, u32[]{:S(2)}, u32[]{:S(2)}) %collective-permute-start.2) | collective-permute-done | bytes 49184 | tf_op jit(solution)/shard_map/ppermute | solution.py:239
  49.3 0.5 collective-permute-done.1
  49.9 1.5 %collective-permute-start.6 = (f32[2,48,128]{2,1,0:T(8,128)S(1)}, f32[2,48,128]{2,1,0:T(8,128)S(1)}, u32[]{:S(2)}, u32[]{:S(2)}) collective-permute-start(f32[2,48,128]{2,1,0:T(8,128)S(1)} %pad_maximum_fusion.1), channel_id=1, source_target_pairs={{0,24},{1,25},{2,26},{3,27},{4,28},{5,29},{6,30},{7,31},{8,16},{9,... | collective-permute-start | bytes 147464 | tf_op jit(solution)/shard_map/ppermute | solution.py:239
  51.5 0.6 collective-permute-start.5
  52.1 2.3 %collective-permute-start.4 = (f32[2,48,128]{2,1,0:T(8,128)S(1)}, f32[2,48,128]{2,1,0:T(8,128)S(1)}, u32[]{:S(2)}, u32[]{:S(2)}) collective-permute-start(f32[2,48,128]{2,1,0:T(8,128)S(1)} %pad_maximum_fusion.1), channel_id=1, source_target_pairs={{0,8},{1,9},{2,10},{3,11},{4,12},{5,13},{6,14},{7,15},{8,0},{9,1},... | collective-permute-start | bytes 147464 | tf_op jit(solution)/shard_map/ppermute | solution.py:239
  54.4 1.5 %collective-permute-done.6 = f32[2,48,128]{2,1,0:T(8,128)S(1)} collective-permute-done((f32[2,48,128]{2,1,0:T(8,128)S(1)}, f32[2,48,128]{2,1,0:T(8,128)S(1)}, u32[]{:S(2)}, u32[]{:S(2)}) %collective-permute-start.6) | collective-permute-done | bytes 49184 | tf_op jit(solution)/shard_map/ppermute | solution.py:239
  55.9 1.1 %collective-permute-done.5 = f32[2,48,128]{2,1,0:T(8,128)S(1)} collective-permute-done((f32[2,48,128]{2,1,0:T(8,128)S(1)}, f32[2,48,128]{2,1,0:T(8,128)S(1)}, u32[]{:S(2)}, u32[]{:S(2)}) %collective-permute-start.5) | collective-permute-done | bytes 49184 | tf_op jit(solution)/shard_map/ppermute | solution.py:239
  57.0 0.0 collective-permute-done.4
  57.1 0.1 collective-permute-start.7
  57.1 1.2 %collective-permute-done.7.other_ref = f32[2,48,128]{2,1,0:T(8,128)S(1)} collective-permute-done((f32[2,48,128]{2,1,0:T(8,128)S(1)}, f32[2,48,128]{2,1,0:T(8,128)S(1)}, u32[]{:S(2)}, u32[]{:S(2)}) %collective-permute-start.7) | collective-permute-done | bytes 49184 | tf_op jit(solution)/shard_map/ppermute | solution.py:239
  58.4 10.8 %make_basis.1 = (f32[16384,128]{1,0:T(8,128)}, f32[128,128]{1,0:T(8,128)}) custom-call(s32[1]{0:T(128)} %bitcast.me_ref, f32[2,48,128]{2,1,0:T(8,128)S(1)} %pad_maximum_fusion.2.mine_ref, f32[2,48,128]{2,1,0:T(8,128)S(1)} %collective-permute-done.7.other_ref, f32[2048,128]{1,0:T(8,128)S(1)} %bitcast.6, bf16[16384,128]{1,0:T(8,128)(2,1)} %get-tuple-element.9.mat_hbm), custom_call_target="tpu_custom_call" | custom-call | tf_op jit(solution)/shard_map/make_basis/pallas_call | solution.py:476
  (8 shorter events, 0.1 us)
Async XLA Ops:
  4.7 33.5 %all-to-all-start = ((f32[32,64,128]{2,1,0:T(8,128)}), f32[32,64,128]{2,1,0:T(8,128)S(1)}, u32[]{:S(2)}, u32[]{:S(2)}) async-start(f32[32,64,128]{2,1,0:T(8,128)} %bitcast.7), calls=%async_computation | async-start | bytes 2097152 | tf_op jit(solution)/shard_map/all_to_all | solution.py:492
  38.2 1.2 %copy-start = (bf16[2048,256]{1,0:T(8,128)(2,1)S(1)}, bf16[2048,256]{1,0:T(8,128)(2,1)}, u32[]{:S(2)}) copy-start(bf16[2048,256]{1,0:T(8,128)(2,1)} %get-tuple-element.6.slot_ref) | copy-start | bytes 3145732
  41.5 1.3 %collective-permute-start = (f32[2,48,128]{2,1,0:T(8,128)S(1)}, f32[2,48,128]{2,1,0:T(8,128)S(1)}, u32[]{:S(2)}, u32[]{:S(2)}) collective-permute-start(f32[2,48,128]{2,1,0:T(8,128)S(1)} %get-tuple-element.8), channel_id=1, source_target_pairs={{0,1},{1,0},{2,3},{3,2},{4,5},{5,4},{6,7},{7,6},{8,9},{9,8},{10,11... | collective-permute-start | bytes 147464 | tf_op jit(solution)/shard_map/ppermute | solution.py:239
  42.8 5.1 %collective-permute-start.3 = (f32[2,48,128]{2,1,0:T(8,128)S(1)}, f32[2,48,128]{2,1,0:T(8,128)S(1)}, u32[]{:S(2)}, u32[]{:S(2)}) collective-permute-start(f32[2,48,128]{2,1,0:T(8,128)S(1)} %pad_maximum_fusion), channel_id=1, source_target_pairs={{0,6},{1,7},{2,4},{3,5},{4,2},{5,3},{6,0},{7,1},{8,14},{9,15},{10,... | collective-permute-start | bytes 147464 | tf_op jit(solution)/shard_map/ppermute | solution.py:239
  45.3 4.1 %collective-permute-start.2 = (f32[2,48,128]{2,1,0:T(8,128)S(1)}, f32[2,48,128]{2,1,0:T(8,128)S(1)}, u32[]{:S(2)}, u32[]{:S(2)}) collective-permute-start(f32[2,48,128]{2,1,0:T(8,128)S(1)} %pad_maximum_fusion), channel_id=1, source_target_pairs={{0,4},{1,5},{2,6},{3,7},{4,0},{5,1},{6,2},{7,3},{8,12},{9,13},{10,... | collective-permute-start | bytes 147464 | tf_op jit(solution)/shard_map/ppermute | solution.py:239
  45.8 4.1 %collective-permute-start.1 = (f32[2,48,128]{2,1,0:T(8,128)S(1)}, f32[2,48,128]{2,1,0:T(8,128)S(1)}, u32[]{:S(2)}, u32[]{:S(2)}) collective-permute-start(f32[2,48,128]{2,1,0:T(8,128)S(1)} %pad_maximum_fusion), channel_id=1, source_target_pairs={{0,2},{1,3},{2,0},{3,1},{4,6},{5,7},{6,4},{7,5},{8,10},{9,11},{10,... | collective-permute-start | bytes 147464 | tf_op jit(solution)/shard_map/ppermute | solution.py:239
  49.9 6.0 %collective-permute-start.6 = (f32[2,48,128]{2,1,0:T(8,128)S(1)}, f32[2,48,128]{2,1,0:T(8,128)S(1)}, u32[]{:S(2)}, u32[]{:S(2)}) collective-permute-start(f32[2,48,128]{2,1,0:T(8,128)S(1)} %pad_maximum_fusion.1), channel_id=1, source_target_pairs={{0,24},{1,25},{2,26},{3,27},{4,28},{5,29},{6,30},{7,31},{8,16},{9,... | collective-permute-start | bytes 147464 | tf_op jit(solution)/shard_map/ppermute | solution.py:239
  51.5 5.5 %collective-permute-start.5 = (f32[2,48,128]{2,1,0:T(8,128)S(1)}, f32[2,48,128]{2,1,0:T(8,128)S(1)}, u32[]{:S(2)}, u32[]{:S(2)}) collective-permute-start(f32[2,48,128]{2,1,0:T(8,128)S(1)} %pad_maximum_fusion.1), channel_id=1, source_target_pairs={{0,16},{1,17},{2,18},{3,19},{4,20},{5,21},{6,22},{7,23},{8,24},{9,... | collective-permute-start | bytes 147464 | tf_op jit(solution)/shard_map/ppermute | solution.py:239
  52.1 4.9 %collective-permute-start.4 = (f32[2,48,128]{2,1,0:T(8,128)S(1)}, f32[2,48,128]{2,1,0:T(8,128)S(1)}, u32[]{:S(2)}, u32[]{:S(2)}) collective-permute-start(f32[2,48,128]{2,1,0:T(8,128)S(1)} %pad_maximum_fusion.1), channel_id=1, source_target_pairs={{0,8},{1,9},{2,10},{3,11},{4,12},{5,13},{6,14},{7,15},{8,0},{9,1},... | collective-permute-start | bytes 147464 | tf_op jit(solution)/shard_map/ppermute | solution.py:239
  57.1 1.3 %collective-permute-start.7 = (f32[2,48,128]{2,1,0:T(8,128)S(1)}, f32[2,48,128]{2,1,0:T(8,128)S(1)}, u32[]{:S(2)}, u32[]{:S(2)}) collective-permute-start(f32[2,48,128]{2,1,0:T(8,128)S(1)} %pad_maximum_fusion.2.mine_ref), channel_id=1, source_target_pairs={{0,1},{1,0},{2,3},{3,2},{4,5},{5,4},{6,7},{7,6},{8,9},{9,8},{10,11... | collective-permute-start | bytes 147464 | tf_op jit(solution)/shard_map/ppermute | solution.py:239
